TPU v7x, 256 devices: a whole 4x4x8 slice. The times are simulated.
256 devices in a mesh: beam: 8 (over x, core), row: 32 (over y, z).
Axes of the slice: x: 4, y: 4, z: 8, core: 2. Of those that a mesh axis runs over, the one named last changes fastest.
Arguments:
- x_in: bfloat16 [4, 2, 16, 8192], P(None, None, None, 'beam'), may hold values from -6 to 6
- w_inner: bfloat16 [8192, 2, 16384], P('beam', None, 'row'), may hold values from -0.0625 to 0.0625
- w_bc: bfloat16 [8192, 2, 2048], P('beam', None, 'row'), may hold values from -0.0625 to 0.0625
- w_dt: bfloat16 [8192, 256], P('beam', 'row'), may hold values from -0.0625 to 0.0625
- conv_x_w: bfloat16 [4, 16384], P(None, 'row'), may hold values from -3 to 3
- conv_bc_w: bfloat16 [4, 2, 2048], P(None, None, 'row'), may hold values from -3 to 3
- dt_bias: float32 [256], P('row'), may hold values from -4 to 1
- a_log: float32 [256], P('row'), may hold values from 0 to 2.8
- d_skip: float32 [256], P('row'), may hold values from 0.5 to 2
- norm_gain: float32 [16384], P('row'), may hold values from 0.1 to 1.9
- w_out: bfloat16 [16384, 8192], P('row', 'beam'), may hold values from -0.046875 to 0.046875
- ssm_state: bfloat16 [2, 16, 256, 64, 256], P(None, 'beam', 'row'), may hold values from -6 to 6
- conv_x_state: bfloat16 [2, 16, 256, 64, 3], P(None, 'beam', 'row'), may hold values from -6 to 6
- conv_bc_state: bfloat16 [2, 16, 3, 2, 2048], P(None, 'beam', None, None, 'row'), may hold values from -6 to 6
- parents: int32 [4, 2, 16], replicated, may hold values from 0 to 15
Outputs:
- layer_out: bfloat16 [4, 32, 8192], P(None, 'row', 'beam')
- ssm_final: bfloat16 [2, 16, 256, 64, 256], P(None, 'beam', 'row')
- conv_x_final: bfloat16 [2, 16, 256, 64, 3], P(None, 'beam', 'row')
- conv_bc_final: bfloat16 [2, 16, 3, 2, 2048], P(None, 'beam', None, None, 'row')
All inputs are finite; a program needn't handle non-finite values.
Results may differ from a plain program's by a relative error of at most 0.0077.
Values may be sent and summed in bfloat16 or wider, within the bound.
No kernel may reach another device: no remote copies, remote signals or barrier semaphores. Data moves between devices by JAX's collectives and lax.ppermute only.
A program may use at most 64 MiB of HBM per device.

v0:
```python
import jax
import jax.numpy as jnp
from jax import lax
from jax.sharding import PartitionSpec as P

HEADS = 256
HDIM = 64
GROUPS = 8


EPS = 1e-05


def partner_2(shard, axis, stride):
    return lax.ppermute(shard, axis, [(i, i ^ 1 << stride) for i in range(lax.axis_size(axis))])


def stored(value):
    return lax.optimization_barrier(value.astype(jnp.bfloat16))


def local(
    x_in,
    w_inner,
    w_bc,
    w_dt,
    conv_x_w,
    conv_bc_w,
    dt_bias,
    a_log,
    d_skip,
    norm_gain,
    w_out,
    ssm_state,
    conv_x_state,
    conv_bc_state,
    parents,
):
    beam_index = lax.axis_index("beam")
    row_index = lax.axis_index("row")
    steps_all, sessions, width, d_local = x_in.shape
    local_beams = ssm_state.shape[1]
    heads_local = ssm_state.shape[2]
    head_dim = ssm_state.shape[3]
    tap_count = conv_x_w.shape[0]
    group_heads = HEADS // GROUPS
    group_index = row_index * heads_local // group_heads
    group_span = lax.axis_size("row") // GROUPS
    swap_rounds = group_span.bit_length() - 1
    w_inner4 = w_inner.reshape(d_local, 2, heads_local, head_dim)
    w_out3 = w_out.reshape(heads_local, head_dim, w_out.shape[1])
    conv_taps = conv_x_w.astype(jnp.float32).reshape(tap_count, heads_local, head_dim)
    gains = norm_gain.reshape(heads_local, head_dim)
    bc_taps = conv_bc_w.astype(jnp.float32)
    decay_rates = jnp.exp(a_log)
    group_mask = (jnp.arange(GROUPS, dtype=jnp.int32) == group_index).astype(jnp.float32)
    ssm_held = ssm_state
    conv_held = conv_x_state
    rim_held = conv_bc_state
    outputs = []
    for step in range(steps_all):
        parent = parents[step]
        own_parent = lax.dynamic_slice_in_dim(parent, beam_index * local_beams, local_beams, 1)
        pieces = (
            lax.all_gather(ssm_held, "beam", axis=1, tiled=True),
            lax.all_gather(conv_held, "beam", axis=1, tiled=True),
            lax.all_gather(rim_held, "beam", axis=1, tiled=True),
        )
        span_size = pieces[0].shape[1]
        beam_ids = jnp.arange(span_size, dtype=jnp.int32)
        choose = (own_parent[:, :, None] == beam_ids[None, None, :]).astype(jnp.bfloat16)
        ssm_held = jnp.einsum(
            "sij,sjhpn->sihpn", choose, pieces[0], preferred_element_type=jnp.float32
        ).astype(jnp.bfloat16)
        conv_held = jnp.einsum(
            "sij,sjhpk->sihpk", choose, pieces[1], preferred_element_type=jnp.float32
        ).astype(jnp.bfloat16)
        rim_held = jnp.einsum(
            "sij,sjkzc->sikzc", choose, pieces[2], preferred_element_type=jnp.float32
        ).astype(jnp.bfloat16)
        x_step = x_in[step]
        bc_part = jnp.einsum("sbd,dzk->sbzk", x_step, w_bc, preferred_element_type=jnp.float32)
        dt_part = jnp.einsum("sbd,dh->sbh", x_step, w_dt, preferred_element_type=jnp.float32)
        bc_sum, dt_sum = lax.psum((bc_part, dt_part), "beam")
        bc_new = stored(bc_sum)
        dt_raw = stored(dt_sum)
        bc_new = lax.dynamic_slice_in_dim(bc_new, beam_index * local_beams, local_beams, 1)
        dt_raw = lax.dynamic_slice_in_dim(dt_raw, beam_index * local_beams, local_beams, 1)
        inner_part = stored(
            lax.psum_scatter(
                jnp.einsum("sbd,dzhp->bszhp", x_step, w_inner4, preferred_element_type=jnp.float32),
                "beam",
                scatter_dimension=0,
                tiled=True,
            )
        )
        gate_in = jnp.transpose(inner_part[:, :, 0], (1, 0, 2, 3))
        x_new = jnp.transpose(inner_part[:, :, 1], (1, 0, 2, 3))
        mixed = jnp.sum(
            conv_held.astype(jnp.float32) * jnp.transpose(conv_taps[:-1], (1, 2, 0)), axis=-1
        )
        mixed = mixed + conv_taps[-1] * x_new.astype(jnp.float32)
        x_conv = stored(jax.nn.silu(mixed))
        conv_held = jnp.concatenate([conv_held[..., 1:], x_new[..., None]], axis=-1)
        mixed_bc = jnp.sum(rim_held.astype(jnp.float32) * bc_taps[:-1], axis=2) + bc_taps[
            -1
        ] * bc_new.astype(jnp.float32)
        bc_conv = stored(jax.nn.silu(mixed_bc))
        rim_held = jnp.concatenate([rim_held[:, :, 1:], bc_new[:, :, None]], axis=2)
        group_block = bc_conv
        for bit_number in range(swap_rounds):
            partner = partner_2(group_block, "row", bit_number)
            upper = jnp.bitwise_and(jnp.right_shift(row_index, bit_number), 1) == 1
            group_block = jnp.where(
                upper,
                jnp.concatenate([partner, group_block], axis=3),
                jnp.concatenate([group_block, partner], axis=3),
            )
        bc_group = group_block.astype(jnp.float32)
        b_in = bc_group[:, :, 0]
        c_out = bc_group[:, :, 1]
        step_size = jax.nn.softplus(dt_raw.astype(jnp.float32) + dt_bias)
        decay = jnp.exp(-decay_rates * step_size)
        x_val = x_conv.astype(jnp.float32)
        state = (
            decay[..., None, None] * ssm_held.astype(jnp.float32)
            + (step_size[..., None] * x_val)[..., None] * b_in[:, :, None, None, :]
        )
        read = jnp.sum(state * c_out[:, :, None, None, :], axis=-1) + d_skip[:, None] * x_val
        ssm_held = stored(state)
        gated = read * jax.nn.silu(gate_in.astype(jnp.float32))
        square_sum = jnp.sum(gated * gated, axis=(2, 3))
        stat_terms = square_sum[..., None] * group_mask
        totals = lax.psum(stat_terms, "row")
        mean_sq = lax.dynamic_index_in_dim(totals, group_index, 2, keepdims=False) / (
            group_heads * HDIM
        )
        normed = stored(gated * lax.rsqrt(mean_sq + EPS)[..., None, None] * gains)
        partial_out = jnp.einsum(
            "sbhp,hpd->sbd",
            lax.all_gather(normed, "beam", axis=1, tiled=True),
            w_out3,
            preferred_element_type=jnp.float32,
        )
        flat_rows = partial_out.reshape(sessions * width, partial_out.shape[2])
        outputs.append(
            lax.psum_scatter(flat_rows, "row", scatter_dimension=0, tiled=True).astype(jnp.bfloat16)
        )
    return (jnp.stack(outputs), ssm_held, conv_held, rim_held)


def solution(mesh):
    placed = (
        P(None, None, None, "beam"),
        P("beam", None, "row"),
        P("beam", None, "row"),
        P("beam", "row"),
        P(None, "row"),
        P(None, None, "row"),
        P("row"),
        P("row"),
        P("row"),
        P("row"),
        P("row", "beam"),
        P(None, "beam", "row", None, None),
        P(None, "beam", "row", None, None),
        P(None, "beam", None, None, "row"),
        P(),
    )
    return jax.shard_map(
        local,
        mesh=mesh,
        in_specs=placed,
        out_specs=(
            P(None, "row", "beam"),
            P(None, "beam", "row", None, None),
            P(None, "beam", "row", None, None),
            P(None, "beam", None, None, "row"),
        ),
        check_vma=False,
    )
```

profile of v0, /device:TPU:32, one launch (start us, length us, event | category | flops | bytes accessed | tf_op | source)
XLA Modules:
  0.0 759.2 jit_solution(5823953862466214772)
XLA Ops:
  7.2 4.8 copy.199
  24.1 27.4 %all-reduce.6 = (bf16[2,16,2,64]{3,1,2,0:T(8,128)(2,1)S(1)}, bf16[2,16,2,64]{3,1,2,0:T(8,128)(2,1)S(1)}, bf16[2,16,2,64]{3,1,2,0:T(8,128)(2,1)S(1)}, bf16[2,16,8...) all-reduce(f32[2,16,2,64]{3,1,2,0:T(8,128)S(1)} %fusion.30, ...), channel_id=1, replica_groups=mesh['beam'=8,'row'=32] {'beam'}, use_global_device_ids=true, to_apply=%region_22.23 | all-reduce | flops 17408 | bytes 104448 | tf_op jit(solution)/shard_map/psum | solution.py:84
  51.5 12.8 %all_gather.50 = bf16[2,16,3,2,64]{4,3,2,0,1:T(2,128)(2,1)S(1)} all-gather(bf16[2,2,3,2,64]{4,3,2,0,1:T(2,128)(2,1)S(1)} %copy.204), channel_id=1, replica_groups=mesh['beam'=8,'row'=32] {'beam'}, dimensions={1}, use_global_device_ids=true | all-gather | bytes 27648 | tf_op jit(solution)/shard_map/all_gather | solution.py:67
  64.7 12.8 %all_gather.54 = bf16[2,16,3,2,64]{4,3,2,0,1:T(2,128)(2,1)S(1)} all-gather(bf16[2,2,3,2,64]{4,3,2,0,1:T(2,128)(2,1)S(1)} %copy.220), channel_id=1, replica_groups=mesh['beam'=8,'row'=32] {'beam'}, dimensions={1}, use_global_device_ids=true | all-gather | bytes 27648 | tf_op jit(solution)/shard_map/all_gather | solution.py:67
  77.8 12.8 %all_gather.58 = bf16[2,16,3,2,64]{4,3,2,0,1:T(2,128)(2,1)S(1)} all-gather(bf16[2,2,3,2,64]{4,3,2,0,1:T(2,128)(2,1)S(1)} %copy.236), channel_id=1, replica_groups=mesh['beam'=8,'row'=32] {'beam'}, dimensions={1}, use_global_device_ids=true | all-gather | bytes 27648 | tf_op jit(solution)/shard_map/all_gather | solution.py:67
  91.0 12.8 %all_gather.62 = bf16[2,16,3,2,64]{4,3,2,0,1:T(2,128)(2,1)S(1)} all-gather(bf16[2,2,3,2,64]{4,3,2,0,1:T(2,128)(2,1)S(1)} %copy.252), channel_id=1, replica_groups=mesh['beam'=8,'row'=32] {'beam'}, dimensions={1}, use_global_device_ids=true | all-gather | bytes 27648 | tf_op jit(solution)/shard_map/all_gather | solution.py:67
  104.5 12.8 %all_gather.49 = bf16[2,16,8,64,3]{3,2,4,0,1:T(8,128)(2,1)S(1)} all-gather(bf16[2,2,8,64,3]{3,2,4,0,1:T(8,128)(2,1)S(1)} %copy.196), channel_id=1, replica_groups=mesh['beam'=8,'row'=32] {'beam'}, dimensions={1}, use_global_device_ids=true | all-gather | bytes 110592 | tf_op jit(solution)/shard_map/all_gather | solution.py:66
  117.8 3.1 collective-permute-start.1
  124.1 12.8 %all_gather.53 = bf16[2,16,8,64,3]{3,2,4,0,1:T(8,128)(2,1)S(1)} all-gather(bf16[2,2,8,64,3]{3,2,4,0,1:T(8,128)(2,1)S(1)} %copy.214), channel_id=1, replica_groups=mesh['beam'=8,'row'=32] {'beam'}, dimensions={1}, use_global_device_ids=true | all-gather | bytes 110592 | tf_op jit(solution)/shard_map/all_gather | solution.py:66
  138.0 12.8 %all_gather.57 = bf16[2,16,8,64,3]{3,2,4,0,1:T(8,128)(2,1)S(1)} all-gather(bf16[2,2,8,64,3]{3,2,4,0,1:T(8,128)(2,1)S(1)} %copy.230), channel_id=1, replica_groups=mesh['beam'=8,'row'=32] {'beam'}, dimensions={1}, use_global_device_ids=true | all-gather | bytes 110592 | tf_op jit(solution)/shard_map/all_gather | solution.py:66
  151.2 2.7 reduce-scatter.11.cloned.1.call-done
  154.6 12.9 %all_gather.61 = bf16[2,16,8,64,3]{3,2,4,0,1:T(8,128)(2,1)S(1)} all-gather(bf16[2,2,8,64,3]{3,2,4,0,1:T(8,128)(2,1)S(1)} %copy.246), channel_id=1, replica_groups=mesh['beam'=8,'row'=32] {'beam'}, dimensions={1}, use_global_device_ids=true | all-gather | bytes 110592 | tf_op jit(solution)/shard_map/all_gather | solution.py:66
  168.2 39.4 %all-gather.5.cloned.1.call-done = bf16[2,16,8,64,256]{4,3,2,0,1:T(8,128)(2,1)} async-done(((bf16[2,2,8,64,256]{4,3,2,0,1:T(8,128)(2,1)}), bf16[2,16,8,64,256]{4,3,2,0,1:T(8,128)(2,1)}) %all-gather.5.cloned.1.call-update) | async-done | bytes 8388624 | tf_op jit(solution)/shard_map/all_gather | solution.py:65
  207.5 10.6 %multiply_reduce_fusion.3 = (f32[2,2,8,64]{1,3,2,0:T(8,128)S(1)}, bf16[2,2,8,64,256]{4,1,3,2,0:T(2,128)(2,1)S(1)}) fusion(f32[2,2,256]{2,1,0:T(2,128)S(1)} %get-tuple-element.64, f32[2,2,256]{2,1,0:T(2,128)S(1)} %get-tuple-element.65, f32[2,2,8,64]{1,3,2,0:T(8,128)S(1)} %copy.203, bf16[2,16,8,64,256]{4,3,2,0,1:T(8,128)(2,1)} %all-gather.5.cloned.1.call-done, ...), kind=kOutput, calls=%fused_computation.14 | convolution fusion | flops 20969536 | bytes 9461904 | tf_op jit(solution)/shard_map/sij,sjhpn->sihpn/dot_general | solution.py:72
  220.0 3.1 collective-permute-done.2
  223.2 2.6 collective-permute-start.3
  228.0 44.0 %all-gather.7.cloned.1.call-done = bf16[2,16,8,64,256]{4,3,2,0,1:T(8,128)(2,1)} async-done(((bf16[2,2,8,64,256]{4,3,2,0,1:T(8,128)(2,1)}), bf16[2,16,8,64,256]{4,3,2,0,1:T(8,128)(2,1)}) %all-gather.7.cloned.1.call-update) | async-done | bytes 8388624 | tf_op jit(solution)/shard_map/all_gather | solution.py:65
  272.0 10.6 %multiply_reduce_fusion.2 = (f32[2,2,8,64]{1,3,2,0:T(8,128)S(1)}, bf16[2,2,8,64,256]{4,1,3,2,0:T(2,128)(2,1)S(1)}) fusion(f32[2,2,256]{2,1,0:T(2,128)S(1)} %get-tuple-element.66, f32[2,2,256]{2,1,0:T(2,128)S(1)} %get-tuple-element.67, f32[2,2,8,64]{1,3,2,0:T(8,128)S(1)} %copy.219, bf16[2,16,8,64,256]{4,3,2,0,1:T(8,128)(2,1)} %all-gather.7.cloned.1.call-done, ...), kind=kOutput, calls=%fused_computation.12 | convolution fusion | flops 20969536 | bytes 9461904 | tf_op jit(solution)/shard_map/sij,sjhpn->sihpn/dot_general | solution.py:72
  284.6 3.1 collective-permute-done.4
  287.8 2.6 collective-permute-start.5
  292.7 43.8 %all-gather.9.cloned.1.call-done = bf16[2,16,8,64,256]{4,3,2,0,1:T(8,128)(2,1)} async-done(((bf16[2,2,8,64,256]{4,3,2,0,1:T(8,128)(2,1)}), bf16[2,16,8,64,256]{4,3,2,0,1:T(8,128)(2,1)}) %all-gather.9.cloned.1.call-update) | async-done | bytes 8388624 | tf_op jit(solution)/shard_map/all_gather | solution.py:65
  336.4 10.6 %multiply_reduce_fusion.1 = (f32[2,2,8,64]{1,3,2,0:T(8,128)S(1)}, bf16[2,2,8,64,256]{4,1,3,2,0:T(2,128)(2,1)S(1)}) fusion(f32[2,2,256]{2,1,0:T(2,128)S(1)} %get-tuple-element.68, f32[2,2,256]{2,1,0:T(2,128)S(1)} %get-tuple-element.69, f32[2,2,8,64]{1,3,2,0:T(8,128)S(1)} %copy.235, bf16[2,16,8,64,256]{4,3,2,0,1:T(8,128)(2,1)} %all-gather.9.cloned.1.call-done, ...), kind=kOutput, calls=%fused_computation.10 | convolution fusion | flops 20969536 | bytes 9461904 | tf_op jit(solution)/shard_map/sij,sjhpn->sihpn/dot_general | solution.py:72
  348.9 3.1 collective-permute-done.6
  352.0 2.6 collective-permute-start.7
  358.2 42.7 %all-gather.11.cloned.1.call-done = bf16[2,16,8,64,256]{4,3,2,0,1:T(8,128)(2,1)} async-done(((bf16[2,2,8,64,256]{4,3,2,0,1:T(8,128)(2,1)}), bf16[2,16,8,64,256]{4,3,2,0,1:T(8,128)(2,1)}) %all-gather.11.cloned.1.call-update) | async-done | bytes 8388624 | tf_op jit(solution)/shard_map/all_gather | solution.py:65
  400.9 10.6 %fusion.172 = (bf16[2,2,8,64,256]{4,1,3,2,0:T(2,128)(2,1)S(1)}, f32[2,2,8,64]{1,3,2,0:T(8,128)S(1)}) fusion(f32[2,2,256]{2,1,0:T(2,128)S(1)} %get-tuple-element.70, f32[2,2,256]{2,1,0:T(2,128)S(1)} %get-tuple-element.71, f32[2,2,8,64]{1,3,2,0:T(8,128)S(1)} %copy.251, bf16[2,16,8,64,256]{4,3,2,0,1:T(8,128)(2,1)} %all-gather.11.cloned.1.call-done, ...), kind=kOutput, calls=%fused_computation.290 | convolution fusion | flops 20969536 | bytes 9461904 | tf_op jit(solution)/shard_map/sij,sjhpn->sihpn/dot_general | solution.py:72
  412.0 138.3 %all-reduce.5 = (f32[2,2,8]{1,0,2:T(2,128)S(1)}, f32[2,2,8]{1,0,2:T(2,128)S(1)}, f32[2,2,8]{1,0,2:T(2,128)S(1)}, f32[2,2,8]{1,0,2:T(2,128)S(1)}) all-reduce(f32[2,2,8]{1,0,2:T(2,128)S(1)} %get-tuple-element.105, f32[2,2,8]{1,0,2:T(2,128)S(1)} %get-tuple-element.104, ...), channel_id=1, replica_groups=mesh['beam'=8,'row'=32] {'row'}, use_global_device_ids=true, to_apply=%region_34.35 | all-reduce | flops 128 | bytes 1024 | tf_op jit(solution)/shard_map/psum | solution.py:134
  550.5 12.8 %all_gather.63 = bf16[2,16,8,64]{3,2,0,1:T(8,128)(2,1)S(1)} all-gather(bf16[2,2,8,64]{3,2,0,1:T(8,128)(2,1)S(1)} %copy.255), channel_id=1, replica_groups=mesh['beam'=8,'row'=32] {'beam'}, dimensions={1}, use_global_device_ids=true | all-gather | bytes 36864 | tf_op jit(solution)/shard_map/all_gather | solution.py:141
  563.6 12.7 %all_gather.59 = bf16[2,16,8,64]{3,2,0,1:T(8,128)(2,1)S(1)} all-gather(bf16[2,2,8,64]{3,2,0,1:T(8,128)(2,1)S(1)} %copy.239), channel_id=1, replica_groups=mesh['beam'=8,'row'=32] {'beam'}, dimensions={1}, use_global_device_ids=true | all-gather | bytes 36864 | tf_op jit(solution)/shard_map/all_gather | solution.py:141
  576.7 12.7 %all_gather.55 = bf16[2,16,8,64]{3,2,0,1:T(8,128)(2,1)S(1)} all-gather(bf16[2,2,8,64]{3,2,0,1:T(8,128)(2,1)S(1)} %copy.223), channel_id=1, replica_groups=mesh['beam'=8,'row'=32] {'beam'}, dimensions={1}, use_global_device_ids=true | all-gather | bytes 36864 | tf_op jit(solution)/shard_map/all_gather | solution.py:141
  589.7 12.7 %all_gather.51 = bf16[2,16,8,64]{3,2,0,1:T(8,128)(2,1)S(1)} all-gather(bf16[2,2,8,64]{3,2,0,1:T(8,128)(2,1)S(1)} %copy.207), channel_id=1, replica_groups=mesh['beam'=8,'row'=32] {'beam'}, dimensions={1}, use_global_device_ids=true | all-gather | bytes 36864 | tf_op jit(solution)/shard_map/all_gather | solution.py:141
  602.8 144.7 %all-reduce.8 = (bf16[32,1024]{1,0:T(8,128)(2,1)S(1)}, bf16[32,1024]{1,0:T(8,128)(2,1)S(1)}, bf16[32,1024]{1,0:T(8,128)(2,1)S(1)}, bf16[32,1024]{1,0:T(8,128)(2,1)S(1)}) all-reduce(f32[32,1024]{1,0:T(8,128)S(1)} %convolution_bitcast_fusion.4, ...), channel_id=9, replica_groups=mesh['beam'=8,'row'=32] {'row'}, use_global_device_ids=true, to_apply=%region_35.36.clone | all-reduce | flops 131072 | bytes 786432
  (198 shorter events, 40.2 us)
Async XLA Ops:
  7.2 556.1 %copy-start = (bf16[512,1024]{1,0:T(8,128)(2,1)S(1)}, bf16[512,1024]{1,0:T(8,128)(2,1)}, u32[]{:S(2)}) copy-start(bf16[512,1024]{1,0:T(8,128)(2,1)} %param.25) | copy-start | bytes 3145732
  7.2 4.9 copy-start.2
  7.2 115.3 %reduce-scatter.5.cloned.1.call-start = ((), (), s32[]{:S(2)}) async-start(), calls=%async_computation.5 | async-start | bytes 294912 | tf_op jit(solution)/shard_map/reduce_scatter | solution.py:90
  14.0 109.4 %reduce-scatter.7.cloned.1.call-start = ((), (), s32[]{:S(2)}) async-start(), calls=%async_computation.7 | async-start | bytes 294912 | tf_op jit(solution)/shard_map/reduce_scatter | solution.py:90
  15.9 121.3 %reduce-scatter.9.cloned.1.call-start = ((), (), s32[]{:S(2)}) async-start(), calls=%async_computation.9 | async-start | bytes 294912 | tf_op jit(solution)/shard_map/reduce_scatter | solution.py:90
  17.9 135.9 %reduce-scatter.11.cloned.1.call-start = ((), (), s32[]{:S(2)}) async-start(), calls=%async_computation.11 | async-start | bytes 294912 | tf_op jit(solution)/shard_map/reduce_scatter | solution.py:90
  19.0 3.3 copy-start.5
  19.0 3.4 copy-start.11
  19.0 4.1 copy-start.1
  19.9 31.6 %copy-start.6 = (bf16[2,2,3,2,64]{4,3,2,1,0:T(2,128)(2,1)S(1)}, bf16[2,2,3,2,64]{4,3,2,1,0:T(2,128)(2,1)}, u32[]{:S(2)}) copy-start(bf16[2,2,3,2,64]{4,3,2,1,0:T(2,128)(2,1)} %param.28) | copy-start | bytes 9220
  19.9 187.7 %all-gather.5.cloned.1.call-start = ((), (), s32[]{:S(2)}) async-start(), calls=%async_computation.4 | async-start | bytes 9437184 | tf_op jit(solution)/shard_map/all_gather | solution.py:65
  22.2 42.1 %copy-start.7 = (s32[4,2,16]{2,1,0:T(2,128)S(1)}, s32[4,2,16]{2,1,0:T(2,128)}, u32[]{:S(2)}) copy-start(s32[4,2,16]{2,1,0:T(2,128)} %param.29) | copy-start | bytes 1540
  22.2 82.3 %copy-start.4 = (bf16[2,2,8,64,3]{3,2,4,1,0:T(8,128)(2,1)S(1)}, bf16[2,2,8,64,3]{3,2,4,1,0:T(8,128)(2,1)}, u32[]{:S(2)}) copy-start(bf16[2,2,8,64,3]{3,2,4,1,0:T(8,128)(2,1)} %param.27) | copy-start | bytes 36868
  22.2 95.0 %copy-start.12 = (f32[8]{0:T(128)S(1)}, f32[8]{0:T(128)}, u32[]{:S(2)}) copy-start(f32[8]{0:T(128)} %param.22) | copy-start | bytes 100
  22.2 95.3 %copy-start.9 = (f32[8]{0:T(128)S(1)}, f32[8]{0:T(128)}, u32[]{:S(2)}) copy-start(f32[8]{0:T(128)} %param.21) | copy-start | bytes 100
  22.2 95.4 %copy-start.3 = (bf16[4,512]{1,0:T(4,128)(2,1)S(1)}, bf16[4,512]{1,0:T(4,128)(2,1)}, u32[]{:S(2)}) copy-start(bf16[4,512]{1,0:T(4,128)(2,1)} %param.19) | copy-start | bytes 12292
  22.3 249.7 %all-gather.7.cloned.1.call-start = ((), (), s32[]{:S(2)}) async-start(), calls=%async_computation.6 | async-start | bytes 9437184 | tf_op jit(solution)/shard_map/all_gather | solution.py:65
  104.1 13.6 %collective-permute-start = (bf16[2,2,2,64]{3,1,2,0:T(2,128)(2,1)S(1)}, bf16[2,2,2,64]{3,1,2,0:T(2,128)(2,1)S(1)}, u32[]{:S(2)}, u32[]{:S(2)}) collective-permute-start(bf16[2,2,2,64]{3,1,2,0:T(2,128)(2,1)S(1)} %get-tuple-element.101), channel_id=1, source_target_pairs={{0,1},{1,0},{2,3},{3,2},{4,5},{5,4},{6,7},{7,6},{8,9},{9,8},{10,11... | collective-permute-start | bytes 3080 | tf_op jit(solution)/shard_map/ppermute | solution.py:15
  117.8 4.7 collective-permute-start.1
  219.4 117.1 %all-gather.9.cloned.1.call-start = ((), (), s32[]{:S(2)}) async-start(), calls=%async_computation.8 | async-start | bytes 9437184 | tf_op jit(solution)/shard_map/all_gather | solution.py:65
  219.4 3.7 collective-permute-start.2
  223.2 4.5 collective-permute-start.3
  283.8 117.1 %all-gather.11.cloned.1.call-start = ((), (), s32[]{:S(2)}) async-start(), calls=%async_computation.10 | async-start | bytes 9437184 | tf_op jit(solution)/shard_map/all_gather | solution.py:65
  283.9 3.9 collective-permute-start.4
  287.8 4.5 collective-permute-start.5
  347.1 7.6 %copy-start.8 = (f32[512]{0:T(512)S(1)}, f32[512]{0:T(512)}, u32[]{:S(2)}) copy-start(f32[512]{0:T(512)} %param.24) | copy-start | bytes 6148
  347.1 8.3 %copy-start.13 = (u32[256]{0:T(256)S(1)}, u32[256]{0:T(256)}, u32[]{:S(2)}) copy-start(u32[256]{0:T(256)} %constant.86) | copy-start | bytes 3076
  348.3 3.7 collective-permute-start.6
  352.0 4.5 collective-permute-start.7
  400.9 10.8 %copy-start.10 = (f32[8]{0:T(128)S(1)}, f32[8]{0:T(128)}, u32[]{:S(2)}) copy-start(f32[8]{0:T(128)} %param.23) | copy-start | bytes 100
Sparse Core Ops, SparseCore 0:
  14.1 35.6 reduce-scatter.4
  52.4 32.1 reduce-scatter.6
  87.1 31.9 reduce-scatter.8
  121.6 32.1 reduce-scatter.10
  156.1 51.3 all-gather.4
  219.5 52.4 all-gather.6
  283.9 52.4 all-gather.8
  348.4 52.4 all-gather.10
where the time goes:
time: 769 us; the launch traced here: 759 us
  blocking collectives  464 us (60%)
  waiting for transfers between devices  187 us (24%)
  matrix products  51.4 us (7%)
  local copies, waits for them, and re-layouts  25.6 us (3%)
  between operations  15.2 us (2%)
  starting transfers between devices  13.4 us (2%)
    all_gather x4, waiting for transfers between devices, local(): lax.all_gather(ssm_held, 'beam', axis=1, tiled=True)  170 us
    unnamed x1, blocking collectives  145 us
    psum x1, blocking collectives, local(): totals = lax.psum(stat_terms, 'row')  138 us
    all_gather x4, blocking collectives, local(): lax.all_gather(conv_held, 'beam', axis=1, tiled=True)  51.3 us
    all_gather x4, blocking collectives, local(): lax.all_gather(rim_held, 'beam', axis=1, tiled=True)  51.2 us
    all_gather x4, blocking collectives, local(): lax.all_gather(normed, 'beam', axis=1, tiled=True)  51 us
    dot_general x4, matrix products, local(): jnp.einsum('sij,sjhpn->sihpn', choose, pieces[0], preferred_element_type=...  42.5 us
    psum x1, blocking collectives, local(): bc_sum, dt_sum = lax.psum((bc_part, dt_part), 'beam')  27.4 us
  transfers between devices with their start and end apart: 16, of which 12 were waited for; matrix products, arithmetic and copies ran while one was open for 3% of the time, Pallas kernels for 0%

commit v1 on v0

v1 whole, which is shorter than its diff:
```python
import jax
import jax.numpy as jnp
from jax import lax
from jax.experimental import pallas as pl
from jax.experimental.pallas import tpu as pltpu
from jax.sharding import PartitionSpec as P

EPS = 1e-05
F32 = jnp.float32
BF16 = jnp.bfloat16
STEPS = 4
SESS = 2
WIDTH = 16
BEAMS = SESS * WIDTH
ROWS = STEPS * BEAMS
HD = 64
NS = 256
GROUP_CH = 2048.0


def row_of(step, s, b):
    v = s * WIDTH + b
    return (v % 4) * 32 + (v // 4) * 4 + step


def dot(a, b):
    return jnp.dot(a, b, preferred_element_type=F32)


def dot_t(a, b):
    return lax.dot_general(a, b, (((1,), (1,)), ((), ())), preferred_element_type=F32)


def lineage(par):
    r = lax.broadcasted_iota(jnp.int32, (ROWS, 1), 0)
    t = r & 3
    s = (r & 31) >> 4
    before = (par & 3) * 32 + (s * 4 + (par >> 2)) * 4 + t - 1
    before = jnp.where(t > 0, before, -1)
    start = jnp.where(t == 0, (par >> 1) * 4 + s * 2 + (par & 1), -1)
    lanes = lax.broadcasted_iota(jnp.int32, (ROWS, ROWS), 1)
    a1 = jnp.where(lanes == before, 1.0, 0.0)
    lanes_i = lax.broadcasted_iota(jnp.int32, (ROWS, BEAMS), 1)
    g = jnp.where(lanes_i == start, 1.0, 0.0)
    a1b = a1.astype(BF16)
    a2 = dot(a1b, a1b)
    a3 = dot(a1b, a2.astype(BF16))
    gb = g.astype(BF16)
    g1 = dot(a1b, gb)
    g2 = dot(a1b, g1.astype(BF16))
    g3 = dot(a1b, g2.astype(BF16))
    return t, a1, a2, a3, g + g1 + g2 + g3


def conv_kernel(recv, par, taps, sum_out, conv_out, bc_out, dt_out, fin_out, init):
    total = recv[0, 0:ROWS, :].astype(F32)
    dt = recv[0, 128:144, :].astype(F32)
    for k in range(3):
        init[k, 0:4, :] = dt[4 * k : 4 * k + 4]
    for i in range(1, 8):
        total = total + recv[i, 0:ROWS, :].astype(F32)
        extra = recv[i, 128:144, :].astype(F32)
        for k in range(3):
            init[k, 4 * i : 4 * i + 4, :] = extra[4 * k : 4 * k + 4]
        dt = dt + extra
    dt_out[...] = dt[12:13, 0:128] + dt[12:13, 128:256]
    new = total.astype(BF16)
    t, a1, a2, a3, g = lineage(par[...])
    gb = g.astype(BF16)
    start = [dot(gb, init[k].astype(BF16)) for k in range(3)]
    past1 = dot(a1.astype(BF16), new) + jnp.where(t == 0, start[2], 0.0)
    past2 = dot(a2.astype(BF16), new) + jnp.where(t == 0, start[1], 0.0) + jnp.where(t == 1, start[2], 0.0)
    past3 = (
        dot(a3.astype(BF16), new)
        + jnp.where(t == 0, start[0], 0.0)
        + jnp.where(t == 1, start[1], 0.0)
        + jnp.where(t == 2, start[2], 0.0)
    )
    w = taps[...]
    mixed = w[0:1] * past3 + w[1:2] * past2 + w[2:3] * past1 + w[3:4] * new.astype(F32)
    conv = mixed / (1.0 + jnp.exp(-mixed))
    sum_out[...] = new
    conv_out[...] = conv[:, 0:128].astype(BF16)
    bc_out[...] = conv[:, 128:256].astype(BF16)
    e = lax.broadcasted_iota(jnp.int32, (BEAMS, ROWS), 0)
    b = (e >> 2) * 2 + (e & 1)
    s = (e >> 1) & 1
    last = (b & 3) * 32 + (s * 4 + (b >> 2)) * 4 + STEPS - 1
    pick = jnp.where(lax.broadcasted_iota(jnp.int32, (BEAMS, ROWS), 1) == last, 1.0, 0.0).astype(BF16)
    fin_out[0] = dot(pick, past2.astype(BF16)).astype(BF16)
    fin_out[1] = dot(pick, past1.astype(BF16)).astype(BF16)
    fin_out[2] = dot(pick, new).astype(BF16)


def group_columns(blocks, low_row):
    b_cols, c_cols = [], []
    for q in range(4):
        part = jnp.zeros((ROWS, 128), F32)
        for k in range(4):
            part = part + jnp.where(low_row == float(q ^ k), blocks[k], 0.0)
        b_cols.append(part[:, 0:64])
        c_cols.append(part[:, 64:128])
    return jnp.concatenate(b_cols, 1).astype(BF16), jnp.concatenate(c_cols, 1).astype(BF16)


def scan_kernel(
    par, new, conv, bc0, bc1, bc2, bc3, dt_raw, consts, state, send_out, b_out, coef_out, first_out
):
    blocks = [ref[...].astype(F32) for ref in (bc0, bc1, bc2, bc3)]
    b_in, c_out = group_columns(blocks, consts[4:5])
    t, a1, a2, a3, g = lineage(par[...])
    raw = dt_raw[...].astype(BF16).astype(F32) + consts[2:3]
    step_size = jnp.maximum(raw, 0.0) + jnp.log1p(jnp.exp(-jnp.abs(raw)))
    rate = jnp.exp(consts[1:2])
    log_decay = -rate * step_size
    rr = lax.broadcasted_iota(jnp.int32, (ROWS, ROWS), 0)
    cc = lax.broadcasted_iota(jnp.int32, (ROWS, ROWS), 1)
    eye = jnp.where(rr == cc, 1.0, 0.0)
    path1 = jnp.sum(eye * log_decay, axis=1, keepdims=True)
    path2 = path1 + jnp.sum(a1 * log_decay, axis=1, keepdims=True)
    path3 = path2 + jnp.sum(a2 * log_decay, axis=1, keepdims=True)
    path4 = path3 + jnp.sum(a3 * log_decay, axis=1, keepdims=True)
    coef = (eye + a1 * jnp.exp(path1) + a2 * jnp.exp(path2) + a3 * jnp.exp(path3)) * step_size
    first = jnp.exp(path4)
    x_conv = conv[:, 0:64]
    inner = dot_t(c_out, b_in) * coef
    read = jnp.dot(inner, x_conv.astype(F32), precision=lax.Precision.HIGHEST, preferred_element_type=F32)
    lanes_i = lax.broadcasted_iota(jnp.int32, (ROWS, BEAMS), 1).astype(F32)
    origin = jnp.sum(g * lanes_i, axis=1, keepdims=True)
    half = jnp.where(lax.broadcasted_iota(jnp.int32, (ROWS, 128), 1) < 64, 0.0, 1.0)
    origin_b = jnp.broadcast_to(origin, (ROWS, 128)) - half
    acc = jnp.zeros((ROWS, 128), F32)
    for p in range(BEAMS // 2):
        both = state[2 * p : 2 * p + 2].reshape(2 * HD, NS)
        acc = acc + jnp.where(origin_b == float(2 * p), dot_t(c_out, both), 0.0)
    old = acc[:, 0:64] + acc[:, 64:128]
    x_val = x_conv.astype(F32)
    read = read + first * old + consts[3:4, 0:64] * x_val
    gate = new[:, 64:128].astype(F32)
    gated = read * (gate / (1.0 + jnp.exp(-gate)))
    square = jnp.sum(gated * gated, axis=1, keepdims=True)
    high = square.astype(BF16).astype(F32)
    rest = square - high
    lane = lax.broadcasted_iota(jnp.int32, (ROWS, 64), 1)
    stats = jnp.where(lane == 0, high, jnp.where(lane == 1, rest, 0.0))
    send_out[...] = jnp.concatenate([gated * consts[0:1, 0:64], stats], axis=1).astype(BF16)
    b_out[...] = b_in
    coef_out[...] = coef
    first_out[...] = jnp.broadcast_to(first, (ROWS, 128))


def final_kernel(parents, conv, b_in, coef, first, state, fin, out):
    x_t = conv[:, 0:128].astype(F32).T[0:64]
    b = b_in[...]
    for i in range(8):
        for j in range(4):
            s, beam = j // 2, 2 * i + j % 2
            row = row_of(STEPS - 1, s, beam)
            at = beam
            for step in range(STEPS - 1, -1, -1):
                at = parents[step * BEAMS + s * WIDTH + at]
            origin = (at >> 1) * 4 + s * 2 + (at & 1)
            left = (x_t * coef[row : row + 1, :]).astype(BF16)
            update = dot(left, b)
            keep = jnp.broadcast_to(first[row : row + 1, 0:1], (HD, NS))
            out[i, HD * j : HD * j + HD, :] = (keep * state[origin].astype(F32) + update).astype(BF16)
        taps = [fin[k, 4 * i : 4 * i + 4, 0:64].astype(F32) for k in range(3)]
        block = jnp.concatenate(taps + [jnp.zeros((4, 64), F32)], axis=1)
        out[i, 4 * HD : 4 * HD + 16, :] = jnp.concatenate([block, jnp.zeros((12, NS), F32)], axis=0).astype(BF16)


def out_kernel(place, recv, w_out, o0, o1, o2, o3, acc):
    low = place[1]
    stats = recv[0, :, 64:128].astype(F32)
    for i in range(1, 8):
        stats = stats + recv[i, :, 64:128].astype(F32)
    square = stats[:, 0:1] + stats[:, 1:2]
    high = square.astype(BF16).astype(F32)
    rest = square - high
    lane = lax.broadcasted_iota(jnp.int32, (ROWS, 128), 1)
    acc[:, 1024:1152] = jnp.where(lane == 0, high, jnp.where(lane == 1, rest, 0.0))
    left = jnp.concatenate([recv[i, :, 0:64] for i in range(8)], axis=1)
    acc[:, 0:1024] = dot(left, w_out[...])
    for k, ref in enumerate((o0, o1, o2, o3)):
        ref[...] = acc[pl.ds(pl.multiple_of((low ^ k) * 32, 32), 32), :].astype(BF16)


def norm_kernel(place, p0, p1, p2, p3, *refs):
    outs, acc = refs[:8], refs[8]
    total = p0[...].astype(F32) + p1[...].astype(F32) + p2[...].astype(F32) + p3[...].astype(F32)
    square = total[:, 1024:1025] + total[:, 1025:1026]
    scale = lax.rsqrt(square * (1.0 / GROUP_CH) + EPS)
    normed = total[:, 0:1024] * scale
    for m in range(8):
        acc[m] = normed[STEPS * m : STEPS * m + STEPS]
    for k, ref in enumerate(outs):
        ref[...] = acc[place[0] ^ k].astype(BF16)


def sum_kernel(p0, p1, p2, p3, p4, p5, p6, p7, out):
    total = p0[...].astype(F32)
    for ref in (p1, p2, p3, p4, p5, p6, p7):
        total = total + ref[...].astype(F32)
    out[...] = total.astype(BF16)


VM = pl.BlockSpec(memory_space=pltpu.VMEM)
SM = pl.BlockSpec(memory_space=pltpu.SMEM)
FAR = pl.BlockSpec(memory_space=pltpu.HBM)


def call(kernel, name, specs, outs, scratch=(), mib=6):
    def build(*args):
        far = [n for n, spec in enumerate(specs) if spec is FAR]
        count = len(specs)
        buffers = [pltpu.VMEM(args[n].shape, args[n].dtype) for n in far]
        sems = [pltpu.SemaphoreType.DMA((len(far),))] if far else []

        def body(*refs):
            ins = list(refs[:count])
            rest = refs[count : count + len(outs) + len(scratch)]
            held = refs[count + len(outs) + len(scratch) :]
            copies = [pltpu.make_async_copy(ins[n], held[k], held[-1].at[k]) for k, n in enumerate(far)]
            for copy in copies:
                copy.start()
            for copy in copies:
                copy.wait()
            for k, n in enumerate(far):
                ins[n] = held[k]
            kernel(*ins, *rest)

        return pl.pallas_call(
            body,
            name=name,
            in_specs=list(specs),
            out_specs=tuple(VM for _ in outs),
            out_shape=tuple(jax.ShapeDtypeStruct(s, d) for s, d in outs),
            scratch_shapes=list(scratch) + buffers + sems,
            compiler_params=pltpu.CompilerParams(vmem_limit_bytes=mib << 20),
        )(*args)

    return build


def swap(value, axis, count, mask):
    return lax.ppermute(value, axis, [(i, i ^ mask) for i in range(count)])


def local(
    x_in,
    w_inner,
    w_bc,
    w_dt,
    conv_x_w,
    conv_bc_w,
    dt_bias,
    a_log,
    d_skip,
    norm_gain,
    w_out,
    ssm_state,
    conv_x_state,
    conv_bc_state,
    parents,
):
    beam = lax.axis_index("beam")
    row = lax.axis_index("row")
    place = jnp.stack([beam, row & 3]).astype(jnp.int32)
    d_local = x_in.shape[-1]
    heads = ssm_state.shape[2]
    parent_column = parents.reshape(STEPS, 8, 4).transpose(2, 1, 0).reshape(ROWS, 1)
    x = x_in.reshape(STEPS, 8, 4, d_local).transpose(2, 1, 0, 3).reshape(ROWS, d_local)

    inner = jnp.einsum("rd,dzk->rzk", x, w_inner, preferred_element_type=F32).astype(BF16)
    inner = inner[:, ::-1].reshape(ROWS, 2, heads, HD).transpose(2, 0, 1, 3).reshape(heads, ROWS, 2 * HD)
    bc = jnp.einsum("rd,dzk->rzk", x, w_bc, preferred_element_type=F32).astype(BF16).reshape(ROWS, 128)
    top = jnp.concatenate([inner, jnp.broadcast_to(bc[None], (heads, ROWS, 128))], axis=2)
    dt = jnp.einsum("dh,rd->hr", w_dt, x, preferred_element_type=F32)
    dt_high = lax.reduce_precision(dt, 8, 7)
    dt_row = jnp.concatenate([dt_high, dt - dt_high], axis=1).astype(BF16)[:, None]
    taps_x = conv_x_state.transpose(2, 4, 0, 1, 3).reshape(heads, 12, HD)
    taps_bc = jnp.broadcast_to(conv_bc_state.transpose(2, 0, 1, 3, 4).reshape(1, 12, 128), (heads, 12, 128))
    extra = jnp.concatenate([taps_x, jnp.zeros((heads, 12, HD), BF16), taps_bc], axis=2)
    bottom = jnp.concatenate([extra, dt_row, jnp.zeros((heads, 3, 256), BF16)], axis=1)
    payload = jnp.concatenate([top, bottom], axis=1)
    recv = lax.all_to_all(payload, "beam", split_axis=0, concat_axis=0, tiled=True)

    conv_head = lax.dynamic_slice_in_dim(conv_x_w, beam * HD, HD, 1)
    taps = jnp.concatenate([conv_head, jnp.zeros((4, HD), BF16), conv_bc_w.reshape(4, 128)], axis=1).astype(F32)
    gain = jnp.pad(lax.dynamic_slice_in_dim(norm_gain, beam * HD, HD, 0), (0, HD)).reshape(1, 128)
    scalars = [lax.dynamic_slice_in_dim(v, beam, 1, 0) for v in (a_log, dt_bias, d_skip)] + [(row & 3).astype(F32)[None]]
    fills = [jnp.broadcast_to(v[:, None], (1, 128)) for v in scalars]
    consts = jnp.concatenate([gain] + fills + [jnp.zeros((3, 128), F32)], axis=0)
    by_head = ssm_state.transpose(2, 0, 1, 3, 4).reshape(heads, 4, HD, NS)
    taps, consts, by_head, place, parent_column = lax.optimization_barrier((taps, consts, by_head, place, parent_column))
    taps, consts, by_head, place, parent_column, recv = lax.optimization_barrier(
        (taps, consts, by_head, place, parent_column, recv)
    )
    state = lax.all_to_all(by_head, "beam", split_axis=0, concat_axis=0, tiled=True).reshape(BEAMS, HD, NS)

    new, conv, bc_conv, dt_raw, fin = call(
        conv_kernel,
        "conv",
        [FAR, VM, VM],
        [((ROWS, 256), BF16), ((ROWS, 128), BF16), ((ROWS, 128), BF16), ((1, ROWS), F32), ((3, BEAMS, 256), BF16)],
        [pltpu.VMEM((3, BEAMS, 256), F32)],
    )(recv, parent_column, taps)

    others = [swap(bc_conv, "row", 32, k) for k in (1, 2, 3)]

    send, b_in, coef, first = call(
        scan_kernel,
        "scan",
        [FAR] * 10,
        [((ROWS, 128), BF16), ((ROWS, NS), BF16), ((ROWS, ROWS), F32), ((ROWS, 128), F32)],
    )(parent_column, new, conv, bc_conv, *others, dt_raw, consts, state)

    gathered = lax.all_to_all(
        jnp.broadcast_to(send[None], (heads, ROWS, 128)), "beam", split_axis=0, concat_axis=0, tiled=True
    )
    (final,) = call(
        final_kernel,
        "final",
        [SM] + [FAR] * 6,
        [((heads, 4 * HD + 16, NS), BF16)],
    )(parents.reshape(ROWS), conv, b_in, coef, first, state, fin)
    home = lax.all_to_all(final, "beam", split_axis=0, concat_axis=0, tiled=True)

    parts = call(
        out_kernel,
        "project",
        [SM, FAR, VM],
        [((32, 1152), BF16)] * 4,
        [pltpu.VMEM((ROWS, 1152), F32)],
    )(place, gathered, w_out)
    got = [parts[0]] + [swap(parts[k], "row", 32, k) for k in (1, 2, 3)]
    place_z = jnp.stack([row >> 2]).astype(jnp.int32)
    pieces = call(norm_kernel, "norm", [SM] + [VM] * 4, [((STEPS, 1024), BF16)] * 8, [pltpu.VMEM((8, STEPS, 1024), F32)])(
        place_z, *got
    )
    far_first = (5, 7, 3, 1, 4, 6, 2)
    arrived = [pieces[0]] + [swap(pieces[k], "row", 32, k * 4) for k in far_first]
    (layer_out,) = call(sum_kernel, "total", [VM] * 8, [((STEPS, 1024), BF16)])(*arrived)
    layer_out = layer_out[:, None]

    ssm_final = home[:, : 4 * HD].reshape(heads, SESS, 2, HD, NS).transpose(1, 2, 0, 3, 4)
    conv_x_final = home[:, 4 * HD : 4 * HD + 4, :192].reshape(heads, SESS, 2, 3, HD).transpose(1, 2, 0, 4, 3)
    own = lax.dynamic_slice_in_dim(fin, beam * 4, 4, 1)[:, :, 128:]
    conv_bc_final = own.reshape(3, SESS, 2, 2, 64).transpose(1, 2, 0, 3, 4)
    return layer_out, ssm_final, conv_x_final, conv_bc_final


def solution(mesh):
    placed = (
        P(None, None, None, "beam"),
        P("beam", None, "row"),
        P("beam", None, "row"),
        P("beam", "row"),
        P(None, "row"),
        P(None, None, "row"),
        P("row"),
        P("row"),
        P("row"),
        P("row"),
        P("row", "beam"),
        P(None, "beam", "row", None, None),
        P(None, "beam", "row", None, None),
        P(None, "beam", None, None, "row"),
        P(),
    )
    return jax.shard_map(
        local,
        mesh=mesh,
        in_specs=placed,
        out_specs=(
            P(None, "row", "beam"),
            P(None, "beam", "row", None, None),
            P(None, "beam", "row", None, None),
            P(None, "beam", None, None, "row"),
        ),
        check_vma=False,
    )
```

time: 769 us -> 108 us (0.14); the launches traced: 759 us -> 106 us
  blocking collectives: 464 us -> 0 us
  waiting for transfers between devices: 187 us -> 21.7 us
  matrix products: 51.4 us -> 0.86 us
  starting transfers between devices: 13.4 us -> 43.4 us
  between operations: 15.2 us -> 1.07 us
    all_gather x4 -> x0, waiting for transfers between devices: 170 us -> none  [local(): lax.all_gather(ssm_held, 'beam', axis=1, tiled=True)]
    psum x2 -> x0, blocking collectives: 166 us -> none  [the longest x1 138 us: local(): totals = lax.psum(stat_terms, 'row')]
    all_gather x12 -> x0, blocking collectives: 154 us -> none  [the longest x4 51.3 us: local(): lax.all_gather(conv_held, 'beam', axis=1, tiled=True)]
    unnamed x1 -> x0, blocking collectives: 145 us -> none
    dot_general x28 -> x2, matrix products: 51.4 us -> 0.61 us  [the longest x1 0.45 us: local(): jnp.einsum('rd,dzk->rzk', x, w_inner, preferred_element_type=F32)]
    all_to_all x0 -> x4, starting transfers between devices: none -> 15.5 us  [the longest x1 4.3 us: local(): lax.all_to_all(payload, 'beam', split_axis=0, concat_axis=0, tiled=True)]
    ppermute x8 -> x13, starting transfers between devices: 13.1 us -> 27.9 us  [swap(): return lax.ppermute(value, axis, [(i, i ^ mask) for i in range(count)])]
    all_to_all x0 -> x4, waiting for transfers between devices: none -> 9.91 us  [the longest x1 4.66 us: local(): lax.all_to_all(by_head, 'beam', split_axis=0, concat_axis=0, tiled=True)]
  transfers between devices with their start and end apart: 16 -> 17, of which waited for: 12 -> 10; matrix products, arithmetic and copies ran while one was open for 3% -> 9% of each run, Pallas kernels for 0% -> 5%
where the time goes in v1:
time: 108 us; the launch traced here: 106 us
  starting transfers between devices  43.4 us (40%)
  local copies, waits for them, and re-layouts  31.3 us (29%)
  waiting for transfers between devices  21.7 us (20%)
  Pallas kernels  6.62 us (6%)
  other arithmetic  1.58 us (1%)
    ppermute x13, starting transfers between devices, swap(): return lax.ppermute(value, axis, [(i, i ^ mask) for i in range(count)])  27.9 us
    unnamed x68, local copies, waits for them, and re-layouts  12.8 us
    ppermute x13, waiting for transfers between devices, swap(): return lax.ppermute(value, axis, [(i, i ^ mask) for i in range(count)])  11.7 us
    pallas_call x6, Pallas kernels, build(): pl.pallas_call(body, name=name, in_specs=list(specs), out_specs=tuple((VM...  6.62 us
    all_to_all x1, waiting for transfers between devices, local(): lax.all_to_all(by_head, 'beam', split_axis=0, concat_axis=0, tiled=True)  4.66 us
    all_to_all x1, starting transfers between devices, local(): lax.all_to_all(payload, 'beam', split_axis=0, concat_axis=0, tiled=True)  4.3 us
    all_to_all x1, starting transfers between devices, local(): lax.all_to_all(final, 'beam', split_axis=0, concat_axis=0, tiled=True)  4.26 us
    all_to_all x1, waiting for transfers between devices, local(): lax.all_to_all(payload, 'beam', split_axis=0, concat_axis=0, tiled=True)  3.97 us
  transfers between devices with their start and end apart: 17, of which 10 were waited for; matrix products, arithmetic and copies ran while one was open for 9% of the time, Pallas kernels for 5%

profile of v1, /device:TPU:32, one launch (start us, length us, event | category | flops | bytes accessed | tf_op | source)
XLA Modules:
  0.0 106.5 jit_solution(3530145345464660462)
XLA Ops:
  0.7 1.2 %reshape.105 = bf16[4,8,4,1024]{3,2,1,0:T(4,128)(2,1)S(1)} reshape(bf16[4,2,16,1024]{3,2,1,0:T(8,128)(2,1)} %param.15) | data formatting | bytes 524288 | tf_op jit(solution)/shard_map/reshape | solution.py:272
  6.6 4.3 %all-to-all-start = ((bf16[8,144,256]{2,1,0:T(8,128)(2,1)}), bf16[8,144,256]{2,1,0:T(8,128)(2,1)S(1)}, u32[]{:S(2)}, u32[]{:S(2)}) async-start(bf16[8,144,256]{2,1,0:T(8,128)(2,1)} %maximum_maximum_fusion), calls=%async_computation | async-start | bytes 1179648 | tf_op jit(solution)/shard_map/all_to_all | solution.py:286
  17.9 4.0 %all-to-all-done.refs_0_ = bf16[8,144,256]{2,1,0:T(8,128)(2,1)S(1)} async-done(((bf16[8,144,256]{2,1,0:T(8,128)(2,1)}), bf16[8,144,256]{2,1,0:T(8,128)(2,1)S(1)}, u32[]{:S(2)}, u32[]{:S(2)}) %all-to-all-start) | async-done | bytes 589856 | tf_op jit(solution)/shard_map/all_to_all | solution.py:286
  21.9 2.5 %copy.63 = bf16[8,4,64,256]{3,2,1,0:T(8,128)(2,1)} copy(bf16[8,4,64,256]{3,2,0,1:T(8,128)(2,1)} %bitcast.50) | data formatting | bytes 2097152 | tf_op jit(solution)/shard_map/optimization_barrier | solution.py:296
  24.4 3.6 %all-to-all-start.1 = ((bf16[8,4,64,256]{3,2,1,0:T(8,128)(2,1)}), bf16[8,4,64,256]{3,2,1,0:T(8,128)(2,1)S(1)}, u32[]{:S(2)}, u32[]{:S(2)}) async-start(bf16[8,4,64,256]{3,2,1,0:T(8,128)(2,1)} %copy.63), calls=%async_computation.1 | async-start | bytes 2097152 | tf_op jit(solution)/shard_map/all_to_all | solution.py:299
  28.1 1.1 copy-done.3
  29.2 1.1 %conv.1 = (bf16[128,256]{1,0:T(8,128)(2,1)S(1)}, bf16[128,128]{1,0:T(8,128)(2,1)S(1)}, bf16[128,128]{1,0:T(8,128)(2,1)S(1)}, f32[1,128]{1,0:T(1,128)S(1)}, bf16[3,32,256]{2,1,0:T(8,128)(2,1)S(1)}) custom-call(bf16[8,144,256]{2,1,0:T(8,128)(2,1)S(1)} %copy-done.3, s32[128,1]{1,0:T(8,128)S(1)} %copy.64.refs_1_.refs_0_, f32[4,256]{1,0:T(4,128)S(1)} %maximum_convert_fusion.refs_2_), custom_call_target="tpu_custom_call" | custom-call | tf_op jit(solution)/shard_map/conv/pallas_call | solution.py:232
  30.8 1.9 %collective-permute-start.2 = (bf16[128,128]{1,0:T(8,128)(2,1)S(1)}, bf16[128,128]{1,0:T(8,128)(2,1)S(1)}, u32[]{:S(2)}, u32[]{:S(2)}) collective-permute-start(bf16[128,128]{1,0:T(8,128)(2,1)S(1)} %get-tuple-element.47.refs_3_), channel_id=1, source_target_pairs={{0,3},{1,2},{2,1},{3,0},{4,7},{5,6},{6,5},{7,4},{8,11},{9,10},{10,... | collective-permute-start | bytes 98312 | tf_op jit(solution)/shard_map/ppermute | solution.py:246
  32.7 1.4 %collective-permute-start.1 = (bf16[128,128]{1,0:T(8,128)(2,1)S(1)}, bf16[128,128]{1,0:T(8,128)(2,1)S(1)}, u32[]{:S(2)}, u32[]{:S(2)}) collective-permute-start(bf16[128,128]{1,0:T(8,128)(2,1)S(1)} %get-tuple-element.47.refs_3_), channel_id=1, source_target_pairs={{0,2},{1,3},{2,0},{3,1},{4,6},{5,7},{6,4},{7,5},{8,10},{9,11},{10,... | collective-permute-start | bytes 98312 | tf_op jit(solution)/shard_map/ppermute | solution.py:246
  34.1 1.4 %collective-permute-start = (bf16[128,128]{1,0:T(8,128)(2,1)S(1)}, bf16[128,128]{1,0:T(8,128)(2,1)S(1)}, u32[]{:S(2)}, u32[]{:S(2)}) collective-permute-start(bf16[128,128]{1,0:T(8,128)(2,1)S(1)} %get-tuple-element.47.refs_3_), channel_id=1, source_target_pairs={{0,1},{1,0},{2,3},{3,2},{4,5},{5,4},{6,7},{7,6},{8,9},{9,8},{10,11... | collective-permute-start | bytes 98312 | tf_op jit(solution)/shard_map/ppermute | solution.py:246
  39.2 4.7 %all-to-all-done.1 = bf16[8,4,64,256]{3,2,1,0:T(8,128)(2,1)S(1)} async-done(((bf16[8,4,64,256]{3,2,1,0:T(8,128)(2,1)}), bf16[8,4,64,256]{3,2,1,0:T(8,128)(2,1)S(1)}, u32[]{:S(2)}, u32[]{:S(2)}) %all-to-all-start.1) | async-done | bytes 1048608 | tf_op jit(solution)/shard_map/all_to_all | solution.py:299
  48.3 1.6 %scan.1 = (bf16[128,128]{1,0:T(8,128)(2,1)S(1)}, bf16[128,256]{1,0:T(8,128)(2,1)S(1)}, f32[128,128]{1,0:T(8,128)S(1)}, f32[128,128]{1,0:T(8,128)S(1)}) custom-call(s32[128,1]{1,0:T(8,128)S(1)} %copy.64.refs_1_.refs_0_, bf16[128,256]{1,0:T(8,128)(2,1)S(1)} %get-tuple-element.45.refs_1_, bf16[128,128]{1,0:T(8,128)(2,1)S(1)} %get-tuple-element.46.refs_2_.refs_1_, ...), custom_call_target="tpu_custom_call" | custom-call | tf_op jit(solution)/shard_map/scan/pallas_call | solution.py:232
  50.7 3.4 %all-to-all-start.2 = ((bf16[8,128,128]{2,1,0:T(8,128)(2,1)}), bf16[8,128,128]{2,1,0:T(8,128)(2,1)S(1)}, u32[]{:S(2)}, u32[]{:S(2)}) async-start(bf16[8,128,128]{2,1,0:T(8,128)(2,1)} %broadcast_in_dim.80), calls=%async_computation.2 | async-start | bytes 524288 | tf_op jit(solution)/shard_map/all_to_all | solution.py:318
  54.1 1.3 %reshape.111.refs_0_ = s32[128]{0:T(128)} reshape(s32[4,2,16]{2,1,0:T(2,128)} %param.29) | data formatting | bytes 1024 | tf_op jit(solution)/shard_map/reshape | solution.py:326
  57.7 1.5 %final.1 = bf16[8,272,256]{2,1,0:T(8,128)(2,1)S(1)} custom-call(s32[128]{0:T(128)S(1)} %copy-done.18, bf16[128,128]{1,0:T(8,128)(2,1)S(1)} %get-tuple-element.46.refs_2_.refs_1_, bf16[128,256]{1,0:T(8,128)(2,1)S(1)} %get-tuple-element.64.refs_2_, f32[128,128]{1,0:T(8,128)S(1)} %copy-done.6, f32[128,128]{1,0:T(8,128)S(1)} %copy-done.8, ...), custom_call_target="tpu_custom_call" | custom-call | tf_op jit(solution)/shard_map/final/pallas_call | solution.py:232
  59.2 1.0 copy-done.1
  60.2 1.3 %all-to-all-done.2.refs_1_ = bf16[8,128,128]{2,1,0:T(8,128)(2,1)S(1)} async-done(((bf16[8,128,128]{2,1,0:T(8,128)(2,1)}), bf16[8,128,128]{2,1,0:T(8,128)(2,1)S(1)}, u32[]{:S(2)}, u32[]{:S(2)}) %all-to-all-start.2) | async-done | bytes 262176 | tf_op jit(solution)/shard_map/all_to_all | solution.py:318
  61.5 4.3 %all-to-all-start.3 = ((bf16[8,272,256]{2,1,0:T(8,128)(2,1)}), bf16[8,272,256]{2,1,0:T(8,128)(2,1)}, u32[]{:S(2)}, u32[]{:S(2)}) async-start(bf16[8,272,256]{2,1,0:T(8,128)(2,1)} %copy-done.1), calls=%async_computation.3 | async-start | bytes 2228224 | tf_op jit(solution)/shard_map/all_to_all | solution.py:327
  65.8 1.6 %project.1 = (bf16[32,1152]{1,0:T(8,128)(2,1)S(1)}, bf16[32,1152]{1,0:T(8,128)(2,1)}, bf16[32,1152]{1,0:T(8,128)(2,1)}, bf16[32,1152]{1,0:T(8,128)(2,1)}) custom-call(s32[2]{0:T(128)S(1)} %copy-done.21, bf16[8,128,128]{2,1,0:T(8,128)(2,1)S(1)} %all-to-all-done.2.refs_1_, bf16[512,1024]{1,0:T(8,128)(2,1)S(1)} %copy-done.4), custom_call_target="tpu_custom_call" | custom-call | tf_op jit(solution)/shard_map/project/pallas_call | solution.py:232
  67.4 1.1 %collective-permute-start.3 = (bf16[32,1152]{1,0:T(8,128)(2,1)}, bf16[32,1152]{1,0:T(8,128)(2,1)S(1)}, u32[]{:S(2)}, u32[]{:S(2)}) collective-permute-start(bf16[32,1152]{1,0:T(8,128)(2,1)} %get-tuple-element.53), channel_id=1, source_target_pairs={{0,1},{1,0},{2,3},{3,2},{4,5},{5,4},{6,7},{7,6},{8,9},{9,8},{10,11... | collective-permute-start | bytes 221192 | tf_op jit(solution)/shard_map/ppermute | solution.py:246
  68.5 2.4 %collective-permute-start.4 = (bf16[32,1152]{1,0:T(8,128)(2,1)}, bf16[32,1152]{1,0:T(8,128)(2,1)S(1)}, u32[]{:S(2)}, u32[]{:S(2)}) collective-permute-start(bf16[32,1152]{1,0:T(8,128)(2,1)} %get-tuple-element.54), channel_id=1, source_target_pairs={{0,2},{1,3},{2,0},{3,1},{4,6},{5,7},{6,4},{7,5},{8,10},{9,11},{10,... | collective-permute-start | bytes 221192 | tf_op jit(solution)/shard_map/ppermute | solution.py:246
  72.3 4.8 %collective-permute-done.4.refs_3_ = bf16[32,1152]{1,0:T(8,128)(2,1)S(1)} collective-permute-done((bf16[32,1152]{1,0:T(8,128)(2,1)}, bf16[32,1152]{1,0:T(8,128)(2,1)S(1)}, u32[]{:S(2)}, u32[]{:S(2)}) %collective-permute-start.4) | collective-permute-done | bytes 73760 | tf_op jit(solution)/shard_map/ppermute | solution.py:246
  77.0 1.8 %collective-permute-done.5.refs_4_ = bf16[32,1152]{1,0:T(8,128)(2,1)S(1)} collective-permute-done((bf16[32,1152]{1,0:T(8,128)(2,1)}, bf16[32,1152]{1,0:T(8,128)(2,1)S(1)}, u32[]{:S(2)}, u32[]{:S(2)}) %collective-permute-start.5) | collective-permute-done | bytes 73760 | tf_op jit(solution)/shard_map/ppermute | solution.py:246
  79.0 8.4 %collective-permute-start.6 = (bf16[4,1024]{1,0:T(4,128)(2,1)S(1)}, bf16[4,1024]{1,0:T(4,128)(2,1)S(1)}, u32[]{:S(2)}, u32[]{:S(2)}) collective-permute-start(bf16[4,1024]{1,0:T(4,128)(2,1)S(1)} %get-tuple-element.57), channel_id=1, source_target_pairs={{0,20},{1,21},{2,22},{3,23},{4,16},{5,17},{6,18},{7,19},{8,28},{9,... | collective-permute-start | bytes 24584 | tf_op jit(solution)/shard_map/ppermute | solution.py:246
  88.2 4.3 %collective-permute-start.8 = (bf16[4,1024]{1,0:T(4,128)(2,1)S(1)}, bf16[4,1024]{1,0:T(4,128)(2,1)S(1)}, u32[]{:S(2)}, u32[]{:S(2)}) collective-permute-start(bf16[4,1024]{1,0:T(4,128)(2,1)S(1)} %get-tuple-element.59), channel_id=1, source_target_pairs={{0,12},{1,13},{2,14},{3,15},{4,8},{5,9},{6,10},{7,11},{8,4},{9,5},... | collective-permute-start | bytes 24584 | tf_op jit(solution)/shard_map/ppermute | solution.py:246
  92.5 1.3 %collective-permute-start.9 = (bf16[4,1024]{1,0:T(4,128)(2,1)S(1)}, bf16[4,1024]{1,0:T(4,128)(2,1)S(1)}, u32[]{:S(2)}, u32[]{:S(2)}) collective-permute-start(bf16[4,1024]{1,0:T(4,128)(2,1)S(1)} %get-tuple-element.60), channel_id=1, source_target_pairs={{0,4},{1,5},{2,6},{3,7},{4,0},{5,1},{6,2},{7,3},{8,12},{9,13},{10,... | collective-permute-start | bytes 24584 | tf_op jit(solution)/shard_map/ppermute | solution.py:246
  93.8 3.4 %collective-permute-start.10 = (bf16[4,1024]{1,0:T(4,128)(2,1)S(1)}, bf16[4,1024]{1,0:T(4,128)(2,1)S(1)}, u32[]{:S(2)}, u32[]{:S(2)}) collective-permute-start(bf16[4,1024]{1,0:T(4,128)(2,1)S(1)} %get-tuple-element.61), channel_id=1, source_target_pairs={{0,16},{1,17},{2,18},{3,19},{4,20},{5,21},{6,22},{7,23},{8,24},{9,... | collective-permute-start | bytes 24584 | tf_op jit(solution)/shard_map/ppermute | solution.py:246
  97.2 1.1 collective-permute-start.11
  99.0 1.0 collective-permute-done.9.refs_4_
  100.1 2.0 %collective-permute-done.11.refs_6_ = bf16[4,1024]{1,0:T(4,128)(2,1)S(1)} collective-permute-done((bf16[4,1024]{1,0:T(4,128)(2,1)S(1)}, bf16[4,1024]{1,0:T(4,128)(2,1)S(1)}, u32[]{:S(2)}, u32[]{:S(2)}) %collective-permute-start.11) | collective-permute-done | bytes 8224 | tf_op jit(solution)/shard_map/ppermute | solution.py:246
  102.7 1.3 %slice.12 = bf16[8,256,256]{2,1,0:T(8,128)(2,1)S(1)} slice(bf16[8,272,256]{2,1,0:T(8,128)(2,1)} %all-to-all-done.3), slice={[0:8], [0:256], [0:256]} | slice | bytes 2097152 | tf_op jit(solution)/shard_map/slice | solution.py:346
  104.0 1.0 copy.75
  (133 shorter events, 28.5 us)
Async XLA Ops:
  0.6 3.0 %copy-start = (bf16[1024,2,512]{2,1,0:T(2,128)(2,1)S(1)}, bf16[1024,2,512]{2,1,0:T(2,128)(2,1)}, u32[]{:S(2)}) copy-start(bf16[1024,2,512]{2,1,0:T(2,128)(2,1)} %param.16) | copy-start | bytes 6291460
  0.6 1.6 %copy-start.27 = (bf16[2,2,3,2,64]{4,3,2,1,0:T(2,128)(2,1)S(1)}, bf16[2,2,3,2,64]{4,3,2,1,0:T(2,128)(2,1)}, u32[]{:S(2)}) copy-start(bf16[2,2,3,2,64]{4,3,2,1,0:T(2,128)(2,1)} %param.28) | copy-start | bytes 9220
  0.7 1.7 %copy-start.24 = (bf16[2,2,8,64,3]{3,2,4,1,0:T(8,128)(2,1)S(1)}, bf16[2,2,8,64,3]{3,2,4,1,0:T(8,128)(2,1)}, u32[]{:S(2)}) copy-start(bf16[2,2,8,64,3]{3,2,4,1,0:T(8,128)(2,1)} %param.27) | copy-start | bytes 36868
  4.3 1.2 %copy-start.23 = (bf16[8,12,64]{2,1,0:T(8,128)(2,1)S(1)}, bf16[8,12,64]{2,1,0:T(8,128)(2,1)}, u32[]{:S(2)}) copy-start(bf16[8,12,64]{2,1,0:T(8,128)(2,1)} %copy.59) | copy-start | bytes 36868
  4.3 1.2 %copy-start.29 = (bf16[144]{0:T(256)(128)(2,1)S(1)}, bf16[144]{0:T(256)(128)(2,1)}, u32[]{:S(2)}) copy-start(bf16[144]{0:T(256)(128)(2,1)} %pad.12.clone) | copy-start | bytes 868
  5.5 5.3 %copy-start.30 = (f32[8]{0:T(128)S(1)}, f32[8]{0:T(128)}, u32[]{:S(2)}) copy-start(f32[8]{0:T(128)} %param.23) | copy-start | bytes 100
  5.5 6.0 %copy-start.31 = (f32[8]{0:T(128)S(1)}, f32[8]{0:T(128)}, u32[]{:S(2)}) copy-start(f32[8]{0:T(128)} %param.22) | copy-start | bytes 100
  5.5 6.6 %copy-start.32 = (f32[8]{0:T(128)S(1)}, f32[8]{0:T(128)}, u32[]{:S(2)}) copy-start(f32[8]{0:T(128)} %param.21) | copy-start | bytes 100
  5.6 7.2 %copy-start.28 = (bf16[4,2,64]{2,1,0:T(2,128)(2,1)S(1)}, bf16[4,2,64]{2,1,0:T(2,128)(2,1)}, u32[]{:S(2)}) copy-start(bf16[4,2,64]{2,1,0:T(2,128)(2,1)} %param.20) | copy-start | bytes 3076
  5.6 7.3 %copy-start.26 = (s32[4,2,16]{2,1,0:T(2,128)S(1)}, s32[4,2,16]{2,1,0:T(2,128)}, u32[]{:S(2)}) copy-start(s32[4,2,16]{2,1,0:T(2,128)} %param.29) | copy-start | bytes 1540
  6.6 15.4 %all-to-all-start = ((bf16[8,144,256]{2,1,0:T(8,128)(2,1)}), bf16[8,144,256]{2,1,0:T(8,128)(2,1)S(1)}, u32[]{:S(2)}, u32[]{:S(2)}) async-start(bf16[8,144,256]{2,1,0:T(8,128)(2,1)} %maximum_maximum_fusion), calls=%async_computation | async-start | bytes 1179648 | tf_op jit(solution)/shard_map/all_to_all | solution.py:286
  21.9 2.5 %copy-start.2 = (bf16[8,144,256]{2,1,0:T(8,128)(2,1)}, bf16[8,144,256]{2,1,0:T(8,128)(2,1)S(1)}, u32[]{:S(2)}) copy-start(bf16[8,144,256]{2,1,0:T(8,128)(2,1)S(1)} %all-to-all-done.refs_0_) | copy-start | bytes 1769476
  24.4 19.5 %all-to-all-start.1 = ((bf16[8,4,64,256]{3,2,1,0:T(8,128)(2,1)}), bf16[8,4,64,256]{3,2,1,0:T(8,128)(2,1)S(1)}, u32[]{:S(2)}, u32[]{:S(2)}) async-start(bf16[8,4,64,256]{3,2,1,0:T(8,128)(2,1)} %copy.63), calls=%async_computation.1 | async-start | bytes 2097152 | tf_op jit(solution)/shard_map/all_to_all | solution.py:299
  28.1 1.1 %copy-start.3 = (bf16[8,144,256]{2,1,0:T(8,128)(2,1)S(1)}, bf16[8,144,256]{2,1,0:T(8,128)(2,1)}, u32[]{:S(2)}) copy-start(bf16[8,144,256]{2,1,0:T(8,128)(2,1)} %copy-done.2) | copy-start | bytes 1769476
  30.8 5.3 %collective-permute-start.2 = (bf16[128,128]{1,0:T(8,128)(2,1)S(1)}, bf16[128,128]{1,0:T(8,128)(2,1)S(1)}, u32[]{:S(2)}, u32[]{:S(2)}) collective-permute-start(bf16[128,128]{1,0:T(8,128)(2,1)S(1)} %get-tuple-element.47.refs_3_), channel_id=1, source_target_pairs={{0,3},{1,2},{2,1},{3,0},{4,7},{5,6},{6,5},{7,4},{8,11},{9,10},{10,... | collective-permute-start | bytes 98312 | tf_op jit(solution)/shard_map/ppermute | solution.py:246
  32.7 4.8 %collective-permute-start.1 = (bf16[128,128]{1,0:T(8,128)(2,1)S(1)}, bf16[128,128]{1,0:T(8,128)(2,1)S(1)}, u32[]{:S(2)}, u32[]{:S(2)}) collective-permute-start(bf16[128,128]{1,0:T(8,128)(2,1)S(1)} %get-tuple-element.47.refs_3_), channel_id=1, source_target_pairs={{0,2},{1,3},{2,0},{3,1},{4,6},{5,7},{6,4},{7,5},{8,10},{9,11},{10,... | collective-permute-start | bytes 98312 | tf_op jit(solution)/shard_map/ppermute | solution.py:246
  34.1 4.5 %collective-permute-start = (bf16[128,128]{1,0:T(8,128)(2,1)S(1)}, bf16[128,128]{1,0:T(8,128)(2,1)S(1)}, u32[]{:S(2)}, u32[]{:S(2)}) collective-permute-start(bf16[128,128]{1,0:T(8,128)(2,1)S(1)} %get-tuple-element.47.refs_3_), channel_id=1, source_target_pairs={{0,1},{1,0},{2,3},{3,2},{4,5},{5,4},{6,7},{7,6},{8,9},{9,8},{10,11... | collective-permute-start | bytes 98312 | tf_op jit(solution)/shard_map/ppermute | solution.py:246
  50.7 10.9 %all-to-all-start.2 = ((bf16[8,128,128]{2,1,0:T(8,128)(2,1)}), bf16[8,128,128]{2,1,0:T(8,128)(2,1)S(1)}, u32[]{:S(2)}, u32[]{:S(2)}) async-start(bf16[8,128,128]{2,1,0:T(8,128)(2,1)} %broadcast_in_dim.80), calls=%async_computation.2 | async-start | bytes 524288 | tf_op jit(solution)/shard_map/all_to_all | solution.py:318
  59.2 1.0 copy-start.1
  60.2 5.6 %copy-start.4 = (bf16[512,1024]{1,0:T(8,128)(2,1)S(1)}, bf16[512,1024]{1,0:T(8,128)(2,1)}, u32[]{:S(2)}) copy-start(bf16[512,1024]{1,0:T(8,128)(2,1)} %refs_2_.1) | copy-start | bytes 3145732
  60.2 5.6 %copy-start.21 = (s32[2]{0:T(128)S(1)}, s32[2]{0:T(128)}, u32[]{:S(2)}) copy-start(s32[2]{0:T(128)} %pad_add_fusion.refs_0_) | copy-start | bytes 28
  61.5 41.1 %all-to-all-start.3 = ((bf16[8,272,256]{2,1,0:T(8,128)(2,1)}), bf16[8,272,256]{2,1,0:T(8,128)(2,1)}, u32[]{:S(2)}, u32[]{:S(2)}) async-start(bf16[8,272,256]{2,1,0:T(8,128)(2,1)} %copy-done.1), calls=%async_computation.3 | async-start | bytes 2228224 | tf_op jit(solution)/shard_map/all_to_all | solution.py:327
  67.4 4.8 %collective-permute-start.3 = (bf16[32,1152]{1,0:T(8,128)(2,1)}, bf16[32,1152]{1,0:T(8,128)(2,1)S(1)}, u32[]{:S(2)}, u32[]{:S(2)}) collective-permute-start(bf16[32,1152]{1,0:T(8,128)(2,1)} %get-tuple-element.53), channel_id=1, source_target_pairs={{0,1},{1,0},{2,3},{3,2},{4,5},{5,4},{6,7},{7,6},{8,9},{9,8},{10,11... | collective-permute-start | bytes 221192 | tf_op jit(solution)/shard_map/ppermute | solution.py:246
  68.5 8.5 %collective-permute-start.4 = (bf16[32,1152]{1,0:T(8,128)(2,1)}, bf16[32,1152]{1,0:T(8,128)(2,1)S(1)}, u32[]{:S(2)}, u32[]{:S(2)}) collective-permute-start(bf16[32,1152]{1,0:T(8,128)(2,1)} %get-tuple-element.54), channel_id=1, source_target_pairs={{0,2},{1,3},{2,0},{3,1},{4,6},{5,7},{6,4},{7,5},{8,10},{9,11},{10,... | collective-permute-start | bytes 221192 | tf_op jit(solution)/shard_map/ppermute | solution.py:246
  70.9 7.9 %collective-permute-start.5 = (bf16[32,1152]{1,0:T(8,128)(2,1)}, bf16[32,1152]{1,0:T(8,128)(2,1)S(1)}, u32[]{:S(2)}, u32[]{:S(2)}) collective-permute-start(bf16[32,1152]{1,0:T(8,128)(2,1)} %get-tuple-element.55), channel_id=1, source_target_pairs={{0,3},{1,2},{2,1},{3,0},{4,7},{5,6},{6,5},{7,4},{8,11},{9,10},{10,... | collective-permute-start | bytes 221192 | tf_op jit(solution)/shard_map/ppermute | solution.py:246
  79.0 18.2 %collective-permute-start.6 = (bf16[4,1024]{1,0:T(4,128)(2,1)S(1)}, bf16[4,1024]{1,0:T(4,128)(2,1)S(1)}, u32[]{:S(2)}, u32[]{:S(2)}) collective-permute-start(bf16[4,1024]{1,0:T(4,128)(2,1)S(1)} %get-tuple-element.57), channel_id=1, source_target_pairs={{0,20},{1,21},{2,22},{3,23},{4,16},{5,17},{6,18},{7,19},{8,28},{9,... | collective-permute-start | bytes 24584 | tf_op jit(solution)/shard_map/ppermute | solution.py:246
  87.4 10.8 %collective-permute-start.7 = (bf16[4,1024]{1,0:T(4,128)(2,1)S(1)}, bf16[4,1024]{1,0:T(4,128)(2,1)S(1)}, u32[]{:S(2)}, u32[]{:S(2)}) collective-permute-start(bf16[4,1024]{1,0:T(4,128)(2,1)S(1)} %get-tuple-element.58), channel_id=1, source_target_pairs={{0,28},{1,29},{2,30},{3,31},{4,24},{5,25},{6,26},{7,27},{8,20},{9,... | collective-permute-start | bytes 24584 | tf_op jit(solution)/shard_map/ppermute | solution.py:246
  88.2 10.9 %collective-permute-start.8 = (bf16[4,1024]{1,0:T(4,128)(2,1)S(1)}, bf16[4,1024]{1,0:T(4,128)(2,1)S(1)}, u32[]{:S(2)}, u32[]{:S(2)}) collective-permute-start(bf16[4,1024]{1,0:T(4,128)(2,1)S(1)} %get-tuple-element.59), channel_id=1, source_target_pairs={{0,12},{1,13},{2,14},{3,15},{4,8},{5,9},{6,10},{7,11},{8,4},{9,5},... | collective-permute-start | bytes 24584 | tf_op jit(solution)/shard_map/ppermute | solution.py:246
  92.5 7.6 %collective-permute-start.9 = (bf16[4,1024]{1,0:T(4,128)(2,1)S(1)}, bf16[4,1024]{1,0:T(4,128)(2,1)S(1)}, u32[]{:S(2)}, u32[]{:S(2)}) collective-permute-start(bf16[4,1024]{1,0:T(4,128)(2,1)S(1)} %get-tuple-element.60), channel_id=1, source_target_pairs={{0,4},{1,5},{2,6},{3,7},{4,0},{5,1},{6,2},{7,3},{8,12},{9,13},{10,... | collective-permute-start | bytes 24584 | tf_op jit(solution)/shard_map/ppermute | solution.py:246
  93.8 6.2 %collective-permute-start.10 = (bf16[4,1024]{1,0:T(4,128)(2,1)S(1)}, bf16[4,1024]{1,0:T(4,128)(2,1)S(1)}, u32[]{:S(2)}, u32[]{:S(2)}) collective-permute-start(bf16[4,1024]{1,0:T(4,128)(2,1)S(1)} %get-tuple-element.61), channel_id=1, source_target_pairs={{0,16},{1,17},{2,18},{3,19},{4,20},{5,21},{6,22},{7,23},{8,24},{9,... | collective-permute-start | bytes 24584 | tf_op jit(solution)/shard_map/ppermute | solution.py:246
  97.2 4.9 %collective-permute-start.11 = (bf16[4,1024]{1,0:T(4,128)(2,1)S(1)}, bf16[4,1024]{1,0:T(4,128)(2,1)S(1)}, u32[]{:S(2)}, u32[]{:S(2)}) collective-permute-start(bf16[4,1024]{1,0:T(4,128)(2,1)S(1)} %get-tuple-element.62), channel_id=1, source_target_pairs={{0,24},{1,25},{2,26},{3,27},{4,28},{5,29},{6,30},{7,31},{8,16},{9,... | collective-permute-start | bytes 24584 | tf_op jit(solution)/shard_map/ppermute | solution.py:246
  98.2 3.8 %collective-permute-start.12 = (bf16[4,1024]{1,0:T(4,128)(2,1)S(1)}, bf16[4,1024]{1,0:T(4,128)(2,1)S(1)}, u32[]{:S(2)}, u32[]{:S(2)}) collective-permute-start(bf16[4,1024]{1,0:T(4,128)(2,1)S(1)} %get-tuple-element.63), channel_id=1, source_target_pairs={{0,8},{1,9},{2,10},{3,11},{4,12},{5,13},{6,14},{7,15},{8,0},{9,1},... | collective-permute-start | bytes 24584 | tf_op jit(solution)/shard_map/ppermute | solution.py:246
  (18 other events, 12.9 us)

commit v2 on v1

--- a/solution.py
+++ b/solution.py
@@ -52,7 +52,38 @@
     return t, a1, a2, a3, g + g1 + g2 + g3
 
 
-def conv_kernel(recv, par, taps, sum_out, conv_out, bc_out, dt_out, fin_out, init):
+def head_part(ref, width):
+    head = lax.axis_index("beam")
+    part = jnp.zeros((ref.shape[0], width), F32)
+    for h in range(8):
+        part = part + jnp.where(head == h, ref[:, width * h : width * h + width].astype(F32), 0.0)
+    return part
+
+
+def head_value(ref):
+    lane = lax.broadcasted_iota(jnp.int32, (1, 8), 1)
+    return jnp.sum(jnp.where(lane == lax.axis_index("beam"), ref[...], 0.0), axis=1, keepdims=True)
+
+
+def pack_kernel(state, *refs):
+    outs, (held, sem_in, sem_out) = refs[:8], refs[8:]
+    head = lax.axis_index("beam")
+    loads = []
+    for k in range(8):
+        for j in range(4):
+            loads.append(pltpu.make_async_copy(state.at[j // 2, j % 2, head ^ k], held.at[k, j], sem_in.at[k, j]))
+            loads[-1].start()
+    copies = []
+    for k in range(8):
+        for j in range(4):
+            loads[4 * k + j].wait()
+        copies.append(pltpu.make_async_copy(held.at[k], outs[k], sem_out.at[k]))
+        copies[-1].start()
+    for copy in copies:
+        copy.wait()
+
+
+def conv_kernel(recv, par, conv_x_w, conv_bc_w, sum_out, conv_out, bc_out, dt_out, fin_out, init):
     total = recv[0, 0:ROWS, :].astype(F32)
     dt = recv[0, 128:144, :].astype(F32)
     for k in range(3):
@@ -76,7 +107,7 @@
         + jnp.where(t == 1, start[1], 0.0)
         + jnp.where(t == 2, start[2], 0.0)
     )
-    w = taps[...]
+    w = jnp.concatenate([head_part(conv_x_w, HD), jnp.zeros((4, HD), F32), conv_bc_w[...].astype(F32)], axis=1)
     mixed = w[0:1] * past3 + w[1:2] * past2 + w[2:3] * past1 + w[3:4] * new.astype(F32)
     conv = mixed / (1.0 + jnp.exp(-mixed))
     sum_out[...] = new
@@ -92,26 +123,33 @@
     fin_out[2] = dot(pick, new).astype(BF16)
 
 
-def group_columns(blocks, low_row):
+def group_columns(blocks, low):
     b_cols, c_cols = [], []
     for q in range(4):
         part = jnp.zeros((ROWS, 128), F32)
         for k in range(4):
-            part = part + jnp.where(low_row == float(q ^ k), blocks[k], 0.0)
+            part = part + jnp.where(low == (q ^ k), blocks[k], 0.0)
         b_cols.append(part[:, 0:64])
         c_cols.append(part[:, 64:128])
     return jnp.concatenate(b_cols, 1).astype(BF16), jnp.concatenate(c_cols, 1).astype(BF16)
 
 
 def scan_kernel(
-    par, new, conv, bc0, bc1, bc2, bc3, dt_raw, consts, state, send_out, b_out, coef_out, first_out
+    par, new, conv, bc0, bc1, bc2, bc3, dt_raw, norm_gain, a_log, dt_bias, d_skip, *refs
 ):
+    parts, (send_out, b_out, coef_out, first_out) = refs[:8], refs[8:12]
+    state, send, b_buf, coef_buf, first_buf, sem_in, sem_send = refs[12:]
+    head = lax.axis_index("beam")
+    loads = [pltpu.make_async_copy(parts[k], state.at[pl.ds((head ^ k) * 4, 4)], sem_in.at[k]) for k in range(8)]
+    for load in loads:
+        load.start()
+    low = lax.axis_index("row") & 3
     blocks = [ref[...].astype(F32) for ref in (bc0, bc1, bc2, bc3)]
-    b_in, c_out = group_columns(blocks, consts[4:5])
+    b_in, c_out = group_columns(blocks, low)
     t, a1, a2, a3, g = lineage(par[...])
-    raw = dt_raw[...].astype(BF16).astype(F32) + consts[2:3]
+    raw = dt_raw[...].astype(BF16).astype(F32) + head_value(dt_bias)
     step_size = jnp.maximum(raw, 0.0) + jnp.log1p(jnp.exp(-jnp.abs(raw)))
-    rate = jnp.exp(consts[1:2])
+    rate = jnp.exp(head_value(a_log))
     log_decay = -rate * step_size
     rr = lax.broadcasted_iota(jnp.int32, (ROWS, ROWS), 0)
     cc = lax.broadcasted_iota(jnp.int32, (ROWS, ROWS), 1)
@@ -130,12 +168,14 @@
     half = jnp.where(lax.broadcasted_iota(jnp.int32, (ROWS, 128), 1) < 64, 0.0, 1.0)
     origin_b = jnp.broadcast_to(origin, (ROWS, 128)) - half
     acc = jnp.zeros((ROWS, 128), F32)
+    for load in loads:
+        load.wait()
     for p in range(BEAMS // 2):
         both = state[2 * p : 2 * p + 2].reshape(2 * HD, NS)
         acc = acc + jnp.where(origin_b == float(2 * p), dot_t(c_out, both), 0.0)
     old = acc[:, 0:64] + acc[:, 64:128]
     x_val = x_conv.astype(F32)
-    read = read + first * old + consts[3:4, 0:64] * x_val
+    read = read + first * old + head_value(d_skip) * x_val
     gate = new[:, 64:128].astype(F32)
     gated = read * (gate / (1.0 + jnp.exp(-gate)))
     square = jnp.sum(gated * gated, axis=1, keepdims=True)
@@ -143,15 +183,30 @@
     rest = square - high
     lane = lax.broadcasted_iota(jnp.int32, (ROWS, 64), 1)
     stats = jnp.where(lane == 0, high, jnp.where(lane == 1, rest, 0.0))
-    send_out[...] = jnp.concatenate([gated * consts[0:1, 0:64], stats], axis=1).astype(BF16)
-    b_out[...] = b_in
-    coef_out[...] = coef
-    first_out[...] = jnp.broadcast_to(first, (ROWS, 128))
-
-
-def final_kernel(parents, conv, b_in, coef, first, state, fin, out):
-    x_t = conv[:, 0:128].astype(F32).T[0:64]
-    b = b_in[...]
+    send[...] = jnp.concatenate([gated * head_part(norm_gain, HD), stats], axis=1).astype(BF16)
+    sends = [pltpu.make_async_copy(send, send_out.at[k], sem_send.at[k]) for k in range(8)]
+    for copy in sends:
+        copy.start()
+    b_buf[...] = b_in
+    coef_buf[...] = coef
+    first_buf[...] = jnp.broadcast_to(first, (ROWS, 128))
+    for n, (buf, ref) in enumerate(((b_buf, b_out), (coef_buf, coef_out), (first_buf, first_out))):
+        sends.append(pltpu.make_async_copy(buf, ref, sem_send.at[8 + n]))
+        sends[-1].start()
+    for copy in sends:
+        copy.wait()
+
+
+def final_kernel(parents, conv, b_in, coef_ref, first_ref, fin, *refs):
+    parts, homes = refs[:8], refs[8:16]
+    state, block, sem_in, sem_home = refs[16:]
+    head = lax.axis_index("beam")
+    loads = [pltpu.make_async_copy(parts[k], state.at[pl.ds((head ^ k) * 4, 4)], sem_in.at[k]) for k in range(8)]
+    for load in loads:
+        load.start()
+    x_t = conv[...].astype(F32).T[0:HD]
+    for load in loads:
+        load.wait()
     for i in range(8):
         for j in range(4):
             s, beam = j // 2, 2 * i + j % 2
@@ -159,18 +214,41 @@
             at = beam
             for step in range(STEPS - 1, -1, -1):
                 at = parents[step * BEAMS + s * WIDTH + at]
-            origin = (at >> 1) * 4 + s * 2 + (at & 1)
-            left = (x_t * coef[row : row + 1, :]).astype(BF16)
-            update = dot(left, b)
-            keep = jnp.broadcast_to(first[row : row + 1, 0:1], (HD, NS))
-            out[i, HD * j : HD * j + HD, :] = (keep * state[origin].astype(F32) + update).astype(BF16)
+            origin_s = (at >> 1) * 4 + s * 2 + (at & 1)
+            left = (x_t * coef_ref[row : row + 1, :]).astype(BF16)
+            keep = jnp.broadcast_to(first_ref[row : row + 1, 0:1], (HD, NS))
+            value = keep * state[origin_s].astype(F32) + dot(left, b_in[...])
+            block[i, HD * j : HD * j + HD, :] = value.astype(BF16)
         taps = [fin[k, 4 * i : 4 * i + 4, 0:64].astype(F32) for k in range(3)]
-        block = jnp.concatenate(taps + [jnp.zeros((4, 64), F32)], axis=1)
-        out[i, 4 * HD : 4 * HD + 16, :] = jnp.concatenate([block, jnp.zeros((12, NS), F32)], axis=0).astype(BF16)
-
-
-def out_kernel(place, recv, w_out, o0, o1, o2, o3, acc):
-    low = place[1]
+        tail = jnp.concatenate(taps + [jnp.zeros((4, 64), F32)], axis=1)
+        block[i, 4 * HD : 4 * HD + 16, :] = jnp.concatenate([tail, jnp.zeros((12, NS), F32)], axis=0).astype(BF16)
+    saves = [pltpu.make_async_copy(block.at[head ^ k], homes[k], sem_home.at[k]) for k in range(8)]
+    for copy in saves:
+        copy.start()
+    for copy in saves:
+        copy.wait()
+
+
+def unpack_kernel(*refs):
+    parts, (ssm_out, conv_out), (tails, sem_out) = refs[:8], refs[8:10], refs[10:]
+    head = lax.axis_index("beam")
+    copies = []
+    for k in range(8):
+        for j in range(4):
+            src = parts[k].at[pl.ds(HD * j, HD)]
+            copies.append(pltpu.make_async_copy(src, ssm_out.at[j // 2, j % 2, head ^ k], sem_out.at[k, j]))
+            copies[-1].start()
+        tails[head ^ k] = parts[k][4 * HD : 4 * HD + 16, :].astype(F32)
+    for h in range(8):
+        tail = tails[h]
+        for j in range(4):
+            for k in range(3):
+                conv_out[j // 2, j % 2, k, h : h + 1, :] = tail[j : j + 1, HD * k : HD * k + HD].astype(BF16)
+    for copy in copies:
+        copy.wait()
+
+
+def out_kernel(recv, w_out, out):
     stats = recv[0, :, 64:128].astype(F32)
     for i in range(1, 8):
         stats = stats + recv[i, :, 64:128].astype(F32)
@@ -178,38 +256,32 @@
     high = square.astype(BF16).astype(F32)
     rest = square - high
     lane = lax.broadcasted_iota(jnp.int32, (ROWS, 128), 1)
-    acc[:, 1024:1152] = jnp.where(lane == 0, high, jnp.where(lane == 1, rest, 0.0))
+    tail = jnp.where(lane == 0, high, jnp.where(lane == 1, rest, 0.0))
     left = jnp.concatenate([recv[i, :, 0:64] for i in range(8)], axis=1)
-    acc[:, 0:1024] = dot(left, w_out[...])
-    for k, ref in enumerate((o0, o1, o2, o3)):
-        ref[...] = acc[pl.ds(pl.multiple_of((low ^ k) * 32, 32), 32), :].astype(BF16)
-
-
-def norm_kernel(place, p0, p1, p2, p3, *refs):
-    outs, acc = refs[:8], refs[8]
-    total = p0[...].astype(F32) + p1[...].astype(F32) + p2[...].astype(F32) + p3[...].astype(F32)
-    square = total[:, 1024:1025] + total[:, 1025:1026]
-    scale = lax.rsqrt(square * (1.0 / GROUP_CH) + EPS)
-    normed = total[:, 0:1024] * scale
-    for m in range(8):
-        acc[m] = normed[STEPS * m : STEPS * m + STEPS]
-    for k, ref in enumerate(outs):
-        ref[...] = acc[place[0] ^ k].astype(BF16)
-
-
-def sum_kernel(p0, p1, p2, p3, p4, p5, p6, p7, out):
-    total = p0[...].astype(F32)
-    for ref in (p1, p2, p3, p4, p5, p6, p7):
-        total = total + ref[...].astype(F32)
-    out[...] = total.astype(BF16)
+    full = jnp.concatenate([dot(left, w_out[...]), tail], axis=1)
+    for q in range(4):
+        for m in range(8):
+            out[4 * m + q] = full[32 * q + 4 * m : 32 * q + 4 * m + 4].astype(BF16)
+
+
+def norm_kernel(recv, out):
+    result = jnp.zeros((STEPS, 1024), F32)
+    for g in range(8):
+        total = recv[4 * g].astype(F32)
+        for j in range(1, 4):
+            total = total + recv[4 * g + j].astype(F32)
+        square = total[:, 1024:1025] + total[:, 1025:1026]
+        result = result + total[:, 0:1024] * lax.rsqrt(square * (1.0 / GROUP_CH) + EPS)
+    out[...] = result.astype(BF16)
 
 
 VM = pl.BlockSpec(memory_space=pltpu.VMEM)
 SM = pl.BlockSpec(memory_space=pltpu.SMEM)
+ANY = pl.BlockSpec(memory_space=pl.ANY)
 FAR = pl.BlockSpec(memory_space=pltpu.HBM)
 
 
-def call(kernel, name, specs, outs, scratch=(), mib=6):
+def call(kernel, name, specs, outs, scratch=(), mib=6, out_specs=None):
     def build(*args):
         far = [n for n, spec in enumerate(specs) if spec is FAR]
         count = len(specs)
@@ -229,12 +301,19 @@
                 ins[n] = held[k]
             kernel(*ins, *rest)
 
+        args = [
+            pltpu.with_memory_space_constraint(arg, pltpu.HBM) if specs[n] in (ANY, FAR) else arg
+            for n, arg in enumerate(args)
+        ]
         return pl.pallas_call(
             body,
             name=name,
             in_specs=list(specs),
-            out_specs=tuple(VM for _ in outs),
-            out_shape=tuple(jax.ShapeDtypeStruct(s, d) for s, d in outs),
+            out_specs=tuple(out_specs or [VM for _ in outs]),
+            out_shape=tuple(
+                pltpu.HBM(s, d) if out_specs and out_specs[n] is ANY else jax.ShapeDtypeStruct(s, d)
+                for n, (s, d) in enumerate(outs)
+            ),
             scratch_shapes=list(scratch) + buffers + sems,
             compiler_params=pltpu.CompilerParams(vmem_limit_bytes=mib << 20),
         )(*args)
@@ -264,8 +343,6 @@
     parents,
 ):
     beam = lax.axis_index("beam")
-    row = lax.axis_index("row")
-    place = jnp.stack([beam, row & 3]).astype(jnp.int32)
     d_local = x_in.shape[-1]
     heads = ssm_state.shape[2]
     parent_column = parents.reshape(STEPS, 8, 4).transpose(2, 1, 0).reshape(ROWS, 1)
@@ -285,66 +362,97 @@
     payload = jnp.concatenate([top, bottom], axis=1)
     recv = lax.all_to_all(payload, "beam", split_axis=0, concat_axis=0, tiled=True)
 
-    conv_head = lax.dynamic_slice_in_dim(conv_x_w, beam * HD, HD, 1)
-    taps = jnp.concatenate([conv_head, jnp.zeros((4, HD), BF16), conv_bc_w.reshape(4, 128)], axis=1).astype(F32)
-    gain = jnp.pad(lax.dynamic_slice_in_dim(norm_gain, beam * HD, HD, 0), (0, HD)).reshape(1, 128)
-    scalars = [lax.dynamic_slice_in_dim(v, beam, 1, 0) for v in (a_log, dt_bias, d_skip)] + [(row & 3).astype(F32)[None]]
-    fills = [jnp.broadcast_to(v[:, None], (1, 128)) for v in scalars]
-    consts = jnp.concatenate([gain] + fills + [jnp.zeros((3, 128), F32)], axis=0)
-    by_head = ssm_state.transpose(2, 0, 1, 3, 4).reshape(heads, 4, HD, NS)
-    taps, consts, by_head, place, parent_column = lax.optimization_barrier((taps, consts, by_head, place, parent_column))
-    taps, consts, by_head, place, parent_column, recv = lax.optimization_barrier(
-        (taps, consts, by_head, place, parent_column, recv)
-    )
-    state = lax.all_to_all(by_head, "beam", split_axis=0, concat_axis=0, tiled=True).reshape(BEAMS, HD, NS)
+    packed = call(
+        pack_kernel,
+        "pack",
+        [ANY],
+        [((4, HD, NS), BF16)] * 8,
+        [
+            pltpu.VMEM((8, 4, HD, NS), BF16),
+            pltpu.SemaphoreType.DMA((8, 4)),
+            pltpu.SemaphoreType.DMA((8,)),
+        ],
+        out_specs=[ANY] * 8,
+    )(ssm_state)
+    states = [packed[0]] + [swap(packed[k], "beam", 8, k) for k in range(1, 8)]
 
     new, conv, bc_conv, dt_raw, fin = call(
         conv_kernel,
         "conv",
-        [FAR, VM, VM],
+        [FAR, VM, VM, VM],
         [((ROWS, 256), BF16), ((ROWS, 128), BF16), ((ROWS, 128), BF16), ((1, ROWS), F32), ((3, BEAMS, 256), BF16)],
         [pltpu.VMEM((3, BEAMS, 256), F32)],
-    )(recv, parent_column, taps)
+    )(recv, parent_column, conv_x_w, conv_bc_w.reshape(4, 128))
 
     others = [swap(bc_conv, "row", 32, k) for k in (1, 2, 3)]
 
     send, b_in, coef, first = call(
         scan_kernel,
         "scan",
-        [FAR] * 10,
-        [((ROWS, 128), BF16), ((ROWS, NS), BF16), ((ROWS, ROWS), F32), ((ROWS, 128), F32)],
-    )(parent_column, new, conv, bc_conv, *others, dt_raw, consts, state)
-
-    gathered = lax.all_to_all(
-        jnp.broadcast_to(send[None], (heads, ROWS, 128)), "beam", split_axis=0, concat_axis=0, tiled=True
+        [VM] * 12 + [ANY] * 8,
+        [((8, ROWS, 128), BF16), ((ROWS, NS), BF16), ((ROWS, ROWS), F32), ((ROWS, 128), F32)],
+        [
+            pltpu.VMEM((BEAMS, HD, NS), BF16),
+            pltpu.VMEM((ROWS, 128), BF16),
+            pltpu.VMEM((ROWS, NS), BF16),
+            pltpu.VMEM((ROWS, ROWS), F32),
+            pltpu.VMEM((ROWS, 128), F32),
+            pltpu.SemaphoreType.DMA((8,)),
+            pltpu.SemaphoreType.DMA((11,)),
+        ],
+        out_specs=[ANY] * 4,
+    )(
+        parent_column,
+        new,
+        conv,
+        bc_conv,
+        *others,
+        dt_raw,
+        norm_gain.reshape(1, 512),
+        a_log.reshape(1, 8),
+        dt_bias.reshape(1, 8),
+        d_skip.reshape(1, 8),
+        *states,
     )
-    (final,) = call(
+    gathered = lax.all_to_all(send, "beam", split_axis=0, concat_axis=0, tiled=True)
+    final = call(
         final_kernel,
         "final",
-        [SM] + [FAR] * 6,
-        [((heads, 4 * HD + 16, NS), BF16)],
-    )(parents.reshape(ROWS), conv, b_in, coef, first, state, fin)
-    home = lax.all_to_all(final, "beam", split_axis=0, concat_axis=0, tiled=True)
-
-    parts = call(
+        [SM, VM] + [FAR] * 4 + [ANY] * 8,
+        [((4 * HD + 16, NS), BF16)] * 8,
+        [
+            pltpu.VMEM((BEAMS, HD, NS), BF16),
+            pltpu.VMEM((8, 4 * HD + 16, NS), BF16),
+            pltpu.SemaphoreType.DMA((8,)),
+            pltpu.SemaphoreType.DMA((8,)),
+        ],
+        out_specs=[ANY] * 8,
+    )(parents.reshape(ROWS), conv, b_in, coef, first, fin, *states)
+    homes = [final[0]] + [swap(final[k], "beam", 8, k) for k in range(1, 8)]
+    gathered, homes[1] = lax.optimization_barrier((gathered, homes[1]))
+    ssm_final, conv_x_rows = call(
+        unpack_kernel,
+        "unpack",
+        [VM] * 8,
+        [((SESS, 2, heads, HD, NS), BF16), ((SESS, 2, 3, heads, HD), BF16)],
+        [
+            pltpu.VMEM((8, 16, NS), F32),
+            pltpu.SemaphoreType.DMA((8, 4)),
+        ],
+        out_specs=[ANY, VM],
+    )(*homes)
+    conv_x_final = conv_x_rows.transpose(0, 1, 3, 4, 2)
+
+    (parts,) = call(
         out_kernel,
         "project",
-        [SM, FAR, VM],
-        [((32, 1152), BF16)] * 4,
-        [pltpu.VMEM((ROWS, 1152), F32)],
-    )(place, gathered, w_out)
-    got = [parts[0]] + [swap(parts[k], "row", 32, k) for k in (1, 2, 3)]
-    place_z = jnp.stack([row >> 2]).astype(jnp.int32)
-    pieces = call(norm_kernel, "norm", [SM] + [VM] * 4, [((STEPS, 1024), BF16)] * 8, [pltpu.VMEM((8, STEPS, 1024), F32)])(
-        place_z, *got
-    )
-    far_first = (5, 7, 3, 1, 4, 6, 2)
-    arrived = [pieces[0]] + [swap(pieces[k], "row", 32, k * 4) for k in far_first]
-    (layer_out,) = call(sum_kernel, "total", [VM] * 8, [((STEPS, 1024), BF16)])(*arrived)
+        [VM, VM],
+        [((BEAMS, STEPS, 1152), BF16)],
+    )(gathered, w_out)
+    spread = lax.all_to_all(parts, "row", split_axis=0, concat_axis=0, tiled=True)
+    (layer_out,) = call(norm_kernel, "norm", [VM], [((STEPS, 1024), BF16)])(spread)
     layer_out = layer_out[:, None]
 
-    ssm_final = home[:, : 4 * HD].reshape(heads, SESS, 2, HD, NS).transpose(1, 2, 0, 3, 4)
-    conv_x_final = home[:, 4 * HD : 4 * HD + 4, :192].reshape(heads, SESS, 2, 3, HD).transpose(1, 2, 0, 4, 3)
     own = lax.dynamic_slice_in_dim(fin, beam * 4, 4, 1)[:, :, 128:]
     conv_bc_final = own.reshape(3, SESS, 2, 2, 64).transpose(1, 2, 0, 3, 4)
     return layer_out, ssm_final, conv_x_final, conv_bc_final

time: 108 us -> 90.4 us (0.84)
  the two profiles are of different devices: /device:TPU:32 before, /device:TPU:1 now
where the time goes in v2:
time: 90.4 us; the launch traced here: 89.7 us
  starting transfers between devices  49.6 us (55%)
  Pallas kernels  15.7 us (17%)
  waiting for transfers between devices  14 us (15%)
  local copies, waits for them, and re-layouts  7.62 us (8%)
  between operations  1 us (1%)
  other arithmetic  0.98 us (1%)
    ppermute x17, starting transfers between devices, swap(): return lax.ppermute(value, axis, [(i, i ^ mask) for i in range(count)])  28 us
    pallas_call x7, Pallas kernels, build(): pl.pallas_call(body, name=name, in_specs=list(specs), out_specs=tuple(out...  15.7 us
    ppermute x17, waiting for transfers between devices, swap(): return lax.ppermute(value, axis, [(i, i ^ mask) for i in range(count)])  13.9 us
    all_to_all x1, starting transfers between devices, local(): lax.all_to_all(parts, 'row', split_axis=0, concat_axis=0, tiled=True)  9.8 us
    all_to_all x1, starting transfers between devices, local(): lax.all_to_all(payload, 'beam', split_axis=0, concat_axis=0, tiled=True)  6.81 us
    all_to_all x1, starting transfers between devices, local(): lax.all_to_all(send, 'beam', split_axis=0, concat_axis=0, tiled=True)  4.93 us
    unnamed x47, local copies, waits for them, and re-layouts  3.35 us
  transfers between devices with their start and end apart: 20, of which 7 were waited for; matrix products, arithmetic and copies ran while one was open for 2% of the time, Pallas kernels for 12%

profile of v2, /device:TPU:1, one launch (start us, length us, event | category | flops | bytes accessed | tf_op | source)
XLA Modules:
  0.0 89.7 jit_solution(1212422911780969765)
XLA Ops:
  0.7 1.2 %reshape.86 = bf16[4,8,4,1024]{3,2,1,0:T(4,128)(2,1)S(1)} reshape(bf16[4,2,16,1024]{3,2,1,0:T(8,128)(2,1)} %param.15) | data formatting | bytes 524288 | tf_op jit(solution)/shard_map/reshape | solution.py:349
  4.3 1.0 %maximum_maximum_fusion = bf16[8,144,256]{2,1,0:T(8,128)(2,1)} fusion(bf16[8,1,128]{2,1,0:T(2,128)(2,1)S(1)} %copy.54, bf16[8,1,128]{2,1,0:T(2,128)(2,1)S(1)} %copy.53, bf16[8,12,64]{2,1,0:T(8,128)(2,1)S(1)} %copy.52, bf16[8,128,128]{2,1,0:T(8,128)(2,1)S(1)} %copy.49, bf16[144]{0:T(256)(128)(2,1)S(1)} %pad.7.clone, bf16[144,256]{1,0:T(8,128)(2,1)S(1)} %pad.4.clone, ...), kind=kLoop, calls=%fused_computation.3 | loop fusion | flops 4718592 | bytes 1089824 | tf_op jit(solution)/shard_map/concatenate | solution.py:362
  5.3 6.8 %all-to-all-start = ((bf16[8,144,256]{2,1,0:T(8,128)(2,1)}), bf16[8,144,256]{2,1,0:T(8,128)(2,1)S(1)}, u32[]{:S(2)}, u32[]{:S(2)}) async-start(bf16[8,144,256]{2,1,0:T(8,128)(2,1)} %maximum_maximum_fusion), calls=%async_computation | async-start | bytes 1179648 | tf_op jit(solution)/shard_map/all_to_all | solution.py:363
  12.1 2.3 %pack.1 = (bf16[4,64,256]{2,1,0:T(8,128)(2,1)}, bf16[4,64,256]{2,1,0:T(8,128)(2,1)}, bf16[4,64,256]{2,1,0:T(8,128)(2,1)}, bf16[4,64,256]{2,1,0:T(8,128)(2,1)}, b...) custom-call(bf16[2,2,8,64,256]{4,3,2,1,0:T(8,128)(2,1)} %refs_0_.1), custom_call_target="tpu_custom_call" | custom-call | tf_op jit(solution)/shard_map/pack/pallas_call | solution.py:308
  14.6 1.6 %collective-permute-start.4 = (bf16[4,64,256]{2,1,0:T(8,128)(2,1)}, bf16[4,64,256]{2,1,0:T(8,128)(2,1)S(1)}, u32[]{:S(2)}, u32[]{:S(2)}) collective-permute-start(bf16[4,64,256]{2,1,0:T(8,128)(2,1)} %get-tuple-element.39), channel_id=1, source_target_pairs={{0,64},{32,96},{64,0},{96,32},{128,192},{160,224},{192,128},{224,1... | collective-permute-start | bytes 393224 | tf_op jit(solution)/shard_map/ppermute | solution.py:325
  16.6 2.9 %collective-permute-start.6 = (bf16[4,64,256]{2,1,0:T(8,128)(2,1)}, bf16[4,64,256]{2,1,0:T(8,128)(2,1)S(1)}, u32[]{:S(2)}, u32[]{:S(2)}) collective-permute-start(bf16[4,64,256]{2,1,0:T(8,128)(2,1)} %get-tuple-element.41), channel_id=1, source_target_pairs={{0,128},{32,160},{64,192},{96,224},{128,0},{160,32},{192,64},{224,... | collective-permute-start | bytes 393224 | tf_op jit(solution)/shard_map/ppermute | solution.py:325
  19.8 2.6 %collective-permute-start.8 = (bf16[4,64,256]{2,1,0:T(8,128)(2,1)}, bf16[4,64,256]{2,1,0:T(8,128)(2,1)}, u32[]{:S(2)}, u32[]{:S(2)}) collective-permute-start(bf16[4,64,256]{2,1,0:T(8,128)(2,1)} %get-tuple-element.43), channel_id=1, source_target_pairs={{0,192},{32,224},{64,128},{96,160},{128,64},{160,96},{192,0},{224,... | collective-permute-start | bytes 393224 | tf_op jit(solution)/shard_map/ppermute | solution.py:325
  22.5 1.1 %collective-permute-done.4.refs_14_.refs_8_ = bf16[4,64,256]{2,1,0:T(8,128)(2,1)S(1)} collective-permute-done((bf16[4,64,256]{2,1,0:T(8,128)(2,1)}, bf16[4,64,256]{2,1,0:T(8,128)(2,1)S(1)}, u32[]{:S(2)}, u32[]{:S(2)}) %collective-permute-start.4) | collective-permute-done | bytes 131104 | tf_op jit(solution)/shard_map/ppermute | solution.py:325
  23.6 3.0 %collective-permute-start.9 = (bf16[4,64,256]{2,1,0:T(8,128)(2,1)}, bf16[4,64,256]{2,1,0:T(8,128)(2,1)}, u32[]{:S(2)}, u32[]{:S(2)}) collective-permute-start(bf16[4,64,256]{2,1,0:T(8,128)(2,1)} %get-tuple-element.44), channel_id=1, source_target_pairs={{0,224},{32,192},{64,160},{96,128},{128,96},{160,64},{192,32},{224... | collective-permute-start | bytes 393224 | tf_op jit(solution)/shard_map/ppermute | solution.py:325
  27.0 0.8 copy-done.11
  27.8 2.0 %conv.1 = (bf16[128,256]{1,0:T(8,128)(2,1)S(1)}, bf16[128,128]{1,0:T(8,128)(2,1)S(1)}, bf16[128,128]{1,0:T(8,128)(2,1)S(1)}, f32[1,128]{1,0:T(1,128)S(1)}, bf16[3,32,256]{2,1,0:T(8,128)(2,1)S(1)}) custom-call(bf16[8,144,256]{2,1,0:T(8,128)(2,1)} %copy-done.11, s32[128,1]{1,0:T(8,128)S(1)} %reshape.102.refs_1_.refs_0_, bf16[4,512]{1,0:T(4,128)(2,1)S(1)} %copy-done.6, ...), custom_call_target="tpu_custom_call" | custom-call | tf_op jit(solution)/shard_map/conv/pallas_call | solution.py:308
  31.2 3.0 %collective-permute-start.1 = (bf16[128,128]{1,0:T(8,128)(2,1)S(1)}, bf16[128,128]{1,0:T(8,128)(2,1)S(1)}, u32[]{:S(2)}, u32[]{:S(2)}) collective-permute-start(bf16[128,128]{1,0:T(8,128)(2,1)S(1)} %get-tuple-element.35.refs_3_), channel_id=1, source_target_pairs={{0,2},{1,3},{2,0},{3,1},{4,6},{5,7},{6,4},{7,5},{8,10},{9,11},{10,... | collective-permute-start | bytes 98312 | tf_op jit(solution)/shard_map/ppermute | solution.py:325
  34.2 3.0 %collective-permute-start.2 = (bf16[128,128]{1,0:T(8,128)(2,1)S(1)}, bf16[128,128]{1,0:T(8,128)(2,1)S(1)}, u32[]{:S(2)}, u32[]{:S(2)}) collective-permute-start(bf16[128,128]{1,0:T(8,128)(2,1)S(1)} %get-tuple-element.35.refs_3_), channel_id=1, source_target_pairs={{0,3},{1,2},{2,1},{3,0},{4,7},{5,6},{6,5},{7,4},{8,11},{9,10},{10,... | collective-permute-start | bytes 98312 | tf_op jit(solution)/shard_map/ppermute | solution.py:325
  37.3 1.5 %collective-permute-done.2.refs_6_ = bf16[128,128]{1,0:T(8,128)(2,1)S(1)} collective-permute-done((bf16[128,128]{1,0:T(8,128)(2,1)S(1)}, bf16[128,128]{1,0:T(8,128)(2,1)S(1)}, u32[]{:S(2)}, u32[]{:S(2)}) %collective-permute-start.2) | collective-permute-done | bytes 32800 | tf_op jit(solution)/shard_map/ppermute | solution.py:325
  38.9 3.4 %scan.1 = (bf16[8,128,128]{2,1,0:T(8,128)(2,1)}, bf16[128,256]{1,0:T(8,128)(2,1)}, f32[128,128]{1,0:T(8,128)}, f32[128,128]{1,0:T(8,128)}) custom-call(s32[128,1]{1,0:T(8,128)S(1)} %reshape.102.refs_1_.refs_0_, bf16[128,256]{1,0:T(8,128)(2,1)S(1)} %get-tuple-element.33.refs_1_, bf16[128,128]{1,0:T(8,128)(2,1)S(1)} %get-tuple-element.34.refs_2_.refs_1_, ...), custom_call_target="tpu_custom_call" | custom-call | tf_op jit(solution)/shard_map/scan/pallas_call | solution.py:308
  42.2 4.9 %all-to-all-start.1 = ((bf16[8,128,128]{2,1,0:T(8,128)(2,1)}), bf16[8,128,128]{2,1,0:T(8,128)(2,1)S(1)}, u32[]{:S(2)}, u32[]{:S(2)}) async-start(bf16[8,128,128]{2,1,0:T(8,128)(2,1)} %get-tuple-element.45), calls=%async_computation.1 | async-start | bytes 524288 | tf_op jit(solution)/shard_map/all_to_all | solution.py:417
  47.3 4.4 %final.1 = (bf16[272,256]{1,0:T(8,128)(2,1)}, bf16[272,256]{1,0:T(8,128)(2,1)}, bf16[272,256]{1,0:T(8,128)(2,1)}, bf16[272,256]{1,0:T(8,128)(2,1)}, bf16[272,256...) custom-call(s32[128]{0:T(128)S(1)} %reshape.96.refs_0_, ...), custom_call_target="tpu_custom_call" | custom-call | tf_op jit(solution)/shard_map/final/pallas_call | solution.py:308
  51.9 1.5 %collective-permute-done.10.refs_1_ = bf16[272,256]{1,0:T(8,128)(2,1)S(1)} collective-permute-done((bf16[272,256]{1,0:T(8,128)(2,1)}, bf16[272,256]{1,0:T(8,128)(2,1)S(1)}, u32[]{:S(2)}, u32[]{:S(2)}) %collective-permute-start.10) | collective-permute-done | bytes 139296 | tf_op jit(solution)/shard_map/ppermute | solution.py:325
  54.0 1.1 %project.1 = bf16[32,4,1152]{2,1,0:T(4,128)(2,1)} custom-call(bf16[8,128,128]{2,1,0:T(8,128)(2,1)S(1)} %all-to-all-done.1.refs_0_, bf16[512,1024]{1,0:T(8,128)(2,1)S(1)} %copy-done.1), custom_call_target="tpu_custom_call" | custom-call | tf_op jit(solution)/shard_map/project/pallas_call | solution.py:308
  55.1 9.8 %all-to-all-start.2 = ((bf16[32,4,1152]{2,1,0:T(4,128)(2,1)}), bf16[32,4,1152]{2,1,0:T(4,128)(2,1)S(1)}, u32[]{:S(2)}, u32[]{:S(2)}) async-start(bf16[32,4,1152]{2,1,0:T(4,128)(2,1)} %project.1), calls=%async_computation.2 | async-start | bytes 589824 | tf_op jit(solution)/shard_map/all_to_all | solution.py:452
  64.9 1.5 %collective-permute-start.11 = (bf16[272,256]{1,0:T(8,128)(2,1)}, bf16[272,256]{1,0:T(8,128)(2,1)S(1)}, u32[]{:S(2)}, u32[]{:S(2)}) collective-permute-start(bf16[272,256]{1,0:T(8,128)(2,1)} %get-tuple-element.54), channel_id=1, source_target_pairs={{0,64},{32,96},{64,0},{96,32},{128,192},{160,224},{192,128},{224,1... | collective-permute-start | bytes 417800 | tf_op jit(solution)/shard_map/ppermute | solution.py:325
  66.3 1.3 %collective-permute-start.12 = (bf16[272,256]{1,0:T(8,128)(2,1)}, bf16[272,256]{1,0:T(8,128)(2,1)S(1)}, u32[]{:S(2)}, u32[]{:S(2)}) collective-permute-start(bf16[272,256]{1,0:T(8,128)(2,1)} %get-tuple-element.55), channel_id=1, source_target_pairs={{0,96},{32,64},{64,32},{96,0},{128,224},{160,192},{192,160},{224,1... | collective-permute-start | bytes 417800 | tf_op jit(solution)/shard_map/ppermute | solution.py:325
  67.6 2.5 %collective-permute-start.13 = (bf16[272,256]{1,0:T(8,128)(2,1)}, bf16[272,256]{1,0:T(8,128)(2,1)S(1)}, u32[]{:S(2)}, u32[]{:S(2)}) collective-permute-start(bf16[272,256]{1,0:T(8,128)(2,1)} %get-tuple-element.56), channel_id=1, source_target_pairs={{0,128},{32,160},{64,192},{96,224},{128,0},{160,32},{192,64},{224,... | collective-permute-start | bytes 417800 | tf_op jit(solution)/shard_map/ppermute | solution.py:325
  70.4 2.2 %collective-permute-start.15 = (bf16[272,256]{1,0:T(8,128)(2,1)}, bf16[272,256]{1,0:T(8,128)(2,1)S(1)}, u32[]{:S(2)}, u32[]{:S(2)}) collective-permute-start(bf16[272,256]{1,0:T(8,128)(2,1)} %get-tuple-element.58), channel_id=1, source_target_pairs={{0,192},{32,224},{64,128},{96,160},{128,64},{160,96},{192,0},{224,... | collective-permute-start | bytes 417800 | tf_op jit(solution)/shard_map/ppermute | solution.py:325
  72.6 2.3 %collective-permute-start.16 = (bf16[272,256]{1,0:T(8,128)(2,1)}, bf16[272,256]{1,0:T(8,128)(2,1)S(1)}, u32[]{:S(2)}, u32[]{:S(2)}) collective-permute-start(bf16[272,256]{1,0:T(8,128)(2,1)} %get-tuple-element.59), channel_id=1, source_target_pairs={{0,224},{32,192},{64,160},{96,128},{128,96},{160,64},{192,32},{224... | collective-permute-start | bytes 417800 | tf_op jit(solution)/shard_map/ppermute | solution.py:325
  74.9 0.8 constant_dynamic-slice_fusion
  76.3 1.7 %collective-permute-done.13.refs_4_ = bf16[272,256]{1,0:T(8,128)(2,1)S(1)} collective-permute-done((bf16[272,256]{1,0:T(8,128)(2,1)}, bf16[272,256]{1,0:T(8,128)(2,1)S(1)}, u32[]{:S(2)}, u32[]{:S(2)}) %collective-permute-start.13) | collective-permute-done | bytes 139296 | tf_op jit(solution)/shard_map/ppermute | solution.py:325
  78.0 3.9 %collective-permute-done.14.refs_5_ = bf16[272,256]{1,0:T(8,128)(2,1)S(1)} collective-permute-done((bf16[272,256]{1,0:T(8,128)(2,1)}, bf16[272,256]{1,0:T(8,128)(2,1)S(1)}, u32[]{:S(2)}, u32[]{:S(2)}) %collective-permute-start.14) | collective-permute-done | bytes 139296 | tf_op jit(solution)/shard_map/ppermute | solution.py:325
  82.7 3.5 %collective-permute-done.16.refs_7_ = bf16[272,256]{1,0:T(8,128)(2,1)S(1)} collective-permute-done((bf16[272,256]{1,0:T(8,128)(2,1)}, bf16[272,256]{1,0:T(8,128)(2,1)S(1)}, u32[]{:S(2)}, u32[]{:S(2)}) %collective-permute-start.16) | collective-permute-done | bytes 139296 | tf_op jit(solution)/shard_map/ppermute | solution.py:325
  86.2 0.9 %copy-done.4 = bf16[272,256]{1,0:T(8,128)(2,1)S(1)} copy-done((bf16[272,256]{1,0:T(8,128)(2,1)S(1)}, bf16[272,256]{1,0:T(8,128)(2,1)}, u32[]{:S(2)}) %copy-start.4) | copy-done | bytes 139288
  87.1 1.8 %unpack.1 = (bf16[2,2,8,64,256]{4,3,2,1,0:T(8,128)(2,1)}, bf16[2,2,3,8,64]{4,3,2,1,0:T(8,128)(2,1)}) custom-call(bf16[272,256]{1,0:T(8,128)(2,1)S(1)} %copy-done.2, bf16[272,256]{1,0:T(8,128)(2,1)S(1)} %copy-done.4, bf16[272,256]{1,0:T(8,128)(2,1)S(1)} %collective-permute-done.11.refs_2_, bf16[272,256]{1,0:T(8,128)(2,1)S(1)} %collective-permute-done.12.refs_3_, ...), custom_call_target="tpu_custom_call" | custom-call | tf_op jit(solution)/shard_map/unpack/pallas_call | solution.py:308
  88.9 0.8 norm.1
  (95 shorter events, 7.6 us)
Async XLA Ops:
  5.3 21.3 %copy-start.20 = (s32[4,2,16]{2,1,0:T(2,128)S(1)}, s32[4,2,16]{2,1,0:T(2,128)}, u32[]{:S(2)}) copy-start(s32[4,2,16]{2,1,0:T(2,128)} %param.29) | copy-start | bytes 1540
  5.3 21.6 %copy-start.22 = (bf16[4,2,64]{2,1,0:T(2,128)(2,1)S(1)}, bf16[4,2,64]{2,1,0:T(2,128)(2,1)}, u32[]{:S(2)}) copy-start(bf16[4,2,64]{2,1,0:T(2,128)(2,1)} %param.20) | copy-start | bytes 3076
  5.3 22.6 %copy-start.6 = (bf16[4,512]{1,0:T(4,128)(2,1)S(1)}, bf16[4,512]{1,0:T(4,128)(2,1)}, u32[]{:S(2)}) copy-start(bf16[4,512]{1,0:T(4,128)(2,1)} %refs_2_.1) | copy-start | bytes 12292
  5.3 21.7 %all-to-all-start = ((bf16[8,144,256]{2,1,0:T(8,128)(2,1)}), bf16[8,144,256]{2,1,0:T(8,128)(2,1)S(1)}, u32[]{:S(2)}, u32[]{:S(2)}) async-start(bf16[8,144,256]{2,1,0:T(8,128)(2,1)} %maximum_maximum_fusion), calls=%async_computation | async-start | bytes 1179648 | tf_op jit(solution)/shard_map/all_to_all | solution.py:363
  12.1 26.7 %copy-start.7 = (f32[512]{0:T(512)S(1)}, f32[512]{0:T(512)}, u32[]{:S(2)}) copy-start(f32[512]{0:T(512)} %param.24) | copy-start | bytes 6148
  12.1 26.7 %copy-start.8 = (f32[8]{0:T(128)S(1)}, f32[8]{0:T(128)}, u32[]{:S(2)}) copy-start(f32[8]{0:T(128)} %param.22) | copy-start | bytes 100
  12.1 26.7 %copy-start.9 = (f32[8]{0:T(128)S(1)}, f32[8]{0:T(128)}, u32[]{:S(2)}) copy-start(f32[8]{0:T(128)} %param.21) | copy-start | bytes 100
  12.1 26.8 %copy-start.10 = (f32[8]{0:T(128)S(1)}, f32[8]{0:T(128)}, u32[]{:S(2)}) copy-start(f32[8]{0:T(128)} %param.23) | copy-start | bytes 100
  14.4 5.4 %collective-permute-start.3 = (bf16[4,64,256]{2,1,0:T(8,128)(2,1)}, bf16[4,64,256]{2,1,0:T(8,128)(2,1)S(1)}, u32[]{:S(2)}, u32[]{:S(2)}) collective-permute-start(bf16[4,64,256]{2,1,0:T(8,128)(2,1)} %get-tuple-element.38), channel_id=1, source_target_pairs={{0,32},{32,0},{64,96},{96,64},{128,160},{160,128},{192,224},{224,1... | collective-permute-start | bytes 393224 | tf_op jit(solution)/shard_map/ppermute | solution.py:325
  14.6 9.0 %collective-permute-start.4 = (bf16[4,64,256]{2,1,0:T(8,128)(2,1)}, bf16[4,64,256]{2,1,0:T(8,128)(2,1)S(1)}, u32[]{:S(2)}, u32[]{:S(2)}) collective-permute-start(bf16[4,64,256]{2,1,0:T(8,128)(2,1)} %get-tuple-element.39), channel_id=1, source_target_pairs={{0,64},{32,96},{64,0},{96,32},{128,192},{160,224},{192,128},{224,1... | collective-permute-start | bytes 393224 | tf_op jit(solution)/shard_map/ppermute | solution.py:325
  16.2 14.3 %collective-permute-start.5 = (bf16[4,64,256]{2,1,0:T(8,128)(2,1)}, bf16[4,64,256]{2,1,0:T(8,128)(2,1)S(1)}, u32[]{:S(2)}, u32[]{:S(2)}) collective-permute-start(bf16[4,64,256]{2,1,0:T(8,128)(2,1)} %get-tuple-element.40), channel_id=1, source_target_pairs={{0,96},{32,64},{64,32},{96,0},{128,224},{160,192},{192,160},{224,1... | collective-permute-start | bytes 393224 | tf_op jit(solution)/shard_map/ppermute | solution.py:325
  16.6 14.6 %collective-permute-start.6 = (bf16[4,64,256]{2,1,0:T(8,128)(2,1)}, bf16[4,64,256]{2,1,0:T(8,128)(2,1)S(1)}, u32[]{:S(2)}, u32[]{:S(2)}) collective-permute-start(bf16[4,64,256]{2,1,0:T(8,128)(2,1)} %get-tuple-element.41), channel_id=1, source_target_pairs={{0,128},{32,160},{64,192},{96,224},{128,0},{160,32},{192,64},{224,... | collective-permute-start | bytes 393224 | tf_op jit(solution)/shard_map/ppermute | solution.py:325
  19.5 14.7 %collective-permute-start.7 = (bf16[4,64,256]{2,1,0:T(8,128)(2,1)}, bf16[4,64,256]{2,1,0:T(8,128)(2,1)S(1)}, u32[]{:S(2)}, u32[]{:S(2)}) collective-permute-start(bf16[4,64,256]{2,1,0:T(8,128)(2,1)} %get-tuple-element.42), channel_id=1, source_target_pairs={{0,160},{32,128},{64,224},{96,192},{128,32},{160,0},{192,96},{224,... | collective-permute-start | bytes 393224 | tf_op jit(solution)/shard_map/ppermute | solution.py:325
  19.8 19.0 %copy-start.12 = (bf16[4,64,256]{2,1,0:T(8,128)(2,1)}, bf16[4,64,256]{2,1,0:T(8,128)(2,1)S(1)}, u32[]{:S(2)}) copy-start(bf16[4,64,256]{2,1,0:T(8,128)(2,1)S(1)} %collective-permute-done.3.refs_13_.refs_7_) | copy-start | bytes 393220
  19.8 17.4 %collective-permute-start.8 = (bf16[4,64,256]{2,1,0:T(8,128)(2,1)}, bf16[4,64,256]{2,1,0:T(8,128)(2,1)}, u32[]{:S(2)}, u32[]{:S(2)}) collective-permute-start(bf16[4,64,256]{2,1,0:T(8,128)(2,1)} %get-tuple-element.43), channel_id=1, source_target_pairs={{0,192},{32,224},{64,128},{96,160},{128,64},{160,96},{192,0},{224,... | collective-permute-start | bytes 393224 | tf_op jit(solution)/shard_map/ppermute | solution.py:325
  23.6 15.2 %copy-start.13 = (bf16[4,64,256]{2,1,0:T(8,128)(2,1)}, bf16[4,64,256]{2,1,0:T(8,128)(2,1)S(1)}, u32[]{:S(2)}) copy-start(bf16[4,64,256]{2,1,0:T(8,128)(2,1)S(1)} %collective-permute-done.4.refs_14_.refs_8_) | copy-start | bytes 393220
  23.6 13.7 %collective-permute-start.9 = (bf16[4,64,256]{2,1,0:T(8,128)(2,1)}, bf16[4,64,256]{2,1,0:T(8,128)(2,1)}, u32[]{:S(2)}, u32[]{:S(2)}) collective-permute-start(bf16[4,64,256]{2,1,0:T(8,128)(2,1)} %get-tuple-element.44), channel_id=1, source_target_pairs={{0,224},{32,192},{64,160},{96,128},{128,96},{160,64},{192,32},{224... | collective-permute-start | bytes 393224 | tf_op jit(solution)/shard_map/ppermute | solution.py:325
  30.5 8.3 %copy-start.14 = (bf16[4,64,256]{2,1,0:T(8,128)(2,1)}, bf16[4,64,256]{2,1,0:T(8,128)(2,1)S(1)}, u32[]{:S(2)}) copy-start(bf16[4,64,256]{2,1,0:T(8,128)(2,1)S(1)} %collective-permute-done.5.refs_15_.refs_9_) | copy-start | bytes 393220
  30.5 6.8 %collective-permute-start = (bf16[128,128]{1,0:T(8,128)(2,1)S(1)}, bf16[128,128]{1,0:T(8,128)(2,1)S(1)}, u32[]{:S(2)}, u32[]{:S(2)}) collective-permute-start(bf16[128,128]{1,0:T(8,128)(2,1)S(1)} %get-tuple-element.35.refs_3_), channel_id=1, source_target_pairs={{0,1},{1,0},{2,3},{3,2},{4,5},{5,4},{6,7},{7,6},{8,9},{9,8},{10,11... | collective-permute-start | bytes 98312 | tf_op jit(solution)/shard_map/ppermute | solution.py:325
  31.2 6.0 %collective-permute-start.1 = (bf16[128,128]{1,0:T(8,128)(2,1)S(1)}, bf16[128,128]{1,0:T(8,128)(2,1)S(1)}, u32[]{:S(2)}, u32[]{:S(2)}) collective-permute-start(bf16[128,128]{1,0:T(8,128)(2,1)S(1)} %get-tuple-element.35.refs_3_), channel_id=1, source_target_pairs={{0,2},{1,3},{2,0},{3,1},{4,6},{5,7},{6,4},{7,5},{8,10},{9,11},{10,... | collective-permute-start | bytes 98312 | tf_op jit(solution)/shard_map/ppermute | solution.py:325
  34.2 4.6 %collective-permute-start.2 = (bf16[128,128]{1,0:T(8,128)(2,1)S(1)}, bf16[128,128]{1,0:T(8,128)(2,1)S(1)}, u32[]{:S(2)}, u32[]{:S(2)}) collective-permute-start(bf16[128,128]{1,0:T(8,128)(2,1)S(1)} %get-tuple-element.35.refs_3_), channel_id=1, source_target_pairs={{0,3},{1,2},{2,1},{3,0},{4,7},{5,6},{6,5},{7,4},{8,11},{9,10},{10,... | collective-permute-start | bytes 98312 | tf_op jit(solution)/shard_map/ppermute | solution.py:325
  42.2 11.8 %copy-start.1 = (bf16[512,1024]{1,0:T(8,128)(2,1)S(1)}, bf16[512,1024]{1,0:T(8,128)(2,1)}, u32[]{:S(2)}) copy-start(bf16[512,1024]{1,0:T(8,128)(2,1)} %refs_1_.1) | copy-start | bytes 3145732
  42.2 11.7 %all-to-all-start.1 = ((bf16[8,128,128]{2,1,0:T(8,128)(2,1)}), bf16[8,128,128]{2,1,0:T(8,128)(2,1)S(1)}, u32[]{:S(2)}, u32[]{:S(2)}) async-start(bf16[8,128,128]{2,1,0:T(8,128)(2,1)} %get-tuple-element.45), calls=%async_computation.1 | async-start | bytes 524288 | tf_op jit(solution)/shard_map/all_to_all | solution.py:417
  51.6 34.5 %copy-start.2 = (bf16[272,256]{1,0:T(8,128)(2,1)S(1)}, bf16[272,256]{1,0:T(8,128)(2,1)}, u32[]{:S(2)}) copy-start(bf16[272,256]{1,0:T(8,128)(2,1)} %get-tuple-element.52.refs_0_) | copy-start | bytes 417796
  51.7 1.7 %collective-permute-start.10 = (bf16[272,256]{1,0:T(8,128)(2,1)}, bf16[272,256]{1,0:T(8,128)(2,1)S(1)}, u32[]{:S(2)}, u32[]{:S(2)}) collective-permute-start(bf16[272,256]{1,0:T(8,128)(2,1)} %get-tuple-element.50), channel_id=1, source_target_pairs={{0,32},{32,0},{64,96},{96,64},{128,160},{160,128},{192,224},{224,1... | collective-permute-start | bytes 417800 | tf_op jit(solution)/shard_map/ppermute | solution.py:325
  55.1 33.9 %all-to-all-start.2 = ((bf16[32,4,1152]{2,1,0:T(4,128)(2,1)}), bf16[32,4,1152]{2,1,0:T(4,128)(2,1)S(1)}, u32[]{:S(2)}, u32[]{:S(2)}) async-start(bf16[32,4,1152]{2,1,0:T(4,128)(2,1)} %project.1), calls=%async_computation.2 | async-start | bytes 589824 | tf_op jit(solution)/shard_map/all_to_all | solution.py:452
  64.9 7.7 %collective-permute-start.11 = (bf16[272,256]{1,0:T(8,128)(2,1)}, bf16[272,256]{1,0:T(8,128)(2,1)S(1)}, u32[]{:S(2)}, u32[]{:S(2)}) collective-permute-start(bf16[272,256]{1,0:T(8,128)(2,1)} %get-tuple-element.54), channel_id=1, source_target_pairs={{0,64},{32,96},{64,0},{96,32},{128,192},{160,224},{192,128},{224,1... | collective-permute-start | bytes 417800 | tf_op jit(solution)/shard_map/ppermute | solution.py:325
  66.3 10.0 %collective-permute-start.12 = (bf16[272,256]{1,0:T(8,128)(2,1)}, bf16[272,256]{1,0:T(8,128)(2,1)S(1)}, u32[]{:S(2)}, u32[]{:S(2)}) collective-permute-start(bf16[272,256]{1,0:T(8,128)(2,1)} %get-tuple-element.55), channel_id=1, source_target_pairs={{0,96},{32,64},{64,32},{96,0},{128,224},{160,192},{192,160},{224,1... | collective-permute-start | bytes 417800 | tf_op jit(solution)/shard_map/ppermute | solution.py:325
  67.6 10.4 %collective-permute-start.13 = (bf16[272,256]{1,0:T(8,128)(2,1)}, bf16[272,256]{1,0:T(8,128)(2,1)S(1)}, u32[]{:S(2)}, u32[]{:S(2)}) collective-permute-start(bf16[272,256]{1,0:T(8,128)(2,1)} %get-tuple-element.56), channel_id=1, source_target_pairs={{0,128},{32,160},{64,192},{96,224},{128,0},{160,32},{192,64},{224,... | collective-permute-start | bytes 417800 | tf_op jit(solution)/shard_map/ppermute | solution.py:325
  70.1 11.8 %collective-permute-start.14 = (bf16[272,256]{1,0:T(8,128)(2,1)}, bf16[272,256]{1,0:T(8,128)(2,1)S(1)}, u32[]{:S(2)}, u32[]{:S(2)}) collective-permute-start(bf16[272,256]{1,0:T(8,128)(2,1)} %get-tuple-element.57), channel_id=1, source_target_pairs={{0,160},{32,128},{64,224},{96,192},{128,32},{160,0},{192,96},{224,... | collective-permute-start | bytes 417800 | tf_op jit(solution)/shard_map/ppermute | solution.py:325
  70.4 12.3 %collective-permute-start.15 = (bf16[272,256]{1,0:T(8,128)(2,1)}, bf16[272,256]{1,0:T(8,128)(2,1)S(1)}, u32[]{:S(2)}, u32[]{:S(2)}) collective-permute-start(bf16[272,256]{1,0:T(8,128)(2,1)} %get-tuple-element.58), channel_id=1, source_target_pairs={{0,192},{32,224},{64,128},{96,160},{128,64},{160,96},{192,0},{224,... | collective-permute-start | bytes 417800 | tf_op jit(solution)/shard_map/ppermute | solution.py:325
  72.6 13.6 %collective-permute-start.16 = (bf16[272,256]{1,0:T(8,128)(2,1)}, bf16[272,256]{1,0:T(8,128)(2,1)S(1)}, u32[]{:S(2)}, u32[]{:S(2)}) collective-permute-start(bf16[272,256]{1,0:T(8,128)(2,1)} %get-tuple-element.59), channel_id=1, source_target_pairs={{0,224},{32,192},{64,160},{96,128},{128,96},{160,64},{192,32},{224... | collective-permute-start | bytes 417800 | tf_op jit(solution)/shard_map/ppermute | solution.py:325
  (11 other events, 22.0 us)

commit v3 on v2

--- a/solution.py
+++ b/solution.py
@@ -205,26 +205,28 @@
     for load in loads:
         load.start()
     x_t = conv[...].astype(F32).T[0:HD]
+    b = b_in[...]
     for load in loads:
         load.wait()
+    saves = []
     for i in range(8):
+        rows = [row_of(STEPS - 1, j // 2, 2 * i + j % 2) for j in range(4)]
+        left = jnp.concatenate([x_t * coef_ref[row : row + 1, :] for row in rows], axis=0).astype(BF16)
+        update = dot(left, b)
         for j in range(4):
-            s, beam = j // 2, 2 * i + j % 2
-            row = row_of(STEPS - 1, s, beam)
-            at = beam
+            s, at = j // 2, 2 * i + j % 2
             for step in range(STEPS - 1, -1, -1):
                 at = parents[step * BEAMS + s * WIDTH + at]
-            origin_s = (at >> 1) * 4 + s * 2 + (at & 1)
-            left = (x_t * coef_ref[row : row + 1, :]).astype(BF16)
-            keep = jnp.broadcast_to(first_ref[row : row + 1, 0:1], (HD, NS))
-            value = keep * state[origin_s].astype(F32) + dot(left, b_in[...])
+            origin = (at >> 1) * 4 + s * 2 + (at & 1)
+            keep = jnp.broadcast_to(first_ref[rows[j] : rows[j] + 1, 0:1], (HD, NS))
+            value = keep * state[origin].astype(F32) + update[HD * j : HD * j + HD]
             block[i, HD * j : HD * j + HD, :] = value.astype(BF16)
         taps = [fin[k, 4 * i : 4 * i + 4, 0:64].astype(F32) for k in range(3)]
         tail = jnp.concatenate(taps + [jnp.zeros((4, 64), F32)], axis=1)
         block[i, 4 * HD : 4 * HD + 16, :] = jnp.concatenate([tail, jnp.zeros((12, NS), F32)], axis=0).astype(BF16)
-    saves = [pltpu.make_async_copy(block.at[head ^ k], homes[k], sem_home.at[k]) for k in range(8)]
-    for copy in saves:
-        copy.start()
+    for k in range(8):
+        saves.append(pltpu.make_async_copy(block.at[head ^ k], homes[k], sem_home.at[k]))
+        saves[-1].start()
     for copy in saves:
         copy.wait()
 
@@ -415,7 +417,7 @@
         *states,
     )
     gathered = lax.all_to_all(send, "beam", split_axis=0, concat_axis=0, tiled=True)
-    final = call(
+    final = list(call(
         final_kernel,
         "final",
         [SM, VM] + [FAR] * 4 + [ANY] * 8,
@@ -427,9 +429,9 @@
             pltpu.SemaphoreType.DMA((8,)),
         ],
         out_specs=[ANY] * 8,
-    )(parents.reshape(ROWS), conv, b_in, coef, first, fin, *states)
+    )(parents.reshape(ROWS), conv, b_in, coef, first, fin, *states))
+    gathered, *final = lax.optimization_barrier((gathered, *final))
     homes = [final[0]] + [swap(final[k], "beam", 8, k) for k in range(1, 8)]
-    gathered, homes[1] = lax.optimization_barrier((gathered, homes[1]))
     ssm_final, conv_x_rows = call(
         unpack_kernel,
         "unpack",

time: 90.4 us -> 90.1 us (level)
  waiting for transfers between devices: 14 us -> 16.1 us
  local copies, waits for them, and re-layouts: 7.62 us -> 6.04 us
    all_to_all x1, waiting for transfers between devices: 0.01 us -> 2.08 us  [local(): lax.all_to_all(send, 'beam', split_axis=0, concat_axis=0, tiled=True)]
    unnamed x47 -> x43, local copies, waits for them, and re-layouts: 3.35 us -> 1.78 us
where the time goes in v3:
time: 90.1 us; the launch traced here: 89.4 us
  starting transfers between devices  48.7 us (54%)
  waiting for transfers between devices  16.1 us (18%)
  Pallas kernels  15.6 us (17%)
  local copies, waits for them, and re-layouts  6.04 us (7%)
  between operations  1 us (1%)
  other arithmetic  0.98 us (1%)
    ppermute x17, starting transfers between devices, swap(): return lax.ppermute(value, axis, [(i, i ^ mask) for i in range(count)])  27.2 us
    pallas_call x7, Pallas kernels, build(): pl.pallas_call(body, name=name, in_specs=list(specs), out_specs=tuple(out...  15.6 us
    ppermute x17, waiting for transfers between devices, swap(): return lax.ppermute(value, axis, [(i, i ^ mask) for i in range(count)])  14 us
    all_to_all x1, starting transfers between devices, local(): lax.all_to_all(parts, 'row', split_axis=0, concat_axis=0, tiled=True)  9.78 us
    all_to_all x1, starting transfers between devices, local(): lax.all_to_all(payload, 'beam', split_axis=0, concat_axis=0, tiled=True)  6.81 us
    all_to_all x1, starting transfers between devices, local(): lax.all_to_all(send, 'beam', split_axis=0, concat_axis=0, tiled=True)  4.93 us
    all_to_all x1, waiting for transfers between devices, local(): lax.all_to_all(send, 'beam', split_axis=0, concat_axis=0, tiled=True)  2.08 us
  transfers between devices with their start and end apart: 20, of which 7 were waited for; matrix products, arithmetic and copies ran while one was open for 2% of the time, Pallas kernels for 12%

profile of v3, /device:TPU:1, one launch (start us, length us, event | category | flops | bytes accessed | tf_op | source)
XLA Modules:
  0.0 89.4 jit_solution(12414786509798028500)
XLA Ops:
  0.7 1.2 %reshape.86 = bf16[4,8,4,1024]{3,2,1,0:T(4,128)(2,1)S(1)} reshape(bf16[4,2,16,1024]{3,2,1,0:T(8,128)(2,1)} %param.15) | data formatting | bytes 524288 | tf_op jit(solution)/shard_map/reshape | solution.py:351
  4.3 1.0 %maximum_maximum_fusion = bf16[8,144,256]{2,1,0:T(8,128)(2,1)} fusion(bf16[8,1,128]{2,1,0:T(2,128)(2,1)S(1)} %copy.54, bf16[8,1,128]{2,1,0:T(2,128)(2,1)S(1)} %copy.53, bf16[8,12,64]{2,1,0:T(8,128)(2,1)S(1)} %copy.52, bf16[8,128,128]{2,1,0:T(8,128)(2,1)S(1)} %copy.49, bf16[144]{0:T(256)(128)(2,1)S(1)} %pad.7.clone, bf16[144,256]{1,0:T(8,128)(2,1)S(1)} %pad.4.clone, ...), kind=kLoop, calls=%fused_computation.3 | loop fusion | flops 4718592 | bytes 1089824 | tf_op jit(solution)/shard_map/concatenate | solution.py:364
  5.3 6.8 %all-to-all-start = ((bf16[8,144,256]{2,1,0:T(8,128)(2,1)}), bf16[8,144,256]{2,1,0:T(8,128)(2,1)S(1)}, u32[]{:S(2)}, u32[]{:S(2)}) async-start(bf16[8,144,256]{2,1,0:T(8,128)(2,1)} %maximum_maximum_fusion), calls=%async_computation | async-start | bytes 1179648 | tf_op jit(solution)/shard_map/all_to_all | solution.py:365
  12.1 2.2 %pack.1 = (bf16[4,64,256]{2,1,0:T(8,128)(2,1)}, bf16[4,64,256]{2,1,0:T(8,128)(2,1)}, bf16[4,64,256]{2,1,0:T(8,128)(2,1)}, bf16[4,64,256]{2,1,0:T(8,128)(2,1)}, b...) custom-call(bf16[2,2,8,64,256]{4,3,2,1,0:T(8,128)(2,1)} %refs_0_.1), custom_call_target="tpu_custom_call" | custom-call | tf_op jit(solution)/shard_map/pack/pallas_call | solution.py:310
  14.6 1.6 %collective-permute-start.4 = (bf16[4,64,256]{2,1,0:T(8,128)(2,1)}, bf16[4,64,256]{2,1,0:T(8,128)(2,1)S(1)}, u32[]{:S(2)}, u32[]{:S(2)}) collective-permute-start(bf16[4,64,256]{2,1,0:T(8,128)(2,1)} %get-tuple-element.46), channel_id=1, source_target_pairs={{0,64},{32,96},{64,0},{96,32},{128,192},{160,224},{192,128},{224,1... | collective-permute-start | bytes 393224 | tf_op jit(solution)/shard_map/ppermute | solution.py:327
  16.6 2.9 %collective-permute-start.6 = (bf16[4,64,256]{2,1,0:T(8,128)(2,1)}, bf16[4,64,256]{2,1,0:T(8,128)(2,1)S(1)}, u32[]{:S(2)}, u32[]{:S(2)}) collective-permute-start(bf16[4,64,256]{2,1,0:T(8,128)(2,1)} %get-tuple-element.48), channel_id=1, source_target_pairs={{0,128},{32,160},{64,192},{96,224},{128,0},{160,32},{192,64},{224,... | collective-permute-start | bytes 393224 | tf_op jit(solution)/shard_map/ppermute | solution.py:327
  19.8 2.6 %collective-permute-start.8 = (bf16[4,64,256]{2,1,0:T(8,128)(2,1)}, bf16[4,64,256]{2,1,0:T(8,128)(2,1)}, u32[]{:S(2)}, u32[]{:S(2)}) collective-permute-start(bf16[4,64,256]{2,1,0:T(8,128)(2,1)} %get-tuple-element.50), channel_id=1, source_target_pairs={{0,192},{32,224},{64,128},{96,160},{128,64},{160,96},{192,0},{224,... | collective-permute-start | bytes 393224 | tf_op jit(solution)/shard_map/ppermute | solution.py:327
  22.4 1.2 %collective-permute-done.4.refs_14_.refs_8_ = bf16[4,64,256]{2,1,0:T(8,128)(2,1)S(1)} collective-permute-done((bf16[4,64,256]{2,1,0:T(8,128)(2,1)}, bf16[4,64,256]{2,1,0:T(8,128)(2,1)S(1)}, u32[]{:S(2)}, u32[]{:S(2)}) %collective-permute-start.4) | collective-permute-done | bytes 131104 | tf_op jit(solution)/shard_map/ppermute | solution.py:327
  23.6 3.0 %collective-permute-start.9 = (bf16[4,64,256]{2,1,0:T(8,128)(2,1)}, bf16[4,64,256]{2,1,0:T(8,128)(2,1)}, u32[]{:S(2)}, u32[]{:S(2)}) collective-permute-start(bf16[4,64,256]{2,1,0:T(8,128)(2,1)} %get-tuple-element.51), channel_id=1, source_target_pairs={{0,224},{32,192},{64,160},{96,128},{128,96},{160,64},{192,32},{224... | collective-permute-start | bytes 393224 | tf_op jit(solution)/shard_map/ppermute | solution.py:327
  27.0 0.8 copy-done.9
  27.8 2.0 %conv.1 = (bf16[128,256]{1,0:T(8,128)(2,1)S(1)}, bf16[128,128]{1,0:T(8,128)(2,1)S(1)}, bf16[128,128]{1,0:T(8,128)(2,1)S(1)}, f32[1,128]{1,0:T(1,128)S(1)}, bf16[3,32,256]{2,1,0:T(8,128)(2,1)S(1)}) custom-call(bf16[8,144,256]{2,1,0:T(8,128)(2,1)} %copy-done.9, s32[128,1]{1,0:T(8,128)S(1)} %reshape.102.refs_1_.refs_0_, bf16[4,512]{1,0:T(4,128)(2,1)S(1)} %copy-done.4, ...), custom_call_target="tpu_custom_call" | custom-call | tf_op jit(solution)/shard_map/conv/pallas_call | solution.py:310
  31.2 3.0 %collective-permute-start.1 = (bf16[128,128]{1,0:T(8,128)(2,1)S(1)}, bf16[128,128]{1,0:T(8,128)(2,1)S(1)}, u32[]{:S(2)}, u32[]{:S(2)}) collective-permute-start(bf16[128,128]{1,0:T(8,128)(2,1)S(1)} %get-tuple-element.42.refs_3_), channel_id=1, source_target_pairs={{0,2},{1,3},{2,0},{3,1},{4,6},{5,7},{6,4},{7,5},{8,10},{9,11},{10,... | collective-permute-start | bytes 98312 | tf_op jit(solution)/shard_map/ppermute | solution.py:327
  34.2 3.0 %collective-permute-start.2 = (bf16[128,128]{1,0:T(8,128)(2,1)S(1)}, bf16[128,128]{1,0:T(8,128)(2,1)S(1)}, u32[]{:S(2)}, u32[]{:S(2)}) collective-permute-start(bf16[128,128]{1,0:T(8,128)(2,1)S(1)} %get-tuple-element.42.refs_3_), channel_id=1, source_target_pairs={{0,3},{1,2},{2,1},{3,0},{4,7},{5,6},{6,5},{7,4},{8,11},{9,10},{10,... | collective-permute-start | bytes 98312 | tf_op jit(solution)/shard_map/ppermute | solution.py:327
  37.3 1.5 %collective-permute-done.2.refs_6_ = bf16[128,128]{1,0:T(8,128)(2,1)S(1)} collective-permute-done((bf16[128,128]{1,0:T(8,128)(2,1)S(1)}, bf16[128,128]{1,0:T(8,128)(2,1)S(1)}, u32[]{:S(2)}, u32[]{:S(2)}) %collective-permute-start.2) | collective-permute-done | bytes 32800 | tf_op jit(solution)/shard_map/ppermute | solution.py:327
  38.9 3.4 %scan.1 = (bf16[8,128,128]{2,1,0:T(8,128)(2,1)}, bf16[128,256]{1,0:T(8,128)(2,1)}, f32[128,128]{1,0:T(8,128)}, f32[128,128]{1,0:T(8,128)}) custom-call(s32[128,1]{1,0:T(8,128)S(1)} %reshape.102.refs_1_.refs_0_, bf16[128,256]{1,0:T(8,128)(2,1)S(1)} %get-tuple-element.40.refs_1_, bf16[128,128]{1,0:T(8,128)(2,1)S(1)} %get-tuple-element.41.refs_2_.refs_1_, ...), custom_call_target="tpu_custom_call" | custom-call | tf_op jit(solution)/shard_map/scan/pallas_call | solution.py:310
  42.2 4.9 %all-to-all-start.1 = ((bf16[8,128,128]{2,1,0:T(8,128)(2,1)}), bf16[8,128,128]{2,1,0:T(8,128)(2,1)S(1)}, u32[]{:S(2)}, u32[]{:S(2)}) async-start(bf16[8,128,128]{2,1,0:T(8,128)(2,1)} %get-tuple-element.52), calls=%async_computation.1 | async-start | bytes 524288 | tf_op jit(solution)/shard_map/all_to_all | solution.py:419
  47.3 4.3 %final.1 = (bf16[272,256]{1,0:T(8,128)(2,1)}, bf16[272,256]{1,0:T(8,128)(2,1)}, bf16[272,256]{1,0:T(8,128)(2,1)}, bf16[272,256]{1,0:T(8,128)(2,1)}, bf16[272,256...) custom-call(s32[128]{0:T(128)S(1)} %reshape.96.refs_0_, ...), custom_call_target="tpu_custom_call" | custom-call | tf_op jit(solution)/shard_map/final/pallas_call | solution.py:310
  51.6 2.1 %all-to-all-done.1.refs_0_ = bf16[8,128,128]{2,1,0:T(8,128)(2,1)S(1)} async-done(((bf16[8,128,128]{2,1,0:T(8,128)(2,1)}), bf16[8,128,128]{2,1,0:T(8,128)(2,1)S(1)}, u32[]{:S(2)}, u32[]{:S(2)}) %all-to-all-start.1) | async-done | bytes 262176 | tf_op jit(solution)/shard_map/all_to_all | solution.py:419
  53.7 1.1 %project.1 = bf16[32,4,1152]{2,1,0:T(4,128)(2,1)} custom-call(bf16[8,128,128]{2,1,0:T(8,128)(2,1)S(1)} %all-to-all-done.1.refs_0_, bf16[512,1024]{1,0:T(8,128)(2,1)S(1)} %copy-done.1), custom_call_target="tpu_custom_call" | custom-call | tf_op jit(solution)/shard_map/project/pallas_call | solution.py:310
  54.8 9.8 %all-to-all-start.2 = ((bf16[32,4,1152]{2,1,0:T(4,128)(2,1)}), bf16[32,4,1152]{2,1,0:T(4,128)(2,1)S(1)}, u32[]{:S(2)}, u32[]{:S(2)}) async-start(bf16[32,4,1152]{2,1,0:T(4,128)(2,1)} %project.1), calls=%async_computation.2 | async-start | bytes 589824 | tf_op jit(solution)/shard_map/all_to_all | solution.py:454
  64.6 1.4 %collective-permute-start.10 = (bf16[272,256]{1,0:T(8,128)(2,1)}, bf16[272,256]{1,0:T(8,128)(2,1)S(1)}, u32[]{:S(2)}, u32[]{:S(2)}) collective-permute-start(bf16[272,256]{1,0:T(8,128)(2,1)} %get-tuple-element.67), channel_id=1, source_target_pairs={{0,32},{32,0},{64,96},{96,64},{128,160},{160,128},{192,224},{224,1... | collective-permute-start | bytes 417800 | tf_op jit(solution)/shard_map/ppermute | solution.py:327
  66.3 1.4 %collective-permute-start.12 = (bf16[272,256]{1,0:T(8,128)(2,1)}, bf16[272,256]{1,0:T(8,128)(2,1)S(1)}, u32[]{:S(2)}, u32[]{:S(2)}) collective-permute-start(bf16[272,256]{1,0:T(8,128)(2,1)} %get-tuple-element.69), channel_id=1, source_target_pairs={{0,96},{32,64},{64,32},{96,0},{128,224},{160,192},{192,160},{224,1... | collective-permute-start | bytes 417800 | tf_op jit(solution)/shard_map/ppermute | solution.py:327
  68.3 2.7 %collective-permute-start.14 = (bf16[272,256]{1,0:T(8,128)(2,1)}, bf16[272,256]{1,0:T(8,128)(2,1)S(1)}, u32[]{:S(2)}, u32[]{:S(2)}) collective-permute-start(bf16[272,256]{1,0:T(8,128)(2,1)} %get-tuple-element.71), channel_id=1, source_target_pairs={{0,160},{32,128},{64,224},{96,192},{128,32},{160,0},{192,96},{224,... | collective-permute-start | bytes 417800 | tf_op jit(solution)/shard_map/ppermute | solution.py:327
  71.0 0.9 collective-permute-start.15
  71.9 2.0 %collective-permute-start.16 = (bf16[272,256]{1,0:T(8,128)(2,1)}, bf16[272,256]{1,0:T(8,128)(2,1)S(1)}, u32[]{:S(2)}, u32[]{:S(2)}) collective-permute-start(bf16[272,256]{1,0:T(8,128)(2,1)} %get-tuple-element.73), channel_id=1, source_target_pairs={{0,224},{32,192},{64,160},{96,128},{128,96},{160,64},{192,32},{224... | collective-permute-start | bytes 417800 | tf_op jit(solution)/shard_map/ppermute | solution.py:327
  73.9 0.8 constant_dynamic-slice_fusion
  75.4 2.6 %collective-permute-done.13.refs_4_ = bf16[272,256]{1,0:T(8,128)(2,1)S(1)} collective-permute-done((bf16[272,256]{1,0:T(8,128)(2,1)}, bf16[272,256]{1,0:T(8,128)(2,1)S(1)}, u32[]{:S(2)}, u32[]{:S(2)}) %collective-permute-start.13) | collective-permute-done | bytes 139296 | tf_op jit(solution)/shard_map/ppermute | solution.py:327
  78.0 3.2 %collective-permute-done.14.refs_5_ = bf16[272,256]{1,0:T(8,128)(2,1)S(1)} collective-permute-done((bf16[272,256]{1,0:T(8,128)(2,1)}, bf16[272,256]{1,0:T(8,128)(2,1)S(1)}, u32[]{:S(2)}, u32[]{:S(2)}) %collective-permute-start.14) | collective-permute-done | bytes 139296 | tf_op jit(solution)/shard_map/ppermute | solution.py:327
  81.2 2.5 %collective-permute-done.15.refs_6_ = bf16[272,256]{1,0:T(8,128)(2,1)S(1)} collective-permute-done((bf16[272,256]{1,0:T(8,128)(2,1)}, bf16[272,256]{1,0:T(8,128)(2,1)S(1)}, u32[]{:S(2)}, u32[]{:S(2)}) %collective-permute-start.15) | collective-permute-done | bytes 139296 | tf_op jit(solution)/shard_map/ppermute | solution.py:327
  83.8 3.0 %collective-permute-done.16.refs_7_ = bf16[272,256]{1,0:T(8,128)(2,1)S(1)} collective-permute-done((bf16[272,256]{1,0:T(8,128)(2,1)}, bf16[272,256]{1,0:T(8,128)(2,1)S(1)}, u32[]{:S(2)}, u32[]{:S(2)}) %collective-permute-start.16) | collective-permute-done | bytes 139296 | tf_op jit(solution)/shard_map/ppermute | solution.py:327
  86.7 1.8 %unpack.1 = (bf16[2,2,8,64,256]{4,3,2,1,0:T(8,128)(2,1)}, bf16[2,2,3,8,64]{4,3,2,1,0:T(8,128)(2,1)}) custom-call(bf16[272,256]{1,0:T(8,128)(2,1)S(1)} %copy-done.2, bf16[272,256]{1,0:T(8,128)(2,1)S(1)} %collective-permute-done.10.refs_1_, bf16[272,256]{1,0:T(8,128)(2,1)S(1)} %collective-permute-done.11.refs_2_, ...), custom_call_target="tpu_custom_call" | custom-call | tf_op jit(solution)/shard_map/unpack/pallas_call | solution.py:310
  88.6 0.8 norm.1
  (91 shorter events, 6.7 us)
Async XLA Ops:
  5.3 21.3 %copy-start.18 = (s32[4,2,16]{2,1,0:T(2,128)S(1)}, s32[4,2,16]{2,1,0:T(2,128)}, u32[]{:S(2)}) copy-start(s32[4,2,16]{2,1,0:T(2,128)} %param.29) | copy-start | bytes 1540
  5.3 21.6 %copy-start.20 = (bf16[4,2,64]{2,1,0:T(2,128)(2,1)S(1)}, bf16[4,2,64]{2,1,0:T(2,128)(2,1)}, u32[]{:S(2)}) copy-start(bf16[4,2,64]{2,1,0:T(2,128)(2,1)} %param.20) | copy-start | bytes 3076
  5.3 22.6 %copy-start.4 = (bf16[4,512]{1,0:T(4,128)(2,1)S(1)}, bf16[4,512]{1,0:T(4,128)(2,1)}, u32[]{:S(2)}) copy-start(bf16[4,512]{1,0:T(4,128)(2,1)} %refs_2_.1) | copy-start | bytes 12292
  5.3 21.7 %all-to-all-start = ((bf16[8,144,256]{2,1,0:T(8,128)(2,1)}), bf16[8,144,256]{2,1,0:T(8,128)(2,1)S(1)}, u32[]{:S(2)}, u32[]{:S(2)}) async-start(bf16[8,144,256]{2,1,0:T(8,128)(2,1)} %maximum_maximum_fusion), calls=%async_computation | async-start | bytes 1179648 | tf_op jit(solution)/shard_map/all_to_all | solution.py:365
  12.1 26.7 %copy-start.5 = (f32[512]{0:T(512)S(1)}, f32[512]{0:T(512)}, u32[]{:S(2)}) copy-start(f32[512]{0:T(512)} %param.24) | copy-start | bytes 6148
  12.1 26.7 %copy-start.6 = (f32[8]{0:T(128)S(1)}, f32[8]{0:T(128)}, u32[]{:S(2)}) copy-start(f32[8]{0:T(128)} %param.22) | copy-start | bytes 100
  12.1 26.7 %copy-start.7 = (f32[8]{0:T(128)S(1)}, f32[8]{0:T(128)}, u32[]{:S(2)}) copy-start(f32[8]{0:T(128)} %param.21) | copy-start | bytes 100
  12.1 26.7 %copy-start.8 = (f32[8]{0:T(128)S(1)}, f32[8]{0:T(128)}, u32[]{:S(2)}) copy-start(f32[8]{0:T(128)} %param.23) | copy-start | bytes 100
  14.3 5.4 %collective-permute-start.3 = (bf16[4,64,256]{2,1,0:T(8,128)(2,1)}, bf16[4,64,256]{2,1,0:T(8,128)(2,1)S(1)}, u32[]{:S(2)}, u32[]{:S(2)}) collective-permute-start(bf16[4,64,256]{2,1,0:T(8,128)(2,1)} %get-tuple-element.45), channel_id=1, source_target_pairs={{0,32},{32,0},{64,96},{96,64},{128,160},{160,128},{192,224},{224,1... | collective-permute-start | bytes 393224 | tf_op jit(solution)/shard_map/ppermute | solution.py:327
  14.6 9.0 %collective-permute-start.4 = (bf16[4,64,256]{2,1,0:T(8,128)(2,1)}, bf16[4,64,256]{2,1,0:T(8,128)(2,1)S(1)}, u32[]{:S(2)}, u32[]{:S(2)}) collective-permute-start(bf16[4,64,256]{2,1,0:T(8,128)(2,1)} %get-tuple-element.46), channel_id=1, source_target_pairs={{0,64},{32,96},{64,0},{96,32},{128,192},{160,224},{192,128},{224,1... | collective-permute-start | bytes 393224 | tf_op jit(solution)/shard_map/ppermute | solution.py:327
  16.2 14.3 %collective-permute-start.5 = (bf16[4,64,256]{2,1,0:T(8,128)(2,1)}, bf16[4,64,256]{2,1,0:T(8,128)(2,1)S(1)}, u32[]{:S(2)}, u32[]{:S(2)}) collective-permute-start(bf16[4,64,256]{2,1,0:T(8,128)(2,1)} %get-tuple-element.47), channel_id=1, source_target_pairs={{0,96},{32,64},{64,32},{96,0},{128,224},{160,192},{192,160},{224,1... | collective-permute-start | bytes 393224 | tf_op jit(solution)/shard_map/ppermute | solution.py:327
  16.6 14.7 %collective-permute-start.6 = (bf16[4,64,256]{2,1,0:T(8,128)(2,1)}, bf16[4,64,256]{2,1,0:T(8,128)(2,1)S(1)}, u32[]{:S(2)}, u32[]{:S(2)}) collective-permute-start(bf16[4,64,256]{2,1,0:T(8,128)(2,1)} %get-tuple-element.48), channel_id=1, source_target_pairs={{0,128},{32,160},{64,192},{96,224},{128,0},{160,32},{192,64},{224,... | collective-permute-start | bytes 393224 | tf_op jit(solution)/shard_map/ppermute | solution.py:327
  19.5 14.7 %collective-permute-start.7 = (bf16[4,64,256]{2,1,0:T(8,128)(2,1)}, bf16[4,64,256]{2,1,0:T(8,128)(2,1)S(1)}, u32[]{:S(2)}, u32[]{:S(2)}) collective-permute-start(bf16[4,64,256]{2,1,0:T(8,128)(2,1)} %get-tuple-element.49), channel_id=1, source_target_pairs={{0,160},{32,128},{64,224},{96,192},{128,32},{160,0},{192,96},{224,... | collective-permute-start | bytes 393224 | tf_op jit(solution)/shard_map/ppermute | solution.py:327
  19.8 19.0 %copy-start.10 = (bf16[4,64,256]{2,1,0:T(8,128)(2,1)}, bf16[4,64,256]{2,1,0:T(8,128)(2,1)S(1)}, u32[]{:S(2)}) copy-start(bf16[4,64,256]{2,1,0:T(8,128)(2,1)S(1)} %collective-permute-done.3.refs_13_.refs_7_) | copy-start | bytes 393220
  19.8 17.5 %collective-permute-start.8 = (bf16[4,64,256]{2,1,0:T(8,128)(2,1)}, bf16[4,64,256]{2,1,0:T(8,128)(2,1)}, u32[]{:S(2)}, u32[]{:S(2)}) collective-permute-start(bf16[4,64,256]{2,1,0:T(8,128)(2,1)} %get-tuple-element.50), channel_id=1, source_target_pairs={{0,192},{32,224},{64,128},{96,160},{128,64},{160,96},{192,0},{224,... | collective-permute-start | bytes 393224 | tf_op jit(solution)/shard_map/ppermute | solution.py:327
  23.6 15.2 %copy-start.11 = (bf16[4,64,256]{2,1,0:T(8,128)(2,1)}, bf16[4,64,256]{2,1,0:T(8,128)(2,1)S(1)}, u32[]{:S(2)}) copy-start(bf16[4,64,256]{2,1,0:T(8,128)(2,1)S(1)} %collective-permute-done.4.refs_14_.refs_8_) | copy-start | bytes 393220
  23.6 13.7 %collective-permute-start.9 = (bf16[4,64,256]{2,1,0:T(8,128)(2,1)}, bf16[4,64,256]{2,1,0:T(8,128)(2,1)}, u32[]{:S(2)}, u32[]{:S(2)}) collective-permute-start(bf16[4,64,256]{2,1,0:T(8,128)(2,1)} %get-tuple-element.51), channel_id=1, source_target_pairs={{0,224},{32,192},{64,160},{96,128},{128,96},{160,64},{192,32},{224... | collective-permute-start | bytes 393224 | tf_op jit(solution)/shard_map/ppermute | solution.py:327
  30.5 8.3 %copy-start.12 = (bf16[4,64,256]{2,1,0:T(8,128)(2,1)}, bf16[4,64,256]{2,1,0:T(8,128)(2,1)S(1)}, u32[]{:S(2)}) copy-start(bf16[4,64,256]{2,1,0:T(8,128)(2,1)S(1)} %collective-permute-done.5.refs_15_.refs_9_) | copy-start | bytes 393220
  30.5 6.8 %collective-permute-start = (bf16[128,128]{1,0:T(8,128)(2,1)S(1)}, bf16[128,128]{1,0:T(8,128)(2,1)S(1)}, u32[]{:S(2)}, u32[]{:S(2)}) collective-permute-start(bf16[128,128]{1,0:T(8,128)(2,1)S(1)} %get-tuple-element.42.refs_3_), channel_id=1, source_target_pairs={{0,1},{1,0},{2,3},{3,2},{4,5},{5,4},{6,7},{7,6},{8,9},{9,8},{10,11... | collective-permute-start | bytes 98312 | tf_op jit(solution)/shard_map/ppermute | solution.py:327
  31.2 6.0 %collective-permute-start.1 = (bf16[128,128]{1,0:T(8,128)(2,1)S(1)}, bf16[128,128]{1,0:T(8,128)(2,1)S(1)}, u32[]{:S(2)}, u32[]{:S(2)}) collective-permute-start(bf16[128,128]{1,0:T(8,128)(2,1)S(1)} %get-tuple-element.42.refs_3_), channel_id=1, source_target_pairs={{0,2},{1,3},{2,0},{3,1},{4,6},{5,7},{6,4},{7,5},{8,10},{9,11},{10,... | collective-permute-start | bytes 98312 | tf_op jit(solution)/shard_map/ppermute | solution.py:327
  34.2 4.6 %collective-permute-start.2 = (bf16[128,128]{1,0:T(8,128)(2,1)S(1)}, bf16[128,128]{1,0:T(8,128)(2,1)S(1)}, u32[]{:S(2)}, u32[]{:S(2)}) collective-permute-start(bf16[128,128]{1,0:T(8,128)(2,1)S(1)} %get-tuple-element.42.refs_3_), channel_id=1, source_target_pairs={{0,3},{1,2},{2,1},{3,0},{4,7},{5,6},{6,5},{7,4},{8,11},{9,10},{10,... | collective-permute-start | bytes 98312 | tf_op jit(solution)/shard_map/ppermute | solution.py:327
  42.2 11.5 %copy-start.1 = (bf16[512,1024]{1,0:T(8,128)(2,1)S(1)}, bf16[512,1024]{1,0:T(8,128)(2,1)}, u32[]{:S(2)}) copy-start(bf16[512,1024]{1,0:T(8,128)(2,1)} %refs_1_.1) | copy-start | bytes 3145732
  42.2 11.5 %all-to-all-start.1 = ((bf16[8,128,128]{2,1,0:T(8,128)(2,1)}), bf16[8,128,128]{2,1,0:T(8,128)(2,1)S(1)}, u32[]{:S(2)}, u32[]{:S(2)}) async-start(bf16[8,128,128]{2,1,0:T(8,128)(2,1)} %get-tuple-element.52), calls=%async_computation.1 | async-start | bytes 524288 | tf_op jit(solution)/shard_map/all_to_all | solution.py:419
  51.6 35.1 %copy-start.2 = (bf16[272,256]{1,0:T(8,128)(2,1)S(1)}, bf16[272,256]{1,0:T(8,128)(2,1)}, u32[]{:S(2)}) copy-start(bf16[272,256]{1,0:T(8,128)(2,1)} %get-tuple-element.66.refs_0_) | copy-start | bytes 417796
  54.8 33.8 %all-to-all-start.2 = ((bf16[32,4,1152]{2,1,0:T(4,128)(2,1)}), bf16[32,4,1152]{2,1,0:T(4,128)(2,1)S(1)}, u32[]{:S(2)}, u32[]{:S(2)}) async-start(bf16[32,4,1152]{2,1,0:T(4,128)(2,1)} %project.1), calls=%async_computation.2 | async-start | bytes 589824 | tf_op jit(solution)/shard_map/all_to_all | solution.py:454
  64.6 6.4 %collective-permute-start.10 = (bf16[272,256]{1,0:T(8,128)(2,1)}, bf16[272,256]{1,0:T(8,128)(2,1)S(1)}, u32[]{:S(2)}, u32[]{:S(2)}) collective-permute-start(bf16[272,256]{1,0:T(8,128)(2,1)} %get-tuple-element.67), channel_id=1, source_target_pairs={{0,32},{32,0},{64,96},{96,64},{128,160},{160,128},{192,224},{224,1... | collective-permute-start | bytes 417800 | tf_op jit(solution)/shard_map/ppermute | solution.py:327
  66.0 5.9 %collective-permute-start.11 = (bf16[272,256]{1,0:T(8,128)(2,1)}, bf16[272,256]{1,0:T(8,128)(2,1)S(1)}, u32[]{:S(2)}, u32[]{:S(2)}) collective-permute-start(bf16[272,256]{1,0:T(8,128)(2,1)} %get-tuple-element.68), channel_id=1, source_target_pairs={{0,64},{32,96},{64,0},{96,32},{128,192},{160,224},{192,128},{224,1... | collective-permute-start | bytes 417800 | tf_op jit(solution)/shard_map/ppermute | solution.py:327
  66.3 9.1 %collective-permute-start.12 = (bf16[272,256]{1,0:T(8,128)(2,1)}, bf16[272,256]{1,0:T(8,128)(2,1)S(1)}, u32[]{:S(2)}, u32[]{:S(2)}) collective-permute-start(bf16[272,256]{1,0:T(8,128)(2,1)} %get-tuple-element.69), channel_id=1, source_target_pairs={{0,96},{32,64},{64,32},{96,0},{128,224},{160,192},{192,160},{224,1... | collective-permute-start | bytes 417800 | tf_op jit(solution)/shard_map/ppermute | solution.py:327
  67.7 10.3 %collective-permute-start.13 = (bf16[272,256]{1,0:T(8,128)(2,1)}, bf16[272,256]{1,0:T(8,128)(2,1)S(1)}, u32[]{:S(2)}, u32[]{:S(2)}) collective-permute-start(bf16[272,256]{1,0:T(8,128)(2,1)} %get-tuple-element.70), channel_id=1, source_target_pairs={{0,128},{32,160},{64,192},{96,224},{128,0},{160,32},{192,64},{224,... | collective-permute-start | bytes 417800 | tf_op jit(solution)/shard_map/ppermute | solution.py:327
  68.3 13.0 %collective-permute-start.14 = (bf16[272,256]{1,0:T(8,128)(2,1)}, bf16[272,256]{1,0:T(8,128)(2,1)S(1)}, u32[]{:S(2)}, u32[]{:S(2)}) collective-permute-start(bf16[272,256]{1,0:T(8,128)(2,1)} %get-tuple-element.71), channel_id=1, source_target_pairs={{0,160},{32,128},{64,224},{96,192},{128,32},{160,0},{192,96},{224,... | collective-permute-start | bytes 417800 | tf_op jit(solution)/shard_map/ppermute | solution.py:327
  71.0 12.8 %collective-permute-start.15 = (bf16[272,256]{1,0:T(8,128)(2,1)}, bf16[272,256]{1,0:T(8,128)(2,1)S(1)}, u32[]{:S(2)}, u32[]{:S(2)}) collective-permute-start(bf16[272,256]{1,0:T(8,128)(2,1)} %get-tuple-element.72), channel_id=1, source_target_pairs={{0,192},{32,224},{64,128},{96,160},{128,64},{160,96},{192,0},{224,... | collective-permute-start | bytes 417800 | tf_op jit(solution)/shard_map/ppermute | solution.py:327
  71.9 14.9 %collective-permute-start.16 = (bf16[272,256]{1,0:T(8,128)(2,1)}, bf16[272,256]{1,0:T(8,128)(2,1)S(1)}, u32[]{:S(2)}, u32[]{:S(2)}) collective-permute-start(bf16[272,256]{1,0:T(8,128)(2,1)} %get-tuple-element.73), channel_id=1, source_target_pairs={{0,224},{32,192},{64,160},{96,128},{128,96},{160,64},{192,32},{224... | collective-permute-start | bytes 417800 | tf_op jit(solution)/shard_map/ppermute | solution.py:327
  (9 other events, 20.5 us)

commit v4 on v3

--- a/solution.py
+++ b/solution.py
@@ -66,21 +66,15 @@
 
 
 def pack_kernel(state, *refs):
-    outs, (held, sem_in, sem_out) = refs[:8], refs[8:]
+    outs, sems = refs[:8], refs[8]
     head = lax.axis_index("beam")
     loads = []
     for k in range(8):
         for j in range(4):
-            loads.append(pltpu.make_async_copy(state.at[j // 2, j % 2, head ^ k], held.at[k, j], sem_in.at[k, j]))
+            loads.append(pltpu.make_async_copy(state.at[j // 2, j % 2, head ^ k], outs[k].at[j], sems.at[k, j]))
             loads[-1].start()
-    copies = []
-    for k in range(8):
-        for j in range(4):
-            loads[4 * k + j].wait()
-        copies.append(pltpu.make_async_copy(held.at[k], outs[k], sem_out.at[k]))
-        copies[-1].start()
-    for copy in copies:
-        copy.wait()
+    for load in loads:
+        load.wait()
 
 
 def conv_kernel(recv, par, conv_x_w, conv_bc_w, sum_out, conv_out, bc_out, dt_out, fin_out, init):
@@ -94,8 +88,12 @@
         for k in range(3):
             init[k, 4 * i : 4 * i + 4, :] = extra[4 * k : 4 * k + 4]
         dt = dt + extra
-    dt_out[...] = dt[12:13, 0:128] + dt[12:13, 128:256]
-    new = total.astype(BF16)
+    r = lax.broadcasted_iota(jnp.int32, (ROWS, ROWS), 0)
+    source = (r & 3) * 32 + ((r & 31) >> 2) * 4 + (r >> 5)
+    order = jnp.where(lax.broadcasted_iota(jnp.int32, (ROWS, ROWS), 1) == source, 1.0, 0.0)
+    dt_sum = (dt[12:13, 0:128] + dt[12:13, 128:256]).astype(BF16)
+    dt_out[...] = dot_t(jnp.broadcast_to(dt_sum, (8, ROWS)), order.astype(BF16))[0:1]
+    new = dot(order.astype(BF16), total.astype(BF16)).astype(BF16)
     t, a1, a2, a3, g = lineage(par[...])
     gb = g.astype(BF16)
     start = [dot(gb, init[k].astype(BF16)) for k in range(3)]
@@ -348,7 +346,7 @@
     d_local = x_in.shape[-1]
     heads = ssm_state.shape[2]
     parent_column = parents.reshape(STEPS, 8, 4).transpose(2, 1, 0).reshape(ROWS, 1)
-    x = x_in.reshape(STEPS, 8, 4, d_local).transpose(2, 1, 0, 3).reshape(ROWS, d_local)
+    x = x_in.reshape(ROWS, d_local)
 
     inner = jnp.einsum("rd,dzk->rzk", x, w_inner, preferred_element_type=F32).astype(BF16)
     inner = inner[:, ::-1].reshape(ROWS, 2, heads, HD).transpose(2, 0, 1, 3).reshape(heads, ROWS, 2 * HD)
@@ -369,12 +367,7 @@
         "pack",
         [ANY],
         [((4, HD, NS), BF16)] * 8,
-        [
-            pltpu.VMEM((8, 4, HD, NS), BF16),
-            pltpu.SemaphoreType.DMA((8, 4)),
-            pltpu.SemaphoreType.DMA((8,)),
-        ],
-        out_specs=[ANY] * 8,
+        [pltpu.SemaphoreType.DMA((8, 4))],
     )(ssm_state)
     states = [packed[0]] + [swap(packed[k], "beam", 8, k) for k in range(1, 8)]
 
@@ -430,8 +423,15 @@
         ],
         out_specs=[ANY] * 8,
     )(parents.reshape(ROWS), conv, b_in, coef, first, fin, *states))
-    gathered, *final = lax.optimization_barrier((gathered, *final))
     homes = [final[0]] + [swap(final[k], "beam", 8, k) for k in range(1, 8)]
+    (parts,) = call(
+        out_kernel,
+        "project",
+        [VM, VM],
+        [((BEAMS, STEPS, 1152), BF16)],
+    )(gathered, w_out)
+    parts, homes[1], homes[2], homes[6] = lax.optimization_barrier((parts, homes[1], homes[2], homes[6]))
+    spread = lax.all_to_all(parts, "row", split_axis=0, concat_axis=0, tiled=True)
     ssm_final, conv_x_rows = call(
         unpack_kernel,
         "unpack",
@@ -445,13 +445,6 @@
     )(*homes)
     conv_x_final = conv_x_rows.transpose(0, 1, 3, 4, 2)
 
-    (parts,) = call(
-        out_kernel,
-        "project",
-        [VM, VM],
-        [((BEAMS, STEPS, 1152), BF16)],
-    )(gathered, w_out)
-    spread = lax.all_to_all(parts, "row", split_axis=0, concat_axis=0, tiled=True)
     (layer_out,) = call(norm_kernel, "norm", [VM], [((STEPS, 1024), BF16)])(spread)
     layer_out = layer_out[:, None]
 

time: 90.1 us -> 92.6 us (1.028)
  matrix products: 0.85 us -> 3.94 us
  starting transfers between devices: 48.7 us -> 47.6 us
    ppermute x17, waiting for transfers between devices: 14 us -> 16.6 us  [swap(): return lax.ppermute(value, axis, [(i, i ^ mask) for i in range(count)])]
    all_to_all x1, waiting for transfers between devices: 2.08 us -> 0.01 us  [local(): lax.all_to_all(send, 'beam', split_axis=0, concat_axis=0, tiled=True)]
    reshape x3 -> x0, local copies, waits for them, and re-layouts: 1.33 us -> none  [local(): x_in.reshape(STEPS, 8, 4, d_local).transpose(2, 1, 0, 3)]
    unnamed x43 -> x35, local copies, waits for them, and re-layouts: 1.78 us -> 3.05 us
    dot_general x1, matrix products: 0.17 us -> 1.28 us  [local(): dt = jnp.einsum('dh,rd->hr', w_dt, x, preferred_element_type=F32)]
    unnamed x1, matrix products: 0.23 us -> 1.26 us
    dot_general x1, matrix products: 0.45 us -> 1.4 us  [local(): jnp.einsum('rd,dzk->rzk', x, w_inner, preferred_element_type=F32)]
  transfers between devices with their start and end apart: 20 -> 20, of which waited for: 7 -> 7; matrix products, arithmetic and copies ran while one was open for 2% -> 2% of each run, Pallas kernels for 12% -> 13%
where the time goes in v4:
time: 92.6 us; the launch traced here: 91.8 us
  starting transfers between devices  47.6 us (51%)
  waiting for transfers between devices  16.6 us (18%)
  Pallas kernels  16 us (17%)
  local copies, waits for them, and re-layouts  5.77 us (6%)
  matrix products  3.94 us (4%)
  other arithmetic  0.98 us (1%)
  between operations  0.93 us (1%)
    ppermute x17, starting transfers between devices, swap(): return lax.ppermute(value, axis, [(i, i ^ mask) for i in range(count)])  27.1 us
    ppermute x17, waiting for transfers between devices, swap(): return lax.ppermute(value, axis, [(i, i ^ mask) for i in range(count)])  16.6 us
    pallas_call x7, Pallas kernels, build(): pl.pallas_call(body, name=name, in_specs=list(specs), out_specs=tuple(out...  16 us
    all_to_all x1, starting transfers between devices, local(): lax.all_to_all(parts, 'row', split_axis=0, concat_axis=0, tiled=True)  9.52 us
    all_to_all x1, starting transfers between devices, local(): lax.all_to_all(payload, 'beam', split_axis=0, concat_axis=0, tiled=True)  6.81 us
    all_to_all x1, starting transfers between devices, local(): lax.all_to_all(send, 'beam', split_axis=0, concat_axis=0, tiled=True)  4.11 us
    unnamed x35, local copies, waits for them, and re-layouts  3.05 us
  transfers between devices with their start and end apart: 20, of which 7 were waited for; matrix products, arithmetic and copies ran while one was open for 2% of the time, Pallas kernels for 13%

profile of v4, /device:TPU:1, one launch (start us, length us, event | category | flops | bytes accessed | tf_op | source)
XLA Modules:
  0.0 91.8 jit_solution(10513437035502977132)
XLA Ops:
  0.6 1.3 %fusion.7 = (bf16[8,1,128]{2,0,1:T(8,128)(2,1)S(1)}, bf16[8,1,128]{2,0,1:T(8,128)(2,1)S(1)}) fusion(bf16[1024,8]{0,1:T(8,128)(2,1)} %param.18, bf16[128,1024]{1,0:T(8,128)(2,1)} %bitcast.37), kind=kOutput, calls=%fused_computation.9 | convolution fusion | flops 2101248 | bytes 282624 | tf_op jit(solution)/shard_map/dh,rd->hr/dot_general | solution.py:355
  2.0 1.3 %fusion.8 = f32[128,128]{0,1:S(1)} fusion(bf16[128,1024]{1,0:T(8,128)(2,1)} %bitcast.38, bf16[1024,128]{0,1:T(8,128)(2,1)} %bitcast.43), kind=kOutput, calls=%fused_computation.11 | convolution fusion | flops 33554432 | bytes 589824
  3.4 1.4 %fusion.2 = bf16[128,2,512]{2,0,1:T(8,128)(2,1)S(1)} fusion(bf16[128,1024,1]{1,0,2:T(8,128)(2,1)} %bitcast.39, bf16[1024,2,512]{2,1,0:T(2,128)(2,1)S(1)} %copy-done), kind=kOutput, calls=%fused_computation.2 | convolution fusion | flops 268566528 | bytes 2621440 | tf_op jit(solution)/shard_map/rd,dzk->rzk/dot_general | solution.py:351
  5.8 1.0 %maximum_maximum_fusion = bf16[8,144,256]{2,1,0:T(8,128)(2,1)} fusion(bf16[8,1,128]{2,1,0:T(2,128)(2,1)S(1)} %copy.51, bf16[8,1,128]{2,1,0:T(2,128)(2,1)S(1)} %copy.50, bf16[8,12,64]{2,1,0:T(8,128)(2,1)S(1)} %copy.49, bf16[8,128,128]{2,1,0:T(8,128)(2,1)S(1)} %copy.46, bf16[144]{0:T(256)(128)(2,1)S(1)} %pad.7.clone, bf16[144,256]{1,0:T(8,128)(2,1)S(1)} %pad.4.clone, ...), kind=kLoop, calls=%fused_computation.3 | loop fusion | flops 4718592 | bytes 1089824 | tf_op jit(solution)/shard_map/concatenate | solution.py:362
  6.8 6.8 %all-to-all-start = ((bf16[8,144,256]{2,1,0:T(8,128)(2,1)}), bf16[8,144,256]{2,1,0:T(8,128)(2,1)S(1)}, u32[]{:S(2)}, u32[]{:S(2)}) async-start(bf16[8,144,256]{2,1,0:T(8,128)(2,1)} %maximum_maximum_fusion), calls=%async_computation | async-start | bytes 1179648 | tf_op jit(solution)/shard_map/all_to_all | solution.py:363
  13.6 1.5 %pack.1 = (bf16[4,64,256]{2,1,0:T(8,128)(2,1)S(1)}, bf16[4,64,256]{2,1,0:T(8,128)(2,1)S(1)}, bf16[4,64,256]{2,1,0:T(8,128)(2,1)S(1)}, bf16[4,64,256]{2,1,0:T(8,1...) custom-call(bf16[2,2,8,64,256]{4,3,2,1,0:T(8,128)(2,1)} %refs_0_.1), custom_call_target="tpu_custom_call" | custom-call | tf_op jit(solution)/shard_map/pack/pallas_call | solution.py:308
  15.9 1.6 %collective-permute-start.4 = (bf16[4,64,256]{2,1,0:T(8,128)(2,1)S(1)}, bf16[4,64,256]{2,1,0:T(8,128)(2,1)S(1)}, u32[]{:S(2)}, u32[]{:S(2)}) collective-permute-start(bf16[4,64,256]{2,1,0:T(8,128)(2,1)S(1)} %get-tuple-element.41), channel_id=1, source_target_pairs={{0,64},{32,96},{64,0},{96,32},{128,192},{160,224},{192,128},{224,1... | collective-permute-start | bytes 393224 | tf_op jit(solution)/shard_map/ppermute | solution.py:325
  17.9 2.9 %collective-permute-start.6 = (bf16[4,64,256]{2,1,0:T(8,128)(2,1)S(1)}, bf16[4,64,256]{2,1,0:T(8,128)(2,1)}, u32[]{:S(2)}, u32[]{:S(2)}) collective-permute-start(bf16[4,64,256]{2,1,0:T(8,128)(2,1)S(1)} %get-tuple-element.43), channel_id=1, source_target_pairs={{0,128},{32,160},{64,192},{96,224},{128,0},{160,32},{192,64},{224,... | collective-permute-start | bytes 393224 | tf_op jit(solution)/shard_map/ppermute | solution.py:325
  21.1 2.6 %collective-permute-start.8 = (bf16[4,64,256]{2,1,0:T(8,128)(2,1)S(1)}, bf16[4,64,256]{2,1,0:T(8,128)(2,1)}, u32[]{:S(2)}, u32[]{:S(2)}) collective-permute-start(bf16[4,64,256]{2,1,0:T(8,128)(2,1)S(1)} %get-tuple-element.45), channel_id=1, source_target_pairs={{0,192},{32,224},{64,128},{96,160},{128,64},{160,96},{192,0},{224,... | collective-permute-start | bytes 393224 | tf_op jit(solution)/shard_map/ppermute | solution.py:325
  23.8 1.3 %collective-permute-done.4.refs_14_.refs_8_ = bf16[4,64,256]{2,1,0:T(8,128)(2,1)S(1)} collective-permute-done((bf16[4,64,256]{2,1,0:T(8,128)(2,1)S(1)}, bf16[4,64,256]{2,1,0:T(8,128)(2,1)S(1)}, u32[]{:S(2)}, u32[]{:S(2)}) %collective-permute-start.4) | collective-permute-done | bytes 131104 | tf_op jit(solution)/shard_map/ppermute | solution.py:325
  25.8 3.0 %collective-permute-start.9 = (bf16[4,64,256]{2,1,0:T(8,128)(2,1)S(1)}, bf16[4,64,256]{2,1,0:T(8,128)(2,1)}, u32[]{:S(2)}, u32[]{:S(2)}) collective-permute-start(bf16[4,64,256]{2,1,0:T(8,128)(2,1)S(1)} %get-tuple-element.46), channel_id=1, source_target_pairs={{0,224},{32,192},{64,160},{96,128},{128,96},{160,64},{192,32},{224... | collective-permute-start | bytes 393224 | tf_op jit(solution)/shard_map/ppermute | solution.py:325
  29.2 0.8 copy-done.10
  30.0 2.1 %conv.1 = (bf16[128,256]{1,0:T(8,128)(2,1)S(1)}, bf16[128,128]{1,0:T(8,128)(2,1)S(1)}, bf16[128,128]{1,0:T(8,128)(2,1)S(1)}, f32[1,128]{1,0:T(1,128)S(1)}, bf16[3,32,256]{2,1,0:T(8,128)(2,1)S(1)}) custom-call(bf16[8,144,256]{2,1,0:T(8,128)(2,1)} %copy-done.10, s32[128,1]{1,0:T(8,128)S(1)} %reshape.97.refs_1_.refs_0_, bf16[4,512]{1,0:T(4,128)(2,1)S(1)} %copy-done.5, ...), custom_call_target="tpu_custom_call" | custom-call | tf_op jit(solution)/shard_map/conv/pallas_call | solution.py:308
  33.4 3.0 %collective-permute-start.1 = (bf16[128,128]{1,0:T(8,128)(2,1)S(1)}, bf16[128,128]{1,0:T(8,128)(2,1)S(1)}, u32[]{:S(2)}, u32[]{:S(2)}) collective-permute-start(bf16[128,128]{1,0:T(8,128)(2,1)S(1)} %get-tuple-element.37.refs_3_), channel_id=1, source_target_pairs={{0,2},{1,3},{2,0},{3,1},{4,6},{5,7},{6,4},{7,5},{8,10},{9,11},{10,... | collective-permute-start | bytes 98312 | tf_op jit(solution)/shard_map/ppermute | solution.py:325
  36.4 2.4 %collective-permute-start.2 = (bf16[128,128]{1,0:T(8,128)(2,1)S(1)}, bf16[128,128]{1,0:T(8,128)(2,1)S(1)}, u32[]{:S(2)}, u32[]{:S(2)}) collective-permute-start(bf16[128,128]{1,0:T(8,128)(2,1)S(1)} %get-tuple-element.37.refs_3_), channel_id=1, source_target_pairs={{0,3},{1,2},{2,1},{3,0},{4,7},{5,6},{6,5},{7,4},{8,11},{9,10},{10,... | collective-permute-start | bytes 98312 | tf_op jit(solution)/shard_map/ppermute | solution.py:325
  38.9 2.6 %collective-permute-done.2.refs_6_ = bf16[128,128]{1,0:T(8,128)(2,1)S(1)} collective-permute-done((bf16[128,128]{1,0:T(8,128)(2,1)S(1)}, bf16[128,128]{1,0:T(8,128)(2,1)S(1)}, u32[]{:S(2)}, u32[]{:S(2)}) %collective-permute-start.2) | collective-permute-done | bytes 32800 | tf_op jit(solution)/shard_map/ppermute | solution.py:325
  41.5 3.4 %scan.1 = (bf16[8,128,128]{2,1,0:T(8,128)(2,1)}, bf16[128,256]{1,0:T(8,128)(2,1)}, f32[128,128]{1,0:T(8,128)}, f32[128,128]{1,0:T(8,128)}) custom-call(s32[128,1]{1,0:T(8,128)S(1)} %reshape.97.refs_1_.refs_0_, bf16[128,256]{1,0:T(8,128)(2,1)S(1)} %get-tuple-element.35.refs_1_, bf16[128,128]{1,0:T(8,128)(2,1)S(1)} %get-tuple-element.36.refs_2_.refs_1_, ...), custom_call_target="tpu_custom_call" | custom-call | tf_op jit(solution)/shard_map/scan/pallas_call | solution.py:308
  44.9 4.1 %all-to-all-start.1 = ((bf16[8,128,128]{2,1,0:T(8,128)(2,1)}), bf16[8,128,128]{2,1,0:T(8,128)(2,1)S(1)}, u32[]{:S(2)}, u32[]{:S(2)}) async-start(bf16[8,128,128]{2,1,0:T(8,128)(2,1)} %get-tuple-element.47), calls=%async_computation.1 | async-start | bytes 524288 | tf_op jit(solution)/shard_map/all_to_all | solution.py:412
  49.1 4.4 %final.1 = (bf16[272,256]{1,0:T(8,128)(2,1)}, bf16[272,256]{1,0:T(8,128)(2,1)}, bf16[272,256]{1,0:T(8,128)(2,1)}, bf16[272,256]{1,0:T(8,128)(2,1)}, bf16[272,256...) custom-call(s32[128]{0:T(128)S(1)} %reshape.92.refs_0_, ...), custom_call_target="tpu_custom_call" | custom-call | tf_op jit(solution)/shard_map/final/pallas_call | solution.py:308
  53.6 1.6 %collective-permute-start.11 = (bf16[272,256]{1,0:T(8,128)(2,1)}, bf16[272,256]{1,0:T(8,128)(2,1)}, u32[]{:S(2)}, u32[]{:S(2)}) collective-permute-start(bf16[272,256]{1,0:T(8,128)(2,1)} %get-tuple-element.53), channel_id=1, source_target_pairs={{0,64},{32,96},{64,0},{96,32},{128,192},{160,224},{192,128},{224,1... | collective-permute-start | bytes 417800 | tf_op jit(solution)/shard_map/ppermute | solution.py:325
  55.3 1.8 %collective-permute-start.12 = (bf16[272,256]{1,0:T(8,128)(2,1)}, bf16[272,256]{1,0:T(8,128)(2,1)}, u32[]{:S(2)}, u32[]{:S(2)}) collective-permute-start(bf16[272,256]{1,0:T(8,128)(2,1)} %get-tuple-element.54), channel_id=1, source_target_pairs={{0,192},{32,224},{64,128},{96,160},{128,64},{160,96},{192,0},{224,... | collective-permute-start | bytes 417800 | tf_op jit(solution)/shard_map/ppermute | solution.py:325
  57.1 1.1 %project.1 = bf16[32,4,1152]{2,1,0:T(4,128)(2,1)} custom-call(bf16[8,128,128]{2,1,0:T(8,128)(2,1)S(1)} %all-to-all-done.1.refs_0_, bf16[512,1024]{1,0:T(8,128)(2,1)S(1)} %copy-done.1), custom_call_target="tpu_custom_call" | custom-call | tf_op jit(solution)/shard_map/project/pallas_call | solution.py:308
  58.2 1.0 %collective-permute-done.11.refs_2_ = bf16[272,256]{1,0:T(8,128)(2,1)} collective-permute-done((bf16[272,256]{1,0:T(8,128)(2,1)}, bf16[272,256]{1,0:T(8,128)(2,1)}, u32[]{:S(2)}, u32[]{:S(2)}) %collective-permute-start.11) | collective-permute-done | bytes 139296 | tf_op jit(solution)/shard_map/ppermute | solution.py:325
  59.2 2.4 %collective-permute-done.12.refs_6_ = bf16[272,256]{1,0:T(8,128)(2,1)} collective-permute-done((bf16[272,256]{1,0:T(8,128)(2,1)}, bf16[272,256]{1,0:T(8,128)(2,1)}, u32[]{:S(2)}, u32[]{:S(2)}) %collective-permute-start.12) | collective-permute-done | bytes 139296 | tf_op jit(solution)/shard_map/ppermute | solution.py:325
  61.6 9.5 %all-to-all-start.2 = ((bf16[32,4,1152]{2,1,0:T(4,128)(2,1)}), bf16[32,4,1152]{2,1,0:T(4,128)(2,1)S(1)}, u32[]{:S(2)}, u32[]{:S(2)}) async-start(bf16[32,4,1152]{2,1,0:T(4,128)(2,1)} %project.1), calls=%async_computation.2 | async-start | bytes 589824 | tf_op jit(solution)/shard_map/all_to_all | solution.py:434
  71.2 1.0 %collective-permute-start.13 = (bf16[272,256]{1,0:T(8,128)(2,1)}, bf16[272,256]{1,0:T(8,128)(2,1)S(1)}, u32[]{:S(2)}, u32[]{:S(2)}) collective-permute-start(bf16[272,256]{1,0:T(8,128)(2,1)} %get-tuple-element.59), channel_id=1, source_target_pairs={{0,96},{32,64},{64,32},{96,0},{128,224},{160,192},{192,160},{224,1... | collective-permute-start | bytes 417800 | tf_op jit(solution)/shard_map/ppermute | solution.py:325
  72.1 3.6 %collective-permute-start.14 = (bf16[272,256]{1,0:T(8,128)(2,1)}, bf16[272,256]{1,0:T(8,128)(2,1)S(1)}, u32[]{:S(2)}, u32[]{:S(2)}) collective-permute-start(bf16[272,256]{1,0:T(8,128)(2,1)} %get-tuple-element.60), channel_id=1, source_target_pairs={{0,128},{32,160},{64,192},{96,224},{128,0},{160,32},{192,64},{224,... | collective-permute-start | bytes 417800 | tf_op jit(solution)/shard_map/ppermute | solution.py:325
  76.0 1.4 %collective-permute-start.16 = (bf16[272,256]{1,0:T(8,128)(2,1)}, bf16[272,256]{1,0:T(8,128)(2,1)S(1)}, u32[]{:S(2)}, u32[]{:S(2)}) collective-permute-start(bf16[272,256]{1,0:T(8,128)(2,1)} %get-tuple-element.63), channel_id=1, source_target_pairs={{0,224},{32,192},{64,160},{96,128},{128,96},{160,64},{192,32},{224... | collective-permute-start | bytes 417800 | tf_op jit(solution)/shard_map/ppermute | solution.py:325
  78.9 4.2 %collective-permute-done.14.refs_4_ = bf16[272,256]{1,0:T(8,128)(2,1)S(1)} collective-permute-done((bf16[272,256]{1,0:T(8,128)(2,1)}, bf16[272,256]{1,0:T(8,128)(2,1)S(1)}, u32[]{:S(2)}, u32[]{:S(2)}) %collective-permute-start.14) | collective-permute-done | bytes 139296 | tf_op jit(solution)/shard_map/ppermute | solution.py:325
  83.1 1.3 %collective-permute-done.15.refs_5_ = bf16[272,256]{1,0:T(8,128)(2,1)S(1)} collective-permute-done((bf16[272,256]{1,0:T(8,128)(2,1)}, bf16[272,256]{1,0:T(8,128)(2,1)S(1)}, u32[]{:S(2)}, u32[]{:S(2)}) %collective-permute-start.15) | collective-permute-done | bytes 139296 | tf_op jit(solution)/shard_map/ppermute | solution.py:325
  84.4 3.7 %collective-permute-done.16.refs_7_ = bf16[272,256]{1,0:T(8,128)(2,1)S(1)} collective-permute-done((bf16[272,256]{1,0:T(8,128)(2,1)}, bf16[272,256]{1,0:T(8,128)(2,1)S(1)}, u32[]{:S(2)}, u32[]{:S(2)}) %collective-permute-start.16) | collective-permute-done | bytes 139296 | tf_op jit(solution)/shard_map/ppermute | solution.py:325
  88.1 2.9 %unpack.1 = (bf16[2,2,8,64,256]{4,3,2,1,0:T(8,128)(2,1)}, bf16[2,2,3,8,64]{4,3,2,1,0:T(8,128)(2,1)}) custom-call(bf16[272,256]{1,0:T(8,128)(2,1)S(1)} %copy-done.3, bf16[272,256]{1,0:T(8,128)(2,1)} %collective-permute-done.10.refs_1_, bf16[272,256]{1,0:T(8,128)(2,1)} %collective-permute-done.11.refs_2_, ...), custom_call_target="tpu_custom_call" | custom-call | tf_op jit(solution)/shard_map/unpack/pallas_call | solution.py:308
  (79 shorter events, 7.8 us)
Async XLA Ops:
  0.6 2.7 %copy-start = (bf16[1024,2,512]{2,1,0:T(2,128)(2,1)S(1)}, bf16[1024,2,512]{2,1,0:T(2,128)(2,1)}, u32[]{:S(2)}) copy-start(bf16[1024,2,512]{2,1,0:T(2,128)(2,1)} %param.16) | copy-start | bytes 6291460
  4.8 0.9 copy-start.13
  6.8 22.0 %copy-start.14 = (s32[4,2,16]{2,1,0:T(2,128)S(1)}, s32[4,2,16]{2,1,0:T(2,128)}, u32[]{:S(2)}) copy-start(s32[4,2,16]{2,1,0:T(2,128)} %param.29) | copy-start | bytes 1540
  6.8 22.3 %copy-start.16 = (bf16[4,2,64]{2,1,0:T(2,128)(2,1)S(1)}, bf16[4,2,64]{2,1,0:T(2,128)(2,1)}, u32[]{:S(2)}) copy-start(bf16[4,2,64]{2,1,0:T(2,128)(2,1)} %param.20) | copy-start | bytes 3076
  6.8 23.2 %copy-start.5 = (bf16[4,512]{1,0:T(4,128)(2,1)S(1)}, bf16[4,512]{1,0:T(4,128)(2,1)}, u32[]{:S(2)}) copy-start(bf16[4,512]{1,0:T(4,128)(2,1)} %refs_2_.1) | copy-start | bytes 12292
  6.8 22.4 %all-to-all-start = ((bf16[8,144,256]{2,1,0:T(8,128)(2,1)}), bf16[8,144,256]{2,1,0:T(8,128)(2,1)S(1)}, u32[]{:S(2)}, u32[]{:S(2)}) async-start(bf16[8,144,256]{2,1,0:T(8,128)(2,1)} %maximum_maximum_fusion), calls=%async_computation | async-start | bytes 1179648 | tf_op jit(solution)/shard_map/all_to_all | solution.py:363
  13.6 27.9 %copy-start.6 = (f32[512]{0:T(512)S(1)}, f32[512]{0:T(512)}, u32[]{:S(2)}) copy-start(f32[512]{0:T(512)} %param.24) | copy-start | bytes 6148
  13.6 27.9 %copy-start.7 = (f32[8]{0:T(128)S(1)}, f32[8]{0:T(128)}, u32[]{:S(2)}) copy-start(f32[8]{0:T(128)} %param.22) | copy-start | bytes 100
  13.6 27.9 %copy-start.8 = (f32[8]{0:T(128)S(1)}, f32[8]{0:T(128)}, u32[]{:S(2)}) copy-start(f32[8]{0:T(128)} %param.21) | copy-start | bytes 100
  13.6 27.9 %copy-start.9 = (f32[8]{0:T(128)S(1)}, f32[8]{0:T(128)}, u32[]{:S(2)}) copy-start(f32[8]{0:T(128)} %param.23) | copy-start | bytes 100
  15.8 5.3 %collective-permute-start.3 = (bf16[4,64,256]{2,1,0:T(8,128)(2,1)S(1)}, bf16[4,64,256]{2,1,0:T(8,128)(2,1)S(1)}, u32[]{:S(2)}, u32[]{:S(2)}) collective-permute-start(bf16[4,64,256]{2,1,0:T(8,128)(2,1)S(1)} %get-tuple-element.40), channel_id=1, source_target_pairs={{0,32},{32,0},{64,96},{96,64},{128,160},{160,128},{192,224},{224,1... | collective-permute-start | bytes 393224 | tf_op jit(solution)/shard_map/ppermute | solution.py:325
  15.9 9.2 %collective-permute-start.4 = (bf16[4,64,256]{2,1,0:T(8,128)(2,1)S(1)}, bf16[4,64,256]{2,1,0:T(8,128)(2,1)S(1)}, u32[]{:S(2)}, u32[]{:S(2)}) collective-permute-start(bf16[4,64,256]{2,1,0:T(8,128)(2,1)S(1)} %get-tuple-element.41), channel_id=1, source_target_pairs={{0,64},{32,96},{64,0},{96,32},{128,192},{160,224},{192,128},{224,1... | collective-permute-start | bytes 393224 | tf_op jit(solution)/shard_map/ppermute | solution.py:325
  17.5 15.2 %collective-permute-start.5 = (bf16[4,64,256]{2,1,0:T(8,128)(2,1)S(1)}, bf16[4,64,256]{2,1,0:T(8,128)(2,1)}, u32[]{:S(2)}, u32[]{:S(2)}) collective-permute-start(bf16[4,64,256]{2,1,0:T(8,128)(2,1)S(1)} %get-tuple-element.42), channel_id=1, source_target_pairs={{0,96},{32,64},{64,32},{96,0},{128,224},{160,192},{192,160},{224,1... | collective-permute-start | bytes 393224 | tf_op jit(solution)/shard_map/ppermute | solution.py:325
  17.9 15.5 %collective-permute-start.6 = (bf16[4,64,256]{2,1,0:T(8,128)(2,1)S(1)}, bf16[4,64,256]{2,1,0:T(8,128)(2,1)}, u32[]{:S(2)}, u32[]{:S(2)}) collective-permute-start(bf16[4,64,256]{2,1,0:T(8,128)(2,1)S(1)} %get-tuple-element.43), channel_id=1, source_target_pairs={{0,128},{32,160},{64,192},{96,224},{128,0},{160,32},{192,64},{224,... | collective-permute-start | bytes 393224 | tf_op jit(solution)/shard_map/ppermute | solution.py:325
  20.8 15.6 %collective-permute-start.7 = (bf16[4,64,256]{2,1,0:T(8,128)(2,1)S(1)}, bf16[4,64,256]{2,1,0:T(8,128)(2,1)}, u32[]{:S(2)}, u32[]{:S(2)}) collective-permute-start(bf16[4,64,256]{2,1,0:T(8,128)(2,1)S(1)} %get-tuple-element.44), channel_id=1, source_target_pairs={{0,160},{32,128},{64,224},{96,192},{128,32},{160,0},{192,96},{224,... | collective-permute-start | bytes 393224 | tf_op jit(solution)/shard_map/ppermute | solution.py:325
  21.1 4.0 %copy-start.11 = (bf16[4,64,256]{2,1,0:T(8,128)(2,1)}, bf16[4,64,256]{2,1,0:T(8,128)(2,1)S(1)}, u32[]{:S(2)}) copy-start(bf16[4,64,256]{2,1,0:T(8,128)(2,1)S(1)} %collective-permute-done.3.refs_13_.refs_7_) | copy-start | bytes 393220
  21.1 17.8 %collective-permute-start.8 = (bf16[4,64,256]{2,1,0:T(8,128)(2,1)S(1)}, bf16[4,64,256]{2,1,0:T(8,128)(2,1)}, u32[]{:S(2)}, u32[]{:S(2)}) collective-permute-start(bf16[4,64,256]{2,1,0:T(8,128)(2,1)S(1)} %get-tuple-element.45), channel_id=1, source_target_pairs={{0,192},{32,224},{64,128},{96,160},{128,64},{160,96},{192,0},{224,... | collective-permute-start | bytes 393224 | tf_op jit(solution)/shard_map/ppermute | solution.py:325
  25.8 13.1 %collective-permute-start.9 = (bf16[4,64,256]{2,1,0:T(8,128)(2,1)S(1)}, bf16[4,64,256]{2,1,0:T(8,128)(2,1)}, u32[]{:S(2)}, u32[]{:S(2)}) collective-permute-start(bf16[4,64,256]{2,1,0:T(8,128)(2,1)S(1)} %get-tuple-element.46), channel_id=1, source_target_pairs={{0,224},{32,192},{64,160},{96,128},{128,96},{160,64},{192,32},{224... | collective-permute-start | bytes 393224 | tf_op jit(solution)/shard_map/ppermute | solution.py:325
  32.7 6.2 %collective-permute-start = (bf16[128,128]{1,0:T(8,128)(2,1)S(1)}, bf16[128,128]{1,0:T(8,128)(2,1)S(1)}, u32[]{:S(2)}, u32[]{:S(2)}) collective-permute-start(bf16[128,128]{1,0:T(8,128)(2,1)S(1)} %get-tuple-element.37.refs_3_), channel_id=1, source_target_pairs={{0,1},{1,0},{2,3},{3,2},{4,5},{5,4},{6,7},{7,6},{8,9},{9,8},{10,11... | collective-permute-start | bytes 98312 | tf_op jit(solution)/shard_map/ppermute | solution.py:325
  33.4 5.4 %collective-permute-start.1 = (bf16[128,128]{1,0:T(8,128)(2,1)S(1)}, bf16[128,128]{1,0:T(8,128)(2,1)S(1)}, u32[]{:S(2)}, u32[]{:S(2)}) collective-permute-start(bf16[128,128]{1,0:T(8,128)(2,1)S(1)} %get-tuple-element.37.refs_3_), channel_id=1, source_target_pairs={{0,2},{1,3},{2,0},{3,1},{4,6},{5,7},{6,4},{7,5},{8,10},{9,11},{10,... | collective-permute-start | bytes 98312 | tf_op jit(solution)/shard_map/ppermute | solution.py:325
  36.4 5.0 %collective-permute-start.2 = (bf16[128,128]{1,0:T(8,128)(2,1)S(1)}, bf16[128,128]{1,0:T(8,128)(2,1)S(1)}, u32[]{:S(2)}, u32[]{:S(2)}) collective-permute-start(bf16[128,128]{1,0:T(8,128)(2,1)S(1)} %get-tuple-element.37.refs_3_), channel_id=1, source_target_pairs={{0,3},{1,2},{2,1},{3,0},{4,7},{5,6},{6,5},{7,4},{8,11},{9,10},{10,... | collective-permute-start | bytes 98312 | tf_op jit(solution)/shard_map/ppermute | solution.py:325
  44.9 12.2 %copy-start.1 = (bf16[512,1024]{1,0:T(8,128)(2,1)S(1)}, bf16[512,1024]{1,0:T(8,128)(2,1)}, u32[]{:S(2)}) copy-start(bf16[512,1024]{1,0:T(8,128)(2,1)} %refs_1_.1) | copy-start | bytes 3145732
  44.9 12.2 %all-to-all-start.1 = ((bf16[8,128,128]{2,1,0:T(8,128)(2,1)}), bf16[8,128,128]{2,1,0:T(8,128)(2,1)S(1)}, u32[]{:S(2)}, u32[]{:S(2)}) async-start(bf16[8,128,128]{2,1,0:T(8,128)(2,1)} %get-tuple-element.47), calls=%async_computation.1 | async-start | bytes 524288 | tf_op jit(solution)/shard_map/all_to_all | solution.py:412
  53.4 34.7 %copy-start.3 = (bf16[272,256]{1,0:T(8,128)(2,1)S(1)}, bf16[272,256]{1,0:T(8,128)(2,1)}, u32[]{:S(2)}) copy-start(bf16[272,256]{1,0:T(8,128)(2,1)} %get-tuple-element.56.refs_0_) | copy-start | bytes 417796
  53.4 4.7 %collective-permute-start.10 = (bf16[272,256]{1,0:T(8,128)(2,1)}, bf16[272,256]{1,0:T(8,128)(2,1)}, u32[]{:S(2)}, u32[]{:S(2)}) collective-permute-start(bf16[272,256]{1,0:T(8,128)(2,1)} %get-tuple-element.52), channel_id=1, source_target_pairs={{0,32},{32,0},{64,96},{96,64},{128,160},{160,128},{192,224},{224,1... | collective-permute-start | bytes 417800 | tf_op jit(solution)/shard_map/ppermute | solution.py:325
  53.6 5.6 %collective-permute-start.11 = (bf16[272,256]{1,0:T(8,128)(2,1)}, bf16[272,256]{1,0:T(8,128)(2,1)}, u32[]{:S(2)}, u32[]{:S(2)}) collective-permute-start(bf16[272,256]{1,0:T(8,128)(2,1)} %get-tuple-element.53), channel_id=1, source_target_pairs={{0,64},{32,96},{64,0},{96,32},{128,192},{160,224},{192,128},{224,1... | collective-permute-start | bytes 417800 | tf_op jit(solution)/shard_map/ppermute | solution.py:325
  55.3 6.3 %collective-permute-start.12 = (bf16[272,256]{1,0:T(8,128)(2,1)}, bf16[272,256]{1,0:T(8,128)(2,1)}, u32[]{:S(2)}, u32[]{:S(2)}) collective-permute-start(bf16[272,256]{1,0:T(8,128)(2,1)} %get-tuple-element.54), channel_id=1, source_target_pairs={{0,192},{32,224},{64,128},{96,160},{128,64},{160,96},{192,0},{224,... | collective-permute-start | bytes 417800 | tf_op jit(solution)/shard_map/ppermute | solution.py:325
  61.6 29.4 %all-to-all-start.2 = ((bf16[32,4,1152]{2,1,0:T(4,128)(2,1)}), bf16[32,4,1152]{2,1,0:T(4,128)(2,1)S(1)}, u32[]{:S(2)}, u32[]{:S(2)}) async-start(bf16[32,4,1152]{2,1,0:T(4,128)(2,1)} %project.1), calls=%async_computation.2 | async-start | bytes 589824 | tf_op jit(solution)/shard_map/all_to_all | solution.py:434
  71.2 7.7 %collective-permute-start.13 = (bf16[272,256]{1,0:T(8,128)(2,1)}, bf16[272,256]{1,0:T(8,128)(2,1)S(1)}, u32[]{:S(2)}, u32[]{:S(2)}) collective-permute-start(bf16[272,256]{1,0:T(8,128)(2,1)} %get-tuple-element.59), channel_id=1, source_target_pairs={{0,96},{32,64},{64,32},{96,0},{128,224},{160,192},{192,160},{224,1... | collective-permute-start | bytes 417800 | tf_op jit(solution)/shard_map/ppermute | solution.py:325
  72.1 11.0 %collective-permute-start.14 = (bf16[272,256]{1,0:T(8,128)(2,1)}, bf16[272,256]{1,0:T(8,128)(2,1)S(1)}, u32[]{:S(2)}, u32[]{:S(2)}) collective-permute-start(bf16[272,256]{1,0:T(8,128)(2,1)} %get-tuple-element.60), channel_id=1, source_target_pairs={{0,128},{32,160},{64,192},{96,224},{128,0},{160,32},{192,64},{224,... | collective-permute-start | bytes 417800 | tf_op jit(solution)/shard_map/ppermute | solution.py:325
  75.7 8.7 %collective-permute-start.15 = (bf16[272,256]{1,0:T(8,128)(2,1)}, bf16[272,256]{1,0:T(8,128)(2,1)S(1)}, u32[]{:S(2)}, u32[]{:S(2)}) collective-permute-start(bf16[272,256]{1,0:T(8,128)(2,1)} %get-tuple-element.61), channel_id=1, source_target_pairs={{0,160},{32,128},{64,224},{96,192},{128,32},{160,0},{192,96},{224,... | collective-permute-start | bytes 417800 | tf_op jit(solution)/shard_map/ppermute | solution.py:325
  76.0 12.1 %collective-permute-start.16 = (bf16[272,256]{1,0:T(8,128)(2,1)}, bf16[272,256]{1,0:T(8,128)(2,1)S(1)}, u32[]{:S(2)}, u32[]{:S(2)}) collective-permute-start(bf16[272,256]{1,0:T(8,128)(2,1)} %get-tuple-element.63), channel_id=1, source_target_pairs={{0,224},{32,192},{64,160},{96,128},{128,96},{160,64},{192,32},{224... | collective-permute-start | bytes 417800 | tf_op jit(solution)/shard_map/ppermute | solution.py:325
  (5 other events, 3.4 us)

commit v5 on v4

--- a/solution.py
+++ b/solution.py
@@ -66,15 +66,38 @@
 
 
 def pack_kernel(state, *refs):
-    outs, sems = refs[:8], refs[8]
+    outs, (held, sem_in, sem_out) = refs[:4], refs[4:]
     head = lax.axis_index("beam")
     loads = []
     for k in range(8):
         for j in range(4):
-            loads.append(pltpu.make_async_copy(state.at[j // 2, j % 2, head ^ k], outs[k].at[j], sems.at[k, j]))
+            loads.append(
+                pltpu.make_async_copy(state.at[j // 2, j % 2, head ^ k], held.at[k // 2, k % 2, j], sem_in.at[k, j])
+            )
             loads[-1].start()
+    copies = []
+    for c in range(4):
+        for load in loads[8 * c : 8 * c + 8]:
+            load.wait()
+        copies.append(pltpu.make_async_copy(held.at[c], outs[c], sem_out.at[c]))
+        copies[-1].start()
+    for copy in copies:
+        copy.wait()
+
+
+def merge_kernel(p0, p1, p2, p3, out, held, sems):
+    loads = [pltpu.make_async_copy(p.at[1], held.at[c], sems.at[c]) for c, p in enumerate((p0, p1, p2, p3))]
+    for load in loads:
+        load.start()
     for load in loads:
         load.wait()
+    copy = pltpu.make_async_copy(held, out, sems.at[4])
+    copy.start()
+    copy.wait()
+
+
+def arrived(parts):
+    return [(k, parts[4].at[k // 2] if k % 2 else parts[k // 2].at[0]) for k in range(8)]
 
 
 def conv_kernel(recv, par, conv_x_w, conv_bc_w, sum_out, conv_out, bc_out, dt_out, fin_out, init):
@@ -88,12 +111,8 @@
         for k in range(3):
             init[k, 4 * i : 4 * i + 4, :] = extra[4 * k : 4 * k + 4]
         dt = dt + extra
-    r = lax.broadcasted_iota(jnp.int32, (ROWS, ROWS), 0)
-    source = (r & 3) * 32 + ((r & 31) >> 2) * 4 + (r >> 5)
-    order = jnp.where(lax.broadcasted_iota(jnp.int32, (ROWS, ROWS), 1) == source, 1.0, 0.0)
-    dt_sum = (dt[12:13, 0:128] + dt[12:13, 128:256]).astype(BF16)
-    dt_out[...] = dot_t(jnp.broadcast_to(dt_sum, (8, ROWS)), order.astype(BF16))[0:1]
-    new = dot(order.astype(BF16), total.astype(BF16)).astype(BF16)
+    dt_out[...] = dt[12:13, 0:128] + dt[12:13, 128:256]
+    new = total.astype(BF16)
     t, a1, a2, a3, g = lineage(par[...])
     gb = g.astype(BF16)
     start = [dot(gb, init[k].astype(BF16)) for k in range(3)]
@@ -135,10 +154,10 @@
 def scan_kernel(
     par, new, conv, bc0, bc1, bc2, bc3, dt_raw, norm_gain, a_log, dt_bias, d_skip, *refs
 ):
-    parts, (send_out, b_out, coef_out, first_out) = refs[:8], refs[8:12]
-    state, send, b_buf, coef_buf, first_buf, sem_in, sem_send = refs[12:]
+    parts, (send_out, b_out, coef_out, first_out) = refs[:5], refs[5:9]
+    state, send, b_buf, coef_buf, first_buf, sem_in, sem_send = refs[9:]
     head = lax.axis_index("beam")
-    loads = [pltpu.make_async_copy(parts[k], state.at[pl.ds((head ^ k) * 4, 4)], sem_in.at[k]) for k in range(8)]
+    loads = [pltpu.make_async_copy(p, state.at[pl.ds((head ^ k) * 4, 4)], sem_in.at[k]) for k, p in arrived(parts)]
     for load in loads:
         load.start()
     low = lax.axis_index("row") & 3
@@ -196,10 +215,10 @@
 
 
 def final_kernel(parents, conv, b_in, coef_ref, first_ref, fin, *refs):
-    parts, homes = refs[:8], refs[8:16]
-    state, block, sem_in, sem_home = refs[16:]
+    parts, homes = refs[:5], refs[5:9]
+    state, block, sem_in, sem_home = refs[9:]
     head = lax.axis_index("beam")
-    loads = [pltpu.make_async_copy(parts[k], state.at[pl.ds((head ^ k) * 4, 4)], sem_in.at[k]) for k in range(8)]
+    loads = [pltpu.make_async_copy(p, state.at[pl.ds((head ^ k) * 4, 4)], sem_in.at[k]) for k, p in arrived(parts)]
     for load in loads:
         load.start()
     x_t = conv[...].astype(F32).T[0:HD]
@@ -223,24 +242,28 @@
         tail = jnp.concatenate(taps + [jnp.zeros((4, 64), F32)], axis=1)
         block[i, 4 * HD : 4 * HD + 16, :] = jnp.concatenate([tail, jnp.zeros((12, NS), F32)], axis=0).astype(BF16)
     for k in range(8):
-        saves.append(pltpu.make_async_copy(block.at[head ^ k], homes[k], sem_home.at[k]))
+        saves.append(pltpu.make_async_copy(block.at[head ^ k], homes[k // 2].at[k % 2], sem_home.at[k]))
         saves[-1].start()
     for copy in saves:
         copy.wait()
 
 
 def unpack_kernel(*refs):
-    parts, (ssm_out, conv_out), (tails, sem_out) = refs[:8], refs[8:10], refs[10:]
+    parts, (ssm_out, conv_out), (held, sem_in, sem_out) = refs[:5], refs[5:7], refs[7:]
     head = lax.axis_index("beam")
+    loads = [pltpu.make_async_copy(p, held.at[head ^ k], sem_in.at[k]) for k, p in arrived(parts)]
+    for load in loads:
+        load.start()
     copies = []
     for k in range(8):
+        loads[k].wait()
+        h = head ^ k
         for j in range(4):
-            src = parts[k].at[pl.ds(HD * j, HD)]
-            copies.append(pltpu.make_async_copy(src, ssm_out.at[j // 2, j % 2, head ^ k], sem_out.at[k, j]))
+            src = held.at[h, pl.ds(HD * j, HD)]
+            copies.append(pltpu.make_async_copy(src, ssm_out.at[j // 2, j % 2, h], sem_out.at[k, j]))
             copies[-1].start()
-        tails[head ^ k] = parts[k][4 * HD : 4 * HD + 16, :].astype(F32)
     for h in range(8):
-        tail = tails[h]
+        tail = held[h, 4 * HD : 4 * HD + 16, :].astype(F32)
         for j in range(4):
             for k in range(3):
                 conv_out[j // 2, j % 2, k, h : h + 1, :] = tail[j : j + 1, HD * k : HD * k + HD].astype(BF16)
@@ -323,6 +346,23 @@
 
 def swap(value, axis, count, mask):
     return lax.ppermute(value, axis, [(i, i ^ mask) for i in range(count)])
+
+
+def chips(blocks):
+    return [blocks[0]] + [swap(blocks[c], "beam", 8, 2 * c) for c in range(1, 4)]
+
+
+def cores(got, name):
+    shape = (4,) + got[0].shape[1:]
+    (merged,) = call(
+        merge_kernel,
+        name,
+        [ANY] * 4,
+        [(shape, BF16)],
+        [pltpu.VMEM(shape, BF16), pltpu.SemaphoreType.DMA((5,))],
+        out_specs=[ANY],
+    )(*got)
+    return got + [swap(merged, "beam", 8, 1)]
 
 
 def local(
@@ -346,7 +386,7 @@
     d_local = x_in.shape[-1]
     heads = ssm_state.shape[2]
     parent_column = parents.reshape(STEPS, 8, 4).transpose(2, 1, 0).reshape(ROWS, 1)
-    x = x_in.reshape(ROWS, d_local)
+    x = x_in.reshape(STEPS, 8, 4, d_local).transpose(2, 1, 0, 3).reshape(ROWS, d_local)
 
     inner = jnp.einsum("rd,dzk->rzk", x, w_inner, preferred_element_type=F32).astype(BF16)
     inner = inner[:, ::-1].reshape(ROWS, 2, heads, HD).transpose(2, 0, 1, 3).reshape(heads, ROWS, 2 * HD)
@@ -366,10 +406,15 @@
         pack_kernel,
         "pack",
         [ANY],
-        [((4, HD, NS), BF16)] * 8,
-        [pltpu.SemaphoreType.DMA((8, 4))],
+        [((2, 4, HD, NS), BF16)] * 4,
+        [
+            pltpu.VMEM((4, 2, 4, HD, NS), BF16),
+            pltpu.SemaphoreType.DMA((8, 4)),
+            pltpu.SemaphoreType.DMA((4,)),
+        ],
+        out_specs=[ANY] * 4,
     )(ssm_state)
-    states = [packed[0]] + [swap(packed[k], "beam", 8, k) for k in range(1, 8)]
+    halves = chips(packed)
 
     new, conv, bc_conv, dt_raw, fin = call(
         conv_kernel,
@@ -379,12 +424,14 @@
         [pltpu.VMEM((3, BEAMS, 256), F32)],
     )(recv, parent_column, conv_x_w, conv_bc_w.reshape(4, 128))
 
+    _, *halves = lax.optimization_barrier((bc_conv, *halves))
+    states = cores(halves, "states")
     others = [swap(bc_conv, "row", 32, k) for k in (1, 2, 3)]
 
     send, b_in, coef, first = call(
         scan_kernel,
         "scan",
-        [VM] * 12 + [ANY] * 8,
+        [VM] * 12 + [ANY] * 5,
         [((8, ROWS, 128), BF16), ((ROWS, NS), BF16), ((ROWS, ROWS), F32), ((ROWS, 128), F32)],
         [
             pltpu.VMEM((BEAMS, HD, NS), BF16),
@@ -413,40 +460,41 @@
     final = list(call(
         final_kernel,
         "final",
-        [SM, VM] + [FAR] * 4 + [ANY] * 8,
-        [((4 * HD + 16, NS), BF16)] * 8,
+        [SM, VM] + [FAR] * 4 + [ANY] * 5,
+        [((2, 4 * HD + 16, NS), BF16)] * 4,
         [
             pltpu.VMEM((BEAMS, HD, NS), BF16),
             pltpu.VMEM((8, 4 * HD + 16, NS), BF16),
             pltpu.SemaphoreType.DMA((8,)),
             pltpu.SemaphoreType.DMA((8,)),
         ],
-        out_specs=[ANY] * 8,
+        out_specs=[ANY] * 4,
     )(parents.reshape(ROWS), conv, b_in, coef, first, fin, *states))
-    homes = [final[0]] + [swap(final[k], "beam", 8, k) for k in range(1, 8)]
+    gathered, *final = lax.optimization_barrier((gathered, *final))
+    homes = cores(chips(final), "finals")
     (parts,) = call(
         out_kernel,
         "project",
         [VM, VM],
         [((BEAMS, STEPS, 1152), BF16)],
     )(gathered, w_out)
-    parts, homes[1], homes[2], homes[6] = lax.optimization_barrier((parts, homes[1], homes[2], homes[6]))
     spread = lax.all_to_all(parts, "row", split_axis=0, concat_axis=0, tiled=True)
     ssm_final, conv_x_rows = call(
         unpack_kernel,
         "unpack",
-        [VM] * 8,
+        [ANY] * 5,
         [((SESS, 2, heads, HD, NS), BF16), ((SESS, 2, 3, heads, HD), BF16)],
         [
-            pltpu.VMEM((8, 16, NS), F32),
+            pltpu.VMEM((8, 4 * HD + 16, NS), BF16),
+            pltpu.SemaphoreType.DMA((8,)),
             pltpu.SemaphoreType.DMA((8, 4)),
         ],
         out_specs=[ANY, VM],
     )(*homes)
-    conv_x_final = conv_x_rows.transpose(0, 1, 3, 4, 2)
-
+    spread, conv_x_rows = lax.optimization_barrier((spread, conv_x_rows))
     (layer_out,) = call(norm_kernel, "norm", [VM], [((STEPS, 1024), BF16)])(spread)
     layer_out = layer_out[:, None]
+    conv_x_final = conv_x_rows.transpose(0, 1, 3, 4, 2)
 
     own = lax.dynamic_slice_in_dim(fin, beam * 4, 4, 1)[:, :, 128:]
     conv_bc_final = own.reshape(3, SESS, 2, 2, 64).transpose(1, 2, 0, 3, 4)

time: 92.6 us -> 89.3 us (0.964)
  the two profiles are of different devices: /device:TPU:1 before, /device:TPU:32 now
where the time goes in v5:
time: 89.3 us; the launch traced here: 88 us
  starting transfers between devices  33.9 us (38%)
  waiting for transfers between devices  22.8 us (26%)
  Pallas kernels  20.6 us (23%)
  local copies, waits for them, and re-layouts  7.74 us (9%)
  between operations  0.99 us (1%)
  other arithmetic  0.98 us (1%)
    pallas_call x9, Pallas kernels, build(): pl.pallas_call(body, name=name, in_specs=list(specs), out_specs=tuple(out...  20.6 us
    ppermute x11, starting transfers between devices, swap(): return lax.ppermute(value, axis, [(i, i ^ mask) for i in range(count)])  13.7 us
    all_to_all x1, starting transfers between devices, local(): lax.all_to_all(parts, 'row', split_axis=0, concat_axis=0, tiled=True)  12.3 us
    ppermute x11, waiting for transfers between devices, swap(): return lax.ppermute(value, axis, [(i, i ^ mask) for i in range(count)])  12.1 us
    all_to_all x1, starting transfers between devices, local(): lax.all_to_all(payload, 'beam', split_axis=0, concat_axis=0, tiled=True)  4.43 us
    all_to_all x1, waiting for transfers between devices, local(): lax.all_to_all(payload, 'beam', split_axis=0, concat_axis=0, tiled=True)  4.04 us
    all_to_all x1, waiting for transfers between devices, local(): lax.all_to_all(parts, 'row', split_axis=0, concat_axis=0, tiled=True)  3.73 us
    all_to_all x1, starting transfers between devices, local(): lax.all_to_all(send, 'beam', split_axis=0, concat_axis=0, tiled=True)  3.55 us
  transfers between devices with their start and end apart: 14, of which 9 were waited for; matrix products, arithmetic and copies ran while one was open for 2% of the time, Pallas kernels for 17%

profile of v5, /device:TPU:32, one launch (start us, length us, event | category | flops | bytes accessed | tf_op | source)
XLA Modules:
  0.0 88.0 jit_solution(7816022527501971944)
XLA Ops:
  0.7 1.2 %reshape.86 = bf16[4,8,4,1024]{3,2,1,0:T(4,128)(2,1)S(1)} reshape(bf16[4,2,16,1024]{3,2,1,0:T(8,128)(2,1)} %param.15) | data formatting | bytes 524288 | tf_op jit(solution)/shard_map/reshape | solution.py:389
  4.3 1.0 %maximum_maximum_fusion = bf16[8,144,256]{2,1,0:T(8,128)(2,1)} fusion(bf16[8,1,128]{2,1,0:T(2,128)(2,1)S(1)} %copy.54, bf16[8,1,128]{2,1,0:T(2,128)(2,1)S(1)} %copy.53, bf16[8,12,64]{2,1,0:T(8,128)(2,1)S(1)} %copy.52, bf16[8,128,128]{2,1,0:T(8,128)(2,1)S(1)} %copy.49, bf16[144]{0:T(256)(128)(2,1)S(1)} %pad.7.clone, bf16[144,256]{1,0:T(8,128)(2,1)S(1)} %pad.4.clone, ...), kind=kLoop, calls=%fused_computation.3 | loop fusion | flops 4718592 | bytes 1089824 | tf_op jit(solution)/shard_map/concatenate | solution.py:402
  5.3 4.4 %all-to-all-start = ((bf16[8,144,256]{2,1,0:T(8,128)(2,1)}), bf16[8,144,256]{2,1,0:T(8,128)(2,1)S(1)}, u32[]{:S(2)}, u32[]{:S(2)}) async-start(bf16[8,144,256]{2,1,0:T(8,128)(2,1)} %maximum_maximum_fusion), calls=%async_computation | async-start | bytes 1179648 | tf_op jit(solution)/shard_map/all_to_all | solution.py:403
  9.7 2.2 %pack.1 = (bf16[2,4,64,256]{3,2,1,0:T(8,128)(2,1)}, bf16[2,4,64,256]{3,2,1,0:T(8,128)(2,1)}, bf16[2,4,64,256]{3,2,1,0:T(8,128)(2,1)}, bf16[2,4,64,256]{3,2,1,0:T(8,128)(2,1)}) custom-call(bf16[2,2,8,64,256]{4,3,2,1,0:T(8,128)(2,1)} %refs_0_.1), custom_call_target="tpu_custom_call" | custom-call | tf_op jit(solution)/shard_map/pack/pallas_call | solution.py:331
  11.9 2.1 %collective-permute-start.3 = (bf16[2,4,64,256]{3,2,1,0:T(8,128)(2,1)}, bf16[2,4,64,256]{3,2,1,0:T(8,128)(2,1)S(1)}, u32[]{:S(2)}, u32[]{:S(2)}) collective-permute-start(bf16[2,4,64,256]{3,2,1,0:T(8,128)(2,1)} %get-tuple-element.39), channel_id=1, source_target_pairs={{0,64},{32,96},{64,0},{96,32},{128,192},{160,224},{192,128},{224,1... | collective-permute-start | bytes 786440 | tf_op jit(solution)/shard_map/ppermute | solution.py:348
  14.0 2.7 %collective-permute-start.4 = (bf16[2,4,64,256]{3,2,1,0:T(8,128)(2,1)}, bf16[2,4,64,256]{3,2,1,0:T(8,128)(2,1)S(1)}, u32[]{:S(2)}, u32[]{:S(2)}) collective-permute-start(bf16[2,4,64,256]{3,2,1,0:T(8,128)(2,1)} %get-tuple-element.40), channel_id=1, source_target_pairs={{0,128},{32,160},{64,192},{96,224},{128,0},{160,32},{192,64},{224,... | collective-permute-start | bytes 786440 | tf_op jit(solution)/shard_map/ppermute | solution.py:348
  17.2 4.0 %all-to-all-done.refs_0_ = bf16[8,144,256]{2,1,0:T(8,128)(2,1)S(1)} async-done(((bf16[8,144,256]{2,1,0:T(8,128)(2,1)}), bf16[8,144,256]{2,1,0:T(8,128)(2,1)S(1)}, u32[]{:S(2)}, u32[]{:S(2)}) %all-to-all-start) | async-done | bytes 589856 | tf_op jit(solution)/shard_map/all_to_all | solution.py:403
  21.2 0.8 copy-done.8
  22.1 2.0 %conv.1 = (bf16[128,256]{1,0:T(8,128)(2,1)S(1)}, bf16[128,128]{1,0:T(8,128)(2,1)S(1)}, bf16[128,128]{1,0:T(8,128)(2,1)S(1)}, f32[1,128]{1,0:T(1,128)S(1)}, bf16[3,32,256]{2,1,0:T(8,128)(2,1)S(1)}) custom-call(bf16[8,144,256]{2,1,0:T(8,128)(2,1)} %copy-done.8, s32[128,1]{1,0:T(8,128)S(1)} %reshape.102.refs_1_.refs_0_, bf16[4,512]{1,0:T(4,128)(2,1)S(1)} %copy-done.3, ...), custom_call_target="tpu_custom_call" | custom-call | tf_op jit(solution)/shard_map/conv/pallas_call | solution.py:331
  24.1 1.3 %collective-permute-done.3.refs_1_.refs_13_.refs_7_ = bf16[2,4,64,256]{3,2,1,0:T(8,128)(2,1)S(1)} collective-permute-done((bf16[2,4,64,256]{3,2,1,0:T(8,128)(2,1)}, bf16[2,4,64,256]{3,2,1,0:T(8,128)(2,1)S(1)}, u32[]{:S(2)}, u32[]{:S(2)}) %collective-permute-start.3) | collective-permute-done | bytes 262176 | tf_op jit(solution)/shard_map/ppermute | solution.py:348
  25.4 6.7 %collective-permute-done.4.refs_2_.refs_14_.refs_8_ = bf16[2,4,64,256]{3,2,1,0:T(8,128)(2,1)S(1)} collective-permute-done((bf16[2,4,64,256]{3,2,1,0:T(8,128)(2,1)}, bf16[2,4,64,256]{3,2,1,0:T(8,128)(2,1)S(1)}, u32[]{:S(2)}, u32[]{:S(2)}) %collective-permute-start.4) | collective-permute-done | bytes 262176 | tf_op jit(solution)/shard_map/ppermute | solution.py:348
  32.0 0.7 copy-done.10
  32.7 1.9 %states.1 = bf16[4,4,64,256]{3,2,1,0:T(8,128)(2,1)} custom-call(bf16[2,4,64,256]{3,2,1,0:T(8,128)(2,1)} %get-tuple-element.42.refs_0_.refs_12_.refs_6_, bf16[2,4,64,256]{3,2,1,0:T(8,128)(2,1)} %copy-done.9, bf16[2,4,64,256]{3,2,1,0:T(8,128)(2,1)} %copy-done.10, bf16[2,4,64,256]{3,2,1,0:T(8,128)(2,1)} %collective-permute-done.5.refs_3_.refs_15_.refs_9_), custom_call_target="tpu_custom_call" | custom-call | tf_op jit(solution)/shard_map/states/pallas_call | solution.py:331
  34.8 1.1 %collective-permute-start = (bf16[128,128]{1,0:T(8,128)(2,1)S(1)}, bf16[128,128]{1,0:T(8,128)(2,1)S(1)}, u32[]{:S(2)}, u32[]{:S(2)}) collective-permute-start(bf16[128,128]{1,0:T(8,128)(2,1)S(1)} %get-tuple-element.36.refs_3_), channel_id=1, source_target_pairs={{0,1},{1,0},{2,3},{3,2},{4,5},{5,4},{6,7},{7,6},{8,9},{9,8},{10,11... | collective-permute-start | bytes 98312 | tf_op jit(solution)/shard_map/ppermute | solution.py:348
  35.9 2.4 %collective-permute-start.1 = (bf16[128,128]{1,0:T(8,128)(2,1)S(1)}, bf16[128,128]{1,0:T(8,128)(2,1)S(1)}, u32[]{:S(2)}, u32[]{:S(2)}) collective-permute-start(bf16[128,128]{1,0:T(8,128)(2,1)S(1)} %get-tuple-element.36.refs_3_), channel_id=1, source_target_pairs={{0,2},{1,3},{2,0},{3,1},{4,6},{5,7},{6,4},{7,5},{8,10},{9,11},{10,... | collective-permute-start | bytes 98312 | tf_op jit(solution)/shard_map/ppermute | solution.py:348
  38.8 2.0 %collective-permute-done.1.refs_5_ = bf16[128,128]{1,0:T(8,128)(2,1)S(1)} collective-permute-done((bf16[128,128]{1,0:T(8,128)(2,1)S(1)}, bf16[128,128]{1,0:T(8,128)(2,1)S(1)}, u32[]{:S(2)}, u32[]{:S(2)}) %collective-permute-start.1) | collective-permute-done | bytes 32800 | tf_op jit(solution)/shard_map/ppermute | solution.py:348
  40.8 1.4 %collective-permute-done.2.refs_6_ = bf16[128,128]{1,0:T(8,128)(2,1)S(1)} collective-permute-done((bf16[128,128]{1,0:T(8,128)(2,1)S(1)}, bf16[128,128]{1,0:T(8,128)(2,1)S(1)}, u32[]{:S(2)}, u32[]{:S(2)}) %collective-permute-start.2) | collective-permute-done | bytes 32800 | tf_op jit(solution)/shard_map/ppermute | solution.py:348
  42.2 0.8 copy-done.11
  43.0 3.4 %scan.1 = (bf16[8,128,128]{2,1,0:T(8,128)(2,1)}, bf16[128,256]{1,0:T(8,128)(2,1)}, f32[128,128]{1,0:T(8,128)}, f32[128,128]{1,0:T(8,128)}) custom-call(s32[128,1]{1,0:T(8,128)S(1)} %reshape.102.refs_1_.refs_0_, bf16[128,256]{1,0:T(8,128)(2,1)S(1)} %get-tuple-element.34.refs_1_, bf16[128,128]{1,0:T(8,128)(2,1)S(1)} %get-tuple-element.35.refs_2_.refs_1_, ...), custom_call_target="tpu_custom_call" | custom-call | tf_op jit(solution)/shard_map/scan/pallas_call | solution.py:331
  46.4 3.6 %all-to-all-start.1 = ((bf16[8,128,128]{2,1,0:T(8,128)(2,1)}), bf16[8,128,128]{2,1,0:T(8,128)(2,1)S(1)}, u32[]{:S(2)}, u32[]{:S(2)}) async-start(bf16[8,128,128]{2,1,0:T(8,128)(2,1)} %get-tuple-element.46), calls=%async_computation.1 | async-start | bytes 524288 | tf_op jit(solution)/shard_map/all_to_all | solution.py:459
  50.0 4.4 %final.1 = (bf16[2,272,256]{2,1,0:T(8,128)(2,1)}, bf16[2,272,256]{2,1,0:T(8,128)(2,1)}, bf16[2,272,256]{2,1,0:T(8,128)(2,1)}, bf16[2,272,256]{2,1,0:T(8,128)(2,1)}) custom-call(s32[128]{0:T(128)S(1)} %reshape.96.refs_0_, bf16[128,128]{1,0:T(8,128)(2,1)S(1)} %get-tuple-element.35.refs_2_.refs_1_, bf16[128,256]{1,0:T(8,128)(2,1)} %get-tuple-element.47.refs_2_, ...), custom_call_target="tpu_custom_call" | custom-call | tf_op jit(solution)/shard_map/final/pallas_call | solution.py:331
  54.4 3.0 %all-to-all-done.1.refs_0_ = bf16[8,128,128]{2,1,0:T(8,128)(2,1)S(1)} async-done(((bf16[8,128,128]{2,1,0:T(8,128)(2,1)}), bf16[8,128,128]{2,1,0:T(8,128)(2,1)S(1)}, u32[]{:S(2)}, u32[]{:S(2)}) %all-to-all-start.1) | async-done | bytes 262176 | tf_op jit(solution)/shard_map/all_to_all | solution.py:459
  58.0 2.0 %collective-permute-start.8 = (bf16[2,272,256]{2,1,0:T(8,128)(2,1)}, bf16[2,272,256]{2,1,0:T(8,128)(2,1)}, u32[]{:S(2)}, u32[]{:S(2)}) collective-permute-start(bf16[2,272,256]{2,1,0:T(8,128)(2,1)} %get-tuple-element.58), channel_id=1, source_target_pairs={{0,128},{32,160},{64,192},{96,224},{128,0},{160,32},{192,64},{224,... | collective-permute-start | bytes 835592 | tf_op jit(solution)/shard_map/ppermute | solution.py:348
  60.0 2.1 %collective-permute-start.9 = (bf16[2,272,256]{2,1,0:T(8,128)(2,1)}, bf16[2,272,256]{2,1,0:T(8,128)(2,1)}, u32[]{:S(2)}, u32[]{:S(2)}) collective-permute-start(bf16[2,272,256]{2,1,0:T(8,128)(2,1)} %get-tuple-element.59), channel_id=1, source_target_pairs={{0,192},{32,224},{64,128},{96,160},{128,64},{160,96},{192,0},{224,... | collective-permute-start | bytes 835592 | tf_op jit(solution)/shard_map/ppermute | solution.py:348
  62.1 1.1 %project.1 = bf16[32,4,1152]{2,1,0:T(4,128)(2,1)} custom-call(bf16[8,128,128]{2,1,0:T(8,128)(2,1)S(1)} %all-to-all-done.1.refs_0_, bf16[512,1024]{1,0:T(8,128)(2,1)S(1)} %copy-done.1), custom_call_target="tpu_custom_call" | custom-call | tf_op jit(solution)/shard_map/project/pallas_call | solution.py:331
  63.2 12.3 %all-to-all-start.2 = ((bf16[32,4,1152]{2,1,0:T(4,128)(2,1)}), bf16[32,4,1152]{2,1,0:T(4,128)(2,1)S(1)}, u32[]{:S(2)}, u32[]{:S(2)}) async-start(bf16[32,4,1152]{2,1,0:T(4,128)(2,1)} %project.1), calls=%async_computation.2 | async-start | bytes 589824 | tf_op jit(solution)/shard_map/all_to_all | solution.py:481
  75.5 2.0 %finals.1 = bf16[4,272,256]{2,1,0:T(8,128)(2,1)} custom-call(bf16[2,272,256]{2,1,0:T(8,128)(2,1)} %get-tuple-element.56.refs_0_, bf16[2,272,256]{2,1,0:T(8,128)(2,1)} %collective-permute-done.7.refs_1_, bf16[2,272,256]{2,1,0:T(8,128)(2,1)} %collective-permute-done.8.refs_2_, bf16[2,272,256]{2,1,0:T(8,128)(2,1)} %collective-permute-done.9.refs_3_), custom_call_target="tpu_custom_call" | custom-call | tf_op jit(solution)/shard_map/finals/pallas_call | solution.py:331
  77.5 0.8 constant_dynamic-slice_fusion
  79.7 0.8 copy-done.12
  80.5 2.9 %unpack.1 = (bf16[2,2,8,64,256]{4,3,2,1,0:T(8,128)(2,1)}, bf16[2,2,3,8,64]{4,3,2,1,0:T(8,128)(2,1)}) custom-call(bf16[2,272,256]{2,1,0:T(8,128)(2,1)} %get-tuple-element.56.refs_0_, bf16[2,272,256]{2,1,0:T(8,128)(2,1)} %collective-permute-done.7.refs_1_, bf16[2,272,256]{2,1,0:T(8,128)(2,1)} %collective-permute-done.8.refs_2_, ...), custom_call_target="tpu_custom_call" | custom-call | tf_op jit(solution)/shard_map/unpack/pallas_call | solution.py:331
  83.5 3.7 %all-to-all-done.2.refs_0_ = bf16[32,4,1152]{2,1,0:T(4,128)(2,1)S(1)} async-done(((bf16[32,4,1152]{2,1,0:T(4,128)(2,1)}), bf16[32,4,1152]{2,1,0:T(4,128)(2,1)S(1)}, u32[]{:S(2)}, u32[]{:S(2)}) %all-to-all-start.2) | async-done | bytes 294944 | tf_op jit(solution)/shard_map/all_to_all | solution.py:481
  87.2 0.8 norm.1
  (77 shorter events, 5.6 us)
Async XLA Ops:
  0.6 1.8 %copy-start = (bf16[1024,2,512]{2,1,0:T(2,128)(2,1)S(1)}, bf16[1024,2,512]{2,1,0:T(2,128)(2,1)}, u32[]{:S(2)}) copy-start(bf16[1024,2,512]{2,1,0:T(2,128)(2,1)} %param.16) | copy-start | bytes 6291460
  0.6 1.6 %copy-start.15 = (bf16[1024,8]{0,1:T(8,128)(2,1)S(1)}, bf16[1024,8]{0,1:T(8,128)(2,1)}, u32[]{:S(2)}) copy-start(bf16[1024,8]{0,1:T(8,128)(2,1)} %param.18) | copy-start | bytes 49156
  0.7 1.8 %copy-start.14 = (bf16[2,2,8,64,3]{3,2,4,1,0:T(8,128)(2,1)S(1)}, bf16[2,2,8,64,3]{3,2,4,1,0:T(8,128)(2,1)}, u32[]{:S(2)}) copy-start(bf16[2,2,8,64,3]{3,2,4,1,0:T(8,128)(2,1)} %param.27) | copy-start | bytes 36868
  2.9 1.0 %copy-start.13 = (bf16[1024,2,64]{0,2,1:T(8,128)(2,1)S(1)}, bf16[1024,2,64]{0,2,1:T(8,128)(2,1)}, u32[]{:S(2)}) copy-start(bf16[1024,2,64]{0,2,1:T(8,128)(2,1)} %param.17) | copy-start | bytes 786436
  5.3 11.5 %copy-start.16 = (s32[4,2,16]{2,1,0:T(2,128)S(1)}, s32[4,2,16]{2,1,0:T(2,128)}, u32[]{:S(2)}) copy-start(s32[4,2,16]{2,1,0:T(2,128)} %param.29) | copy-start | bytes 1540
  5.3 11.8 %copy-start.18 = (bf16[4,2,64]{2,1,0:T(2,128)(2,1)S(1)}, bf16[4,2,64]{2,1,0:T(2,128)(2,1)}, u32[]{:S(2)}) copy-start(bf16[4,2,64]{2,1,0:T(2,128)(2,1)} %param.20) | copy-start | bytes 3076
  5.3 16.8 %copy-start.3 = (bf16[4,512]{1,0:T(4,128)(2,1)S(1)}, bf16[4,512]{1,0:T(4,128)(2,1)}, u32[]{:S(2)}) copy-start(bf16[4,512]{1,0:T(4,128)(2,1)} %refs_2_.1) | copy-start | bytes 12292
  5.3 16.0 %all-to-all-start = ((bf16[8,144,256]{2,1,0:T(8,128)(2,1)}), bf16[8,144,256]{2,1,0:T(8,128)(2,1)S(1)}, u32[]{:S(2)}, u32[]{:S(2)}) async-start(bf16[8,144,256]{2,1,0:T(8,128)(2,1)} %maximum_maximum_fusion), calls=%async_computation | async-start | bytes 1179648 | tf_op jit(solution)/shard_map/all_to_all | solution.py:403
  11.9 13.4 %collective-permute-start.3 = (bf16[2,4,64,256]{3,2,1,0:T(8,128)(2,1)}, bf16[2,4,64,256]{3,2,1,0:T(8,128)(2,1)S(1)}, u32[]{:S(2)}, u32[]{:S(2)}) collective-permute-start(bf16[2,4,64,256]{3,2,1,0:T(8,128)(2,1)} %get-tuple-element.39), channel_id=1, source_target_pairs={{0,64},{32,96},{64,0},{96,32},{128,192},{160,224},{192,128},{224,1... | collective-permute-start | bytes 786440 | tf_op jit(solution)/shard_map/ppermute | solution.py:348
  14.0 18.0 %collective-permute-start.4 = (bf16[2,4,64,256]{3,2,1,0:T(8,128)(2,1)}, bf16[2,4,64,256]{3,2,1,0:T(8,128)(2,1)S(1)}, u32[]{:S(2)}, u32[]{:S(2)}) collective-permute-start(bf16[2,4,64,256]{3,2,1,0:T(8,128)(2,1)} %get-tuple-element.40), channel_id=1, source_target_pairs={{0,128},{32,160},{64,192},{96,224},{128,0},{160,32},{192,64},{224,... | collective-permute-start | bytes 786440 | tf_op jit(solution)/shard_map/ppermute | solution.py:348
  16.7 15.3 %collective-permute-start.5 = (bf16[2,4,64,256]{3,2,1,0:T(8,128)(2,1)}, bf16[2,4,64,256]{3,2,1,0:T(8,128)(2,1)}, u32[]{:S(2)}, u32[]{:S(2)}) collective-permute-start(bf16[2,4,64,256]{3,2,1,0:T(8,128)(2,1)} %get-tuple-element.41), channel_id=1, source_target_pairs={{0,192},{32,224},{64,128},{96,160},{128,64},{160,96},{192,0},{224,... | collective-permute-start | bytes 786440 | tf_op jit(solution)/shard_map/ppermute | solution.py:348
  16.9 26.1 %copy-start.4 = (f32[512]{0:T(512)S(1)}, f32[512]{0:T(512)}, u32[]{:S(2)}) copy-start(f32[512]{0:T(512)} %param.24) | copy-start | bytes 6148
  16.9 26.1 %copy-start.5 = (f32[8]{0:T(128)S(1)}, f32[8]{0:T(128)}, u32[]{:S(2)}) copy-start(f32[8]{0:T(128)} %param.22) | copy-start | bytes 100
  16.9 26.1 %copy-start.6 = (f32[8]{0:T(128)S(1)}, f32[8]{0:T(128)}, u32[]{:S(2)}) copy-start(f32[8]{0:T(128)} %param.21) | copy-start | bytes 100
  16.9 26.1 %copy-start.7 = (f32[8]{0:T(128)S(1)}, f32[8]{0:T(128)}, u32[]{:S(2)}) copy-start(f32[8]{0:T(128)} %param.23) | copy-start | bytes 100
  21.2 0.8 copy-start.8
  24.1 22.3 %copy-start.2 = (bf16[3,32,256]{2,1,0:T(8,128)(2,1)}, bf16[3,32,256]{2,1,0:T(8,128)(2,1)S(1)}, u32[]{:S(2)}) copy-start(bf16[3,32,256]{2,1,0:T(8,128)(2,1)S(1)} %get-tuple-element.50.refs_5_) | copy-start | bytes 147460
  25.4 6.7 %copy-start.9 = (bf16[2,4,64,256]{3,2,1,0:T(8,128)(2,1)}, bf16[2,4,64,256]{3,2,1,0:T(8,128)(2,1)S(1)}, u32[]{:S(2)}) copy-start(bf16[2,4,64,256]{3,2,1,0:T(8,128)(2,1)S(1)} %collective-permute-done.3.refs_1_.refs_13_.refs_7_) | copy-start | bytes 786436
  32.0 0.7 copy-start.10
  34.7 7.5 %collective-permute-start.6 = (bf16[4,4,64,256]{3,2,1,0:T(8,128)(2,1)}, bf16[4,4,64,256]{3,2,1,0:T(8,128)(2,1)S(1)}, u32[]{:S(2)}, u32[]{:S(2)}) collective-permute-start(bf16[4,4,64,256]{3,2,1,0:T(8,128)(2,1)} %states.1), channel_id=1, source_target_pairs={{0,32},{32,0},{64,96},{96,64},{128,160},{160,128},{192,224},{224,1... | collective-permute-start | bytes 1572872 | tf_op jit(solution)/shard_map/ppermute | solution.py:348
  34.8 4.0 %collective-permute-start = (bf16[128,128]{1,0:T(8,128)(2,1)S(1)}, bf16[128,128]{1,0:T(8,128)(2,1)S(1)}, u32[]{:S(2)}, u32[]{:S(2)}) collective-permute-start(bf16[128,128]{1,0:T(8,128)(2,1)S(1)} %get-tuple-element.36.refs_3_), channel_id=1, source_target_pairs={{0,1},{1,0},{2,3},{3,2},{4,5},{5,4},{6,7},{7,6},{8,9},{9,8},{10,11... | collective-permute-start | bytes 98312 | tf_op jit(solution)/shard_map/ppermute | solution.py:348
  35.9 4.9 %collective-permute-start.1 = (bf16[128,128]{1,0:T(8,128)(2,1)S(1)}, bf16[128,128]{1,0:T(8,128)(2,1)S(1)}, u32[]{:S(2)}, u32[]{:S(2)}) collective-permute-start(bf16[128,128]{1,0:T(8,128)(2,1)S(1)} %get-tuple-element.36.refs_3_), channel_id=1, source_target_pairs={{0,2},{1,3},{2,0},{3,1},{4,6},{5,7},{6,4},{7,5},{8,10},{9,11},{10,... | collective-permute-start | bytes 98312 | tf_op jit(solution)/shard_map/ppermute | solution.py:348
  38.2 3.9 %collective-permute-start.2 = (bf16[128,128]{1,0:T(8,128)(2,1)S(1)}, bf16[128,128]{1,0:T(8,128)(2,1)S(1)}, u32[]{:S(2)}, u32[]{:S(2)}) collective-permute-start(bf16[128,128]{1,0:T(8,128)(2,1)S(1)} %get-tuple-element.36.refs_3_), channel_id=1, source_target_pairs={{0,3},{1,2},{2,1},{3,0},{4,7},{5,6},{6,5},{7,4},{8,11},{9,10},{10,... | collective-permute-start | bytes 98312 | tf_op jit(solution)/shard_map/ppermute | solution.py:348
  42.2 0.8 copy-start.11
  46.4 15.7 %copy-start.1 = (bf16[512,1024]{1,0:T(8,128)(2,1)S(1)}, bf16[512,1024]{1,0:T(8,128)(2,1)}, u32[]{:S(2)}) copy-start(bf16[512,1024]{1,0:T(8,128)(2,1)} %refs_1_.1) | copy-start | bytes 3145732
  46.4 11.0 %all-to-all-start.1 = ((bf16[8,128,128]{2,1,0:T(8,128)(2,1)}), bf16[8,128,128]{2,1,0:T(8,128)(2,1)S(1)}, u32[]{:S(2)}, u32[]{:S(2)}) async-start(bf16[8,128,128]{2,1,0:T(8,128)(2,1)} %get-tuple-element.46), calls=%async_computation.1 | async-start | bytes 524288 | tf_op jit(solution)/shard_map/all_to_all | solution.py:459
  57.4 18.0 %collective-permute-start.7 = (bf16[2,272,256]{2,1,0:T(8,128)(2,1)}, bf16[2,272,256]{2,1,0:T(8,128)(2,1)}, u32[]{:S(2)}, u32[]{:S(2)}) collective-permute-start(bf16[2,272,256]{2,1,0:T(8,128)(2,1)} %get-tuple-element.57), channel_id=1, source_target_pairs={{0,64},{32,96},{64,0},{96,32},{128,192},{160,224},{192,128},{224,1... | collective-permute-start | bytes 835592 | tf_op jit(solution)/shard_map/ppermute | solution.py:348
  58.0 17.5 %collective-permute-start.8 = (bf16[2,272,256]{2,1,0:T(8,128)(2,1)}, bf16[2,272,256]{2,1,0:T(8,128)(2,1)}, u32[]{:S(2)}, u32[]{:S(2)}) collective-permute-start(bf16[2,272,256]{2,1,0:T(8,128)(2,1)} %get-tuple-element.58), channel_id=1, source_target_pairs={{0,128},{32,160},{64,192},{96,224},{128,0},{160,32},{192,64},{224,... | collective-permute-start | bytes 835592 | tf_op jit(solution)/shard_map/ppermute | solution.py:348
  60.0 15.4 %collective-permute-start.9 = (bf16[2,272,256]{2,1,0:T(8,128)(2,1)}, bf16[2,272,256]{2,1,0:T(8,128)(2,1)}, u32[]{:S(2)}, u32[]{:S(2)}) collective-permute-start(bf16[2,272,256]{2,1,0:T(8,128)(2,1)} %get-tuple-element.59), channel_id=1, source_target_pairs={{0,192},{32,224},{64,128},{96,160},{128,64},{160,96},{192,0},{224,... | collective-permute-start | bytes 835592 | tf_op jit(solution)/shard_map/ppermute | solution.py:348
  63.2 24.0 %all-to-all-start.2 = ((bf16[32,4,1152]{2,1,0:T(4,128)(2,1)}), bf16[32,4,1152]{2,1,0:T(4,128)(2,1)S(1)}, u32[]{:S(2)}, u32[]{:S(2)}) async-start(bf16[32,4,1152]{2,1,0:T(4,128)(2,1)} %project.1), calls=%async_computation.2 | async-start | bytes 589824 | tf_op jit(solution)/shard_map/all_to_all | solution.py:481
  77.4 2.3 %collective-permute-start.10 = (bf16[4,272,256]{2,1,0:T(8,128)(2,1)}, bf16[4,272,256]{2,1,0:T(8,128)(2,1)S(1)}, u32[]{:S(2)}, u32[]{:S(2)}) collective-permute-start(bf16[4,272,256]{2,1,0:T(8,128)(2,1)} %finals.1), channel_id=1, source_target_pairs={{0,32},{32,0},{64,96},{96,64},{128,160},{160,128},{192,224},{224,1... | collective-permute-start | bytes 1671176 | tf_op jit(solution)/shard_map/ppermute | solution.py:348
  79.7 0.8 copy-start.12
  (1 other events, 0.7 us)

commit v6 on v5

--- a/solution.py
+++ b/solution.py
@@ -419,14 +419,15 @@
     new, conv, bc_conv, dt_raw, fin = call(
         conv_kernel,
         "conv",
-        [FAR, VM, VM, VM],
+        [VM, VM, VM, VM],
         [((ROWS, 256), BF16), ((ROWS, 128), BF16), ((ROWS, 128), BF16), ((1, ROWS), F32), ((3, BEAMS, 256), BF16)],
         [pltpu.VMEM((3, BEAMS, 256), F32)],
     )(recv, parent_column, conv_x_w, conv_bc_w.reshape(4, 128))
 
-    _, *halves = lax.optimization_barrier((bc_conv, *halves))
+    others = [swap(bc_conv, "row", 32, k) for k in (1, 2, 3)]
+    gated = lax.optimization_barrier((*others, *halves))
+    others, halves = list(gated[:3]), list(gated[3:])
     states = cores(halves, "states")
-    others = [swap(bc_conv, "row", 32, k) for k in (1, 2, 3)]
 
     send, b_in, coef, first = call(
         scan_kernel,

time: 89.3 us -> 82.5 us (0.924)
  waiting for transfers between devices: 22.8 us -> 18.4 us
  Pallas kernels: 20.6 us -> 19.5 us
    ppermute x11, waiting for transfers between devices: 12.1 us -> 7.99 us  [swap(): return lax.ppermute(value, axis, [(i, i ^ mask) for i in range(count)])]
    ppermute x11, starting transfers between devices: 13.7 us -> 14.8 us  [swap(): return lax.ppermute(value, axis, [(i, i ^ mask) for i in range(count)])]
    pallas_call x9, Pallas kernels: 20.6 us -> 19.5 us  [build(): pl.pallas_call(body, name=name, in_specs=list(specs), out_specs=tuple(out...]
    all_to_all x1, starting transfers between devices: 12.3 us -> 11.4 us  [local(): lax.all_to_all(parts, 'row', split_axis=0, concat_axis=0, tiled=True)]
    unnamed x39 -> x37, local copies, waits for them, and re-layouts: 3.48 us -> 2.6 us
  transfers between devices with their start and end apart: 14 -> 14, of which waited for: 9 -> 7; matrix products, arithmetic and copies ran while one was open for 2% -> 2% of each run, Pallas kernels for 17% -> 16%
where the time goes in v6:
time: 82.5 us; the launch traced here: 81.8 us
  starting transfers between devices  34.2 us (41%)
  Pallas kernels  19.5 us (24%)
  waiting for transfers between devices  18.4 us (22%)
  local copies, waits for them, and re-layouts  6.87 us (8%)
  between operations  1 us (1%)
  other arithmetic  0.98 us (1%)
  matrix products  0.85 us (1%)
    pallas_call x9, Pallas kernels, build(): pl.pallas_call(body, name=name, in_specs=list(specs), out_specs=tuple(out...  19.5 us
    ppermute x11, starting transfers between devices, swap(): return lax.ppermute(value, axis, [(i, i ^ mask) for i in range(count)])  14.8 us
    all_to_all x1, starting transfers between devices, local(): lax.all_to_all(parts, 'row', split_axis=0, concat_axis=0, tiled=True)  11.4 us
    ppermute x11, waiting for transfers between devices, swap(): return lax.ppermute(value, axis, [(i, i ^ mask) for i in range(count)])  7.99 us
    all_to_all x1, starting transfers between devices, local(): lax.all_to_all(payload, 'beam', split_axis=0, concat_axis=0, tiled=True)  4.43 us
    all_to_all x1, waiting for transfers between devices, local(): lax.all_to_all(payload, 'beam', split_axis=0, concat_axis=0, tiled=True)  4.04 us
    all_to_all x1, starting transfers between devices, local(): lax.all_to_all(send, 'beam', split_axis=0, concat_axis=0, tiled=True)  3.55 us
    all_to_all x1, waiting for transfers between devices, local(): lax.all_to_all(parts, 'row', split_axis=0, concat_axis=0, tiled=True)  3.33 us
  transfers between devices with their start and end apart: 14, of which 7 were waited for; matrix products, arithmetic and copies ran while one was open for 2% of the time, Pallas kernels for 16%

profile of v6, /device:TPU:32, one launch (start us, length us, event | category | flops | bytes accessed | tf_op | source)
XLA Modules:
  0.0 81.8 jit_solution(1545510549852000743)
XLA Ops:
  0.7 1.2 %reshape.86 = bf16[4,8,4,1024]{3,2,1,0:T(4,128)(2,1)S(1)} reshape(bf16[4,2,16,1024]{3,2,1,0:T(8,128)(2,1)} %param.15) | data formatting | bytes 524288 | tf_op jit(solution)/shard_map/reshape | solution.py:389
  4.3 1.0 %maximum_maximum_fusion = bf16[8,144,256]{2,1,0:T(8,128)(2,1)} fusion(bf16[8,1,128]{2,1,0:T(2,128)(2,1)S(1)} %copy.54, bf16[8,1,128]{2,1,0:T(2,128)(2,1)S(1)} %copy.53, bf16[8,12,64]{2,1,0:T(8,128)(2,1)S(1)} %copy.52, bf16[8,128,128]{2,1,0:T(8,128)(2,1)S(1)} %copy.49, bf16[144]{0:T(256)(128)(2,1)S(1)} %pad.7.clone, bf16[144,256]{1,0:T(8,128)(2,1)S(1)} %pad.4.clone, ...), kind=kLoop, calls=%fused_computation.3 | loop fusion | flops 4718592 | bytes 1089824 | tf_op jit(solution)/shard_map/concatenate | solution.py:402
  5.3 4.4 %all-to-all-start = ((bf16[8,144,256]{2,1,0:T(8,128)(2,1)}), bf16[8,144,256]{2,1,0:T(8,128)(2,1)S(1)}, u32[]{:S(2)}, u32[]{:S(2)}) async-start(bf16[8,144,256]{2,1,0:T(8,128)(2,1)} %maximum_maximum_fusion), calls=%async_computation | async-start | bytes 1179648 | tf_op jit(solution)/shard_map/all_to_all | solution.py:403
  9.7 2.2 %pack.1 = (bf16[2,4,64,256]{3,2,1,0:T(8,128)(2,1)}, bf16[2,4,64,256]{3,2,1,0:T(8,128)(2,1)}, bf16[2,4,64,256]{3,2,1,0:T(8,128)(2,1)}, bf16[2,4,64,256]{3,2,1,0:T(8,128)(2,1)}) custom-call(bf16[2,2,8,64,256]{4,3,2,1,0:T(8,128)(2,1)} %refs_0_.1), custom_call_target="tpu_custom_call" | custom-call | tf_op jit(solution)/shard_map/pack/pallas_call | solution.py:331
  11.9 2.1 %collective-permute-start.3 = (bf16[2,4,64,256]{3,2,1,0:T(8,128)(2,1)}, bf16[2,4,64,256]{3,2,1,0:T(8,128)(2,1)S(1)}, u32[]{:S(2)}, u32[]{:S(2)}) collective-permute-start(bf16[2,4,64,256]{3,2,1,0:T(8,128)(2,1)} %get-tuple-element.41), channel_id=1, source_target_pairs={{0,64},{32,96},{64,0},{96,32},{128,192},{160,224},{192,128},{224,1... | collective-permute-start | bytes 786440 | tf_op jit(solution)/shard_map/ppermute | solution.py:348
  14.0 2.7 %collective-permute-start.4 = (bf16[2,4,64,256]{3,2,1,0:T(8,128)(2,1)}, bf16[2,4,64,256]{3,2,1,0:T(8,128)(2,1)S(1)}, u32[]{:S(2)}, u32[]{:S(2)}) collective-permute-start(bf16[2,4,64,256]{3,2,1,0:T(8,128)(2,1)} %get-tuple-element.42), channel_id=1, source_target_pairs={{0,128},{32,160},{64,192},{96,224},{128,0},{160,32},{192,64},{224,... | collective-permute-start | bytes 786440 | tf_op jit(solution)/shard_map/ppermute | solution.py:348
  17.2 4.0 %all-to-all-done.refs_0_ = bf16[8,144,256]{2,1,0:T(8,128)(2,1)S(1)} async-done(((bf16[8,144,256]{2,1,0:T(8,128)(2,1)}), bf16[8,144,256]{2,1,0:T(8,128)(2,1)S(1)}, u32[]{:S(2)}, u32[]{:S(2)}) %all-to-all-start) | async-done | bytes 589856 | tf_op jit(solution)/shard_map/all_to_all | solution.py:403
  21.3 0.9 %conv.1 = (bf16[128,256]{1,0:T(8,128)(2,1)S(1)}, bf16[128,128]{1,0:T(8,128)(2,1)S(1)}, bf16[128,128]{1,0:T(8,128)(2,1)S(1)}, f32[1,128]{1,0:T(1,128)S(1)}, bf16[3,32,256]{2,1,0:T(8,128)(2,1)S(1)}) custom-call(bf16[8,144,256]{2,1,0:T(8,128)(2,1)S(1)} %all-to-all-done.refs_0_, s32[128,1]{1,0:T(8,128)S(1)} %reshape.102.refs_1_.refs_0_, ...), custom_call_target="tpu_custom_call" | custom-call | tf_op jit(solution)/shard_map/conv/pallas_call | solution.py:331
  22.2 1.1 %collective-permute-start = (bf16[128,128]{1,0:T(8,128)(2,1)S(1)}, bf16[128,128]{1,0:T(8,128)(2,1)S(1)}, u32[]{:S(2)}, u32[]{:S(2)}) collective-permute-start(bf16[128,128]{1,0:T(8,128)(2,1)S(1)} %get-tuple-element.39.refs_3_), channel_id=1, source_target_pairs={{0,1},{1,0},{2,3},{3,2},{4,5},{5,4},{6,7},{7,6},{8,9},{9,8},{10,11... | collective-permute-start | bytes 98312 | tf_op jit(solution)/shard_map/ppermute | solution.py:348
  23.3 2.4 %collective-permute-start.1 = (bf16[128,128]{1,0:T(8,128)(2,1)S(1)}, bf16[128,128]{1,0:T(8,128)(2,1)S(1)}, u32[]{:S(2)}, u32[]{:S(2)}) collective-permute-start(bf16[128,128]{1,0:T(8,128)(2,1)S(1)} %get-tuple-element.39.refs_3_), channel_id=1, source_target_pairs={{0,2},{1,3},{2,0},{3,1},{4,6},{5,7},{6,4},{7,5},{8,10},{9,11},{10,... | collective-permute-start | bytes 98312 | tf_op jit(solution)/shard_map/ppermute | solution.py:348
  25.7 1.6 %collective-permute-start.2 = (bf16[128,128]{1,0:T(8,128)(2,1)S(1)}, bf16[128,128]{1,0:T(8,128)(2,1)S(1)}, u32[]{:S(2)}, u32[]{:S(2)}) collective-permute-start(bf16[128,128]{1,0:T(8,128)(2,1)S(1)} %get-tuple-element.39.refs_3_), channel_id=1, source_target_pairs={{0,3},{1,2},{2,1},{3,0},{4,7},{5,6},{6,5},{7,4},{8,11},{9,10},{10,... | collective-permute-start | bytes 98312 | tf_op jit(solution)/shard_map/ppermute | solution.py:348
  27.3 4.7 %collective-permute-done.4.refs_2_.refs_14_.refs_8_ = bf16[2,4,64,256]{3,2,1,0:T(8,128)(2,1)S(1)} collective-permute-done((bf16[2,4,64,256]{3,2,1,0:T(8,128)(2,1)}, bf16[2,4,64,256]{3,2,1,0:T(8,128)(2,1)S(1)}, u32[]{:S(2)}, u32[]{:S(2)}) %collective-permute-start.4) | collective-permute-done | bytes 262176 | tf_op jit(solution)/shard_map/ppermute | solution.py:348
  32.1 0.7 copy-done.9
  32.7 1.9 %states.1 = bf16[4,4,64,256]{3,2,1,0:T(8,128)(2,1)} custom-call(bf16[2,4,64,256]{3,2,1,0:T(8,128)(2,1)} %get-tuple-element.48.refs_0_.refs_12_.refs_6_, bf16[2,4,64,256]{3,2,1,0:T(8,128)(2,1)} %copy-done.8, bf16[2,4,64,256]{3,2,1,0:T(8,128)(2,1)} %copy-done.9, bf16[2,4,64,256]{3,2,1,0:T(8,128)(2,1)} %collective-permute-done.5.refs_3_.refs_15_.refs_9_), custom_call_target="tpu_custom_call" | custom-call | tf_op jit(solution)/shard_map/states/pallas_call | solution.py:331
  34.8 2.1 %collective-permute-done.6.refs_16_.refs_10_ = bf16[4,4,64,256]{3,2,1,0:T(8,128)(2,1)S(1)} collective-permute-done((bf16[4,4,64,256]{3,2,1,0:T(8,128)(2,1)}, bf16[4,4,64,256]{3,2,1,0:T(8,128)(2,1)S(1)}, u32[]{:S(2)}, u32[]{:S(2)}) %collective-permute-start.6) | collective-permute-done | bytes 524320 | tf_op jit(solution)/shard_map/ppermute | solution.py:348
  36.9 0.8 copy-done.10
  37.7 3.4 %scan.1 = (bf16[8,128,128]{2,1,0:T(8,128)(2,1)}, bf16[128,256]{1,0:T(8,128)(2,1)}, f32[128,128]{1,0:T(8,128)}, f32[128,128]{1,0:T(8,128)}) custom-call(s32[128,1]{1,0:T(8,128)S(1)} %reshape.102.refs_1_.refs_0_, bf16[128,256]{1,0:T(8,128)(2,1)S(1)} %get-tuple-element.37.refs_1_, bf16[128,128]{1,0:T(8,128)(2,1)S(1)} %get-tuple-element.38.refs_2_.refs_1_, ...), custom_call_target="tpu_custom_call" | custom-call | tf_op jit(solution)/shard_map/scan/pallas_call | solution.py:331
  41.1 3.6 %all-to-all-start.1 = ((bf16[8,128,128]{2,1,0:T(8,128)(2,1)}), bf16[8,128,128]{2,1,0:T(8,128)(2,1)S(1)}, u32[]{:S(2)}, u32[]{:S(2)}) async-start(bf16[8,128,128]{2,1,0:T(8,128)(2,1)} %get-tuple-element.52), calls=%async_computation.1 | async-start | bytes 524288 | tf_op jit(solution)/shard_map/all_to_all | solution.py:460
  44.7 4.4 %final.1 = (bf16[2,272,256]{2,1,0:T(8,128)(2,1)}, bf16[2,272,256]{2,1,0:T(8,128)(2,1)}, bf16[2,272,256]{2,1,0:T(8,128)(2,1)}, bf16[2,272,256]{2,1,0:T(8,128)(2,1)}) custom-call(s32[128]{0:T(128)S(1)} %reshape.96.refs_0_, bf16[128,128]{1,0:T(8,128)(2,1)S(1)} %get-tuple-element.38.refs_2_.refs_1_, bf16[128,256]{1,0:T(8,128)(2,1)} %get-tuple-element.53.refs_2_, ...), custom_call_target="tpu_custom_call" | custom-call | tf_op jit(solution)/shard_map/final/pallas_call | solution.py:331
  49.1 3.0 %all-to-all-done.1.refs_0_ = bf16[8,128,128]{2,1,0:T(8,128)(2,1)S(1)} async-done(((bf16[8,128,128]{2,1,0:T(8,128)(2,1)}), bf16[8,128,128]{2,1,0:T(8,128)(2,1)S(1)}, u32[]{:S(2)}, u32[]{:S(2)}) %all-to-all-start.1) | async-done | bytes 262176 | tf_op jit(solution)/shard_map/all_to_all | solution.py:460
  52.7 2.0 %collective-permute-start.8 = (bf16[2,272,256]{2,1,0:T(8,128)(2,1)}, bf16[2,272,256]{2,1,0:T(8,128)(2,1)}, u32[]{:S(2)}, u32[]{:S(2)}) collective-permute-start(bf16[2,272,256]{2,1,0:T(8,128)(2,1)} %get-tuple-element.64), channel_id=1, source_target_pairs={{0,128},{32,160},{64,192},{96,224},{128,0},{160,32},{192,64},{224,... | collective-permute-start | bytes 835592 | tf_op jit(solution)/shard_map/ppermute | solution.py:348
  54.7 2.1 %collective-permute-start.9 = (bf16[2,272,256]{2,1,0:T(8,128)(2,1)}, bf16[2,272,256]{2,1,0:T(8,128)(2,1)}, u32[]{:S(2)}, u32[]{:S(2)}) collective-permute-start(bf16[2,272,256]{2,1,0:T(8,128)(2,1)} %get-tuple-element.65), channel_id=1, source_target_pairs={{0,192},{32,224},{64,128},{96,160},{128,64},{160,96},{192,0},{224,... | collective-permute-start | bytes 835592 | tf_op jit(solution)/shard_map/ppermute | solution.py:348
  56.8 1.1 %project.1 = bf16[32,4,1152]{2,1,0:T(4,128)(2,1)} custom-call(bf16[8,128,128]{2,1,0:T(8,128)(2,1)S(1)} %all-to-all-done.1.refs_0_, bf16[512,1024]{1,0:T(8,128)(2,1)S(1)} %copy-done.1), custom_call_target="tpu_custom_call" | custom-call | tf_op jit(solution)/shard_map/project/pallas_call | solution.py:331
  57.9 11.4 %all-to-all-start.2 = ((bf16[32,4,1152]{2,1,0:T(4,128)(2,1)}), bf16[32,4,1152]{2,1,0:T(4,128)(2,1)S(1)}, u32[]{:S(2)}, u32[]{:S(2)}) async-start(bf16[32,4,1152]{2,1,0:T(4,128)(2,1)} %project.1), calls=%async_computation.2 | async-start | bytes 589824 | tf_op jit(solution)/shard_map/all_to_all | solution.py:482
  69.7 2.0 %finals.1 = bf16[4,272,256]{2,1,0:T(8,128)(2,1)} custom-call(bf16[2,272,256]{2,1,0:T(8,128)(2,1)} %get-tuple-element.62.refs_0_, bf16[2,272,256]{2,1,0:T(8,128)(2,1)} %collective-permute-done.7.refs_1_, bf16[2,272,256]{2,1,0:T(8,128)(2,1)} %collective-permute-done.8.refs_2_, bf16[2,272,256]{2,1,0:T(8,128)(2,1)} %collective-permute-done.9.refs_3_), custom_call_target="tpu_custom_call" | custom-call | tf_op jit(solution)/shard_map/finals/pallas_call | solution.py:331
  71.8 0.8 constant_dynamic-slice_fusion
  72.6 0.6 copy.63
  73.2 0.7 collective-permute-done.10.refs_4_
  73.9 0.8 copy-done.11
  74.7 2.9 %unpack.1 = (bf16[2,2,8,64,256]{4,3,2,1,0:T(8,128)(2,1)}, bf16[2,2,3,8,64]{4,3,2,1,0:T(8,128)(2,1)}) custom-call(bf16[2,272,256]{2,1,0:T(8,128)(2,1)} %get-tuple-element.62.refs_0_, bf16[2,272,256]{2,1,0:T(8,128)(2,1)} %collective-permute-done.7.refs_1_, bf16[2,272,256]{2,1,0:T(8,128)(2,1)} %collective-permute-done.8.refs_2_, ...), custom_call_target="tpu_custom_call" | custom-call | tf_op jit(solution)/shard_map/unpack/pallas_call | solution.py:331
  77.7 3.3 %all-to-all-done.2.refs_0_ = bf16[32,4,1152]{2,1,0:T(4,128)(2,1)S(1)} async-done(((bf16[32,4,1152]{2,1,0:T(4,128)(2,1)}), bf16[32,4,1152]{2,1,0:T(4,128)(2,1)S(1)}, u32[]{:S(2)}, u32[]{:S(2)}) %all-to-all-start.2) | async-done | bytes 294944 | tf_op jit(solution)/shard_map/all_to_all | solution.py:482
  81.0 0.8 norm.1
  (75 shorter events, 4.2 us)
Async XLA Ops:
  0.6 1.8 %copy-start = (bf16[1024,2,512]{2,1,0:T(2,128)(2,1)S(1)}, bf16[1024,2,512]{2,1,0:T(2,128)(2,1)}, u32[]{:S(2)}) copy-start(bf16[1024,2,512]{2,1,0:T(2,128)(2,1)} %param.16) | copy-start | bytes 6291460
  0.6 1.6 %copy-start.14 = (bf16[1024,8]{0,1:T(8,128)(2,1)S(1)}, bf16[1024,8]{0,1:T(8,128)(2,1)}, u32[]{:S(2)}) copy-start(bf16[1024,8]{0,1:T(8,128)(2,1)} %param.18) | copy-start | bytes 49156
  0.7 1.8 %copy-start.13 = (bf16[2,2,8,64,3]{3,2,4,1,0:T(8,128)(2,1)S(1)}, bf16[2,2,8,64,3]{3,2,4,1,0:T(8,128)(2,1)}, u32[]{:S(2)}) copy-start(bf16[2,2,8,64,3]{3,2,4,1,0:T(8,128)(2,1)} %param.27) | copy-start | bytes 36868
  2.9 0.7 copy-start.16
  2.9 1.0 %copy-start.12 = (bf16[1024,2,64]{0,2,1:T(8,128)(2,1)S(1)}, bf16[1024,2,64]{0,2,1:T(8,128)(2,1)}, u32[]{:S(2)}) copy-start(bf16[1024,2,64]{0,2,1:T(8,128)(2,1)} %param.17) | copy-start | bytes 786436
  5.3 11.5 %copy-start.15 = (s32[4,2,16]{2,1,0:T(2,128)S(1)}, s32[4,2,16]{2,1,0:T(2,128)}, u32[]{:S(2)}) copy-start(s32[4,2,16]{2,1,0:T(2,128)} %param.29) | copy-start | bytes 1540
  5.3 11.8 %copy-start.17 = (bf16[4,2,64]{2,1,0:T(2,128)(2,1)S(1)}, bf16[4,2,64]{2,1,0:T(2,128)(2,1)}, u32[]{:S(2)}) copy-start(bf16[4,2,64]{2,1,0:T(2,128)(2,1)} %param.20) | copy-start | bytes 3076
  5.3 16.0 %copy-start.3 = (bf16[4,512]{1,0:T(4,128)(2,1)S(1)}, bf16[4,512]{1,0:T(4,128)(2,1)}, u32[]{:S(2)}) copy-start(bf16[4,512]{1,0:T(4,128)(2,1)} %refs_2_.1) | copy-start | bytes 12292
  5.3 16.0 %all-to-all-start = ((bf16[8,144,256]{2,1,0:T(8,128)(2,1)}), bf16[8,144,256]{2,1,0:T(8,128)(2,1)S(1)}, u32[]{:S(2)}, u32[]{:S(2)}) async-start(bf16[8,144,256]{2,1,0:T(8,128)(2,1)} %maximum_maximum_fusion), calls=%async_computation | async-start | bytes 1179648 | tf_op jit(solution)/shard_map/all_to_all | solution.py:403
  11.9 13.7 %collective-permute-start.3 = (bf16[2,4,64,256]{3,2,1,0:T(8,128)(2,1)}, bf16[2,4,64,256]{3,2,1,0:T(8,128)(2,1)S(1)}, u32[]{:S(2)}, u32[]{:S(2)}) collective-permute-start(bf16[2,4,64,256]{3,2,1,0:T(8,128)(2,1)} %get-tuple-element.41), channel_id=1, source_target_pairs={{0,64},{32,96},{64,0},{96,32},{128,192},{160,224},{192,128},{224,1... | collective-permute-start | bytes 786440 | tf_op jit(solution)/shard_map/ppermute | solution.py:348
  14.0 18.0 %collective-permute-start.4 = (bf16[2,4,64,256]{3,2,1,0:T(8,128)(2,1)}, bf16[2,4,64,256]{3,2,1,0:T(8,128)(2,1)S(1)}, u32[]{:S(2)}, u32[]{:S(2)}) collective-permute-start(bf16[2,4,64,256]{3,2,1,0:T(8,128)(2,1)} %get-tuple-element.42), channel_id=1, source_target_pairs={{0,128},{32,160},{64,192},{96,224},{128,0},{160,32},{192,64},{224,... | collective-permute-start | bytes 786440 | tf_op jit(solution)/shard_map/ppermute | solution.py:348
  16.7 15.3 %collective-permute-start.5 = (bf16[2,4,64,256]{3,2,1,0:T(8,128)(2,1)}, bf16[2,4,64,256]{3,2,1,0:T(8,128)(2,1)}, u32[]{:S(2)}, u32[]{:S(2)}) collective-permute-start(bf16[2,4,64,256]{3,2,1,0:T(8,128)(2,1)} %get-tuple-element.43), channel_id=1, source_target_pairs={{0,192},{32,224},{64,128},{96,160},{128,64},{160,96},{192,0},{224,... | collective-permute-start | bytes 786440 | tf_op jit(solution)/shard_map/ppermute | solution.py:348
  16.9 20.8 %copy-start.4 = (f32[512]{0:T(512)S(1)}, f32[512]{0:T(512)}, u32[]{:S(2)}) copy-start(f32[512]{0:T(512)} %param.24) | copy-start | bytes 6148
  16.9 20.8 %copy-start.5 = (f32[8]{0:T(128)S(1)}, f32[8]{0:T(128)}, u32[]{:S(2)}) copy-start(f32[8]{0:T(128)} %param.22) | copy-start | bytes 100
  16.9 20.8 %copy-start.6 = (f32[8]{0:T(128)S(1)}, f32[8]{0:T(128)}, u32[]{:S(2)}) copy-start(f32[8]{0:T(128)} %param.21) | copy-start | bytes 100
  16.9 20.8 %copy-start.7 = (f32[8]{0:T(128)S(1)}, f32[8]{0:T(128)}, u32[]{:S(2)}) copy-start(f32[8]{0:T(128)} %param.23) | copy-start | bytes 100
  22.2 18.9 %copy-start.2 = (bf16[3,32,256]{2,1,0:T(8,128)(2,1)}, bf16[3,32,256]{2,1,0:T(8,128)(2,1)S(1)}, u32[]{:S(2)}) copy-start(bf16[3,32,256]{2,1,0:T(8,128)(2,1)S(1)} %get-tuple-element.56.refs_5_) | copy-start | bytes 147460
  22.2 9.8 %collective-permute-start = (bf16[128,128]{1,0:T(8,128)(2,1)S(1)}, bf16[128,128]{1,0:T(8,128)(2,1)S(1)}, u32[]{:S(2)}, u32[]{:S(2)}) collective-permute-start(bf16[128,128]{1,0:T(8,128)(2,1)S(1)} %get-tuple-element.39.refs_3_), channel_id=1, source_target_pairs={{0,1},{1,0},{2,3},{3,2},{4,5},{5,4},{6,7},{7,6},{8,9},{9,8},{10,11... | collective-permute-start | bytes 98312 | tf_op jit(solution)/shard_map/ppermute | solution.py:348
  23.3 8.7 %collective-permute-start.1 = (bf16[128,128]{1,0:T(8,128)(2,1)S(1)}, bf16[128,128]{1,0:T(8,128)(2,1)S(1)}, u32[]{:S(2)}, u32[]{:S(2)}) collective-permute-start(bf16[128,128]{1,0:T(8,128)(2,1)S(1)} %get-tuple-element.39.refs_3_), channel_id=1, source_target_pairs={{0,2},{1,3},{2,0},{3,1},{4,6},{5,7},{6,4},{7,5},{8,10},{9,11},{10,... | collective-permute-start | bytes 98312 | tf_op jit(solution)/shard_map/ppermute | solution.py:348
  25.7 6.4 %copy-start.8 = (bf16[2,4,64,256]{3,2,1,0:T(8,128)(2,1)}, bf16[2,4,64,256]{3,2,1,0:T(8,128)(2,1)S(1)}, u32[]{:S(2)}) copy-start(bf16[2,4,64,256]{3,2,1,0:T(8,128)(2,1)S(1)} %collective-permute-done.3.refs_1_.refs_13_.refs_7_) | copy-start | bytes 786436
  25.7 6.4 %collective-permute-start.2 = (bf16[128,128]{1,0:T(8,128)(2,1)S(1)}, bf16[128,128]{1,0:T(8,128)(2,1)S(1)}, u32[]{:S(2)}, u32[]{:S(2)}) collective-permute-start(bf16[128,128]{1,0:T(8,128)(2,1)S(1)} %get-tuple-element.39.refs_3_), channel_id=1, source_target_pairs={{0,3},{1,2},{2,1},{3,0},{4,7},{5,6},{6,5},{7,4},{8,11},{9,10},{10,... | collective-permute-start | bytes 98312 | tf_op jit(solution)/shard_map/ppermute | solution.py:348
  32.0 0.7 copy-start.9
  34.7 2.2 %collective-permute-start.6 = (bf16[4,4,64,256]{3,2,1,0:T(8,128)(2,1)}, bf16[4,4,64,256]{3,2,1,0:T(8,128)(2,1)S(1)}, u32[]{:S(2)}, u32[]{:S(2)}) collective-permute-start(bf16[4,4,64,256]{3,2,1,0:T(8,128)(2,1)} %states.1), channel_id=1, source_target_pairs={{0,32},{32,0},{64,96},{96,64},{128,160},{160,128},{192,224},{224,1... | collective-permute-start | bytes 1572872 | tf_op jit(solution)/shard_map/ppermute | solution.py:348
  36.9 0.8 copy-start.10
  41.1 15.7 %copy-start.1 = (bf16[512,1024]{1,0:T(8,128)(2,1)S(1)}, bf16[512,1024]{1,0:T(8,128)(2,1)}, u32[]{:S(2)}) copy-start(bf16[512,1024]{1,0:T(8,128)(2,1)} %refs_1_.1) | copy-start | bytes 3145732
  41.1 11.0 %all-to-all-start.1 = ((bf16[8,128,128]{2,1,0:T(8,128)(2,1)}), bf16[8,128,128]{2,1,0:T(8,128)(2,1)S(1)}, u32[]{:S(2)}, u32[]{:S(2)}) async-start(bf16[8,128,128]{2,1,0:T(8,128)(2,1)} %get-tuple-element.52), calls=%async_computation.1 | async-start | bytes 524288 | tf_op jit(solution)/shard_map/all_to_all | solution.py:460
  52.1 17.1 %collective-permute-start.7 = (bf16[2,272,256]{2,1,0:T(8,128)(2,1)}, bf16[2,272,256]{2,1,0:T(8,128)(2,1)}, u32[]{:S(2)}, u32[]{:S(2)}) collective-permute-start(bf16[2,272,256]{2,1,0:T(8,128)(2,1)} %get-tuple-element.63), channel_id=1, source_target_pairs={{0,64},{32,96},{64,0},{96,32},{128,192},{160,224},{192,128},{224,1... | collective-permute-start | bytes 835592 | tf_op jit(solution)/shard_map/ppermute | solution.py:348
  52.7 16.6 %collective-permute-start.8 = (bf16[2,272,256]{2,1,0:T(8,128)(2,1)}, bf16[2,272,256]{2,1,0:T(8,128)(2,1)}, u32[]{:S(2)}, u32[]{:S(2)}) collective-permute-start(bf16[2,272,256]{2,1,0:T(8,128)(2,1)} %get-tuple-element.64), channel_id=1, source_target_pairs={{0,128},{32,160},{64,192},{96,224},{128,0},{160,32},{192,64},{224,... | collective-permute-start | bytes 835592 | tf_op jit(solution)/shard_map/ppermute | solution.py:348
  54.7 15.0 %collective-permute-start.9 = (bf16[2,272,256]{2,1,0:T(8,128)(2,1)}, bf16[2,272,256]{2,1,0:T(8,128)(2,1)}, u32[]{:S(2)}, u32[]{:S(2)}) collective-permute-start(bf16[2,272,256]{2,1,0:T(8,128)(2,1)} %get-tuple-element.65), channel_id=1, source_target_pairs={{0,192},{32,224},{64,128},{96,160},{128,64},{160,96},{192,0},{224,... | collective-permute-start | bytes 835592 | tf_op jit(solution)/shard_map/ppermute | solution.py:348
  57.9 23.1 %all-to-all-start.2 = ((bf16[32,4,1152]{2,1,0:T(4,128)(2,1)}), bf16[32,4,1152]{2,1,0:T(4,128)(2,1)S(1)}, u32[]{:S(2)}, u32[]{:S(2)}) async-start(bf16[32,4,1152]{2,1,0:T(4,128)(2,1)} %project.1), calls=%async_computation.2 | async-start | bytes 589824 | tf_op jit(solution)/shard_map/all_to_all | solution.py:482
  71.7 2.3 %collective-permute-start.10 = (bf16[4,272,256]{2,1,0:T(8,128)(2,1)}, bf16[4,272,256]{2,1,0:T(8,128)(2,1)S(1)}, u32[]{:S(2)}, u32[]{:S(2)}) collective-permute-start(bf16[4,272,256]{2,1,0:T(8,128)(2,1)} %finals.1), channel_id=1, source_target_pairs={{0,32},{32,0},{64,96},{96,64},{128,160},{160,128},{192,224},{224,1... | collective-permute-start | bytes 1671176 | tf_op jit(solution)/shard_map/ppermute | solution.py:348
  73.9 0.8 copy-start.11

commit v7 on v6

--- a/solution.py
+++ b/solution.py
@@ -85,15 +85,12 @@
         copy.wait()
 
 
-def merge_kernel(p0, p1, p2, p3, out, held, sems):
-    loads = [pltpu.make_async_copy(p.at[1], held.at[c], sems.at[c]) for c, p in enumerate((p0, p1, p2, p3))]
+def merge_kernel(p0, p1, p2, p3, out, sems):
+    loads = [pltpu.make_async_copy(p.at[1], out.at[c], sems.at[c]) for c, p in enumerate((p0, p1, p2, p3))]
     for load in loads:
         load.start()
     for load in loads:
         load.wait()
-    copy = pltpu.make_async_copy(held, out, sems.at[4])
-    copy.start()
-    copy.wait()
 
 
 def arrived(parts):
@@ -184,6 +181,13 @@
     origin = jnp.sum(g * lanes_i, axis=1, keepdims=True)
     half = jnp.where(lax.broadcasted_iota(jnp.int32, (ROWS, 128), 1) < 64, 0.0, 1.0)
     origin_b = jnp.broadcast_to(origin, (ROWS, 128)) - half
+    early = []
+    b_buf[...] = b_in
+    coef_buf[...] = coef
+    first_buf[...] = jnp.broadcast_to(first, (ROWS, 128))
+    for n, (buf, ref) in enumerate(((b_buf, b_out), (coef_buf, coef_out), (first_buf, first_out))):
+        early.append(pltpu.make_async_copy(buf, ref, sem_send.at[8 + n]))
+        early[-1].start()
     acc = jnp.zeros((ROWS, 128), F32)
     for load in loads:
         load.wait()
@@ -204,12 +208,7 @@
     sends = [pltpu.make_async_copy(send, send_out.at[k], sem_send.at[k]) for k in range(8)]
     for copy in sends:
         copy.start()
-    b_buf[...] = b_in
-    coef_buf[...] = coef
-    first_buf[...] = jnp.broadcast_to(first, (ROWS, 128))
-    for n, (buf, ref) in enumerate(((b_buf, b_out), (coef_buf, coef_out), (first_buf, first_out))):
-        sends.append(pltpu.make_async_copy(buf, ref, sem_send.at[8 + n]))
-        sends[-1].start()
+    sends = early + sends
     for copy in sends:
         copy.wait()
 
@@ -359,8 +358,7 @@
         name,
         [ANY] * 4,
         [(shape, BF16)],
-        [pltpu.VMEM(shape, BF16), pltpu.SemaphoreType.DMA((5,))],
-        out_specs=[ANY],
+        [pltpu.SemaphoreType.DMA((4,))],
     )(*got)
     return got + [swap(merged, "beam", 8, 1)]
 

time: 82.5 us -> 81.5 us (0.988)
  Pallas kernels: 19.5 us -> 17.9 us
    pallas_call x9, Pallas kernels: 19.5 us -> 17.9 us  [build(): pl.pallas_call(body, name=name, in_specs=list(specs), out_specs=tuple(out...]
    all_to_all x1, waiting for transfers between devices: 3.33 us -> 4.35 us  [local(): lax.all_to_all(parts, 'row', split_axis=0, concat_axis=0, tiled=True)]
where the time goes in v7:
time: 81.5 us; the launch traced here: 80.8 us
  starting transfers between devices  34.2 us (42%)
  waiting for transfers between devices  19 us (23%)
  Pallas kernels  17.9 us (22%)
  local copies, waits for them, and re-layouts  6.87 us (8%)
  between operations  1 us (1%)
  other arithmetic  0.98 us (1%)
  matrix products  0.85 us (1%)
    pallas_call x9, Pallas kernels, build(): pl.pallas_call(body, name=name, in_specs=list(specs), out_specs=tuple(out...  17.9 us
    ppermute x11, starting transfers between devices, swap(): return lax.ppermute(value, axis, [(i, i ^ mask) for i in range(count)])  14.8 us
    all_to_all x1, starting transfers between devices, local(): lax.all_to_all(parts, 'row', split_axis=0, concat_axis=0, tiled=True)  11.3 us
    ppermute x11, waiting for transfers between devices, swap(): return lax.ppermute(value, axis, [(i, i ^ mask) for i in range(count)])  7.57 us
    all_to_all x1, starting transfers between devices, local(): lax.all_to_all(payload, 'beam', split_axis=0, concat_axis=0, tiled=True)  4.43 us
    all_to_all x1, waiting for transfers between devices, local(): lax.all_to_all(parts, 'row', split_axis=0, concat_axis=0, tiled=True)  4.35 us
    all_to_all x1, waiting for transfers between devices, local(): lax.all_to_all(payload, 'beam', split_axis=0, concat_axis=0, tiled=True)  4.04 us
    all_to_all x1, starting transfers between devices, local(): lax.all_to_all(send, 'beam', split_axis=0, concat_axis=0, tiled=True)  3.55 us
  transfers between devices with their start and end apart: 14, of which 7 were waited for; matrix products, arithmetic and copies ran while one was open for 2% of the time, Pallas kernels for 16%

profile of v7, /device:TPU:32, one launch (start us, length us, event | category | flops | bytes accessed | tf_op | source)
XLA Modules:
  0.0 80.8 jit_solution(7955045030537889039)
XLA Ops:
  0.7 1.2 %reshape.86 = bf16[4,8,4,1024]{3,2,1,0:T(4,128)(2,1)S(1)} reshape(bf16[4,2,16,1024]{3,2,1,0:T(8,128)(2,1)} %param.15) | data formatting | bytes 524288 | tf_op jit(solution)/shard_map/reshape | solution.py:387
  4.3 1.0 %maximum_maximum_fusion = bf16[8,144,256]{2,1,0:T(8,128)(2,1)} fusion(bf16[8,1,128]{2,1,0:T(2,128)(2,1)S(1)} %copy.54, bf16[8,1,128]{2,1,0:T(2,128)(2,1)S(1)} %copy.53, bf16[8,12,64]{2,1,0:T(8,128)(2,1)S(1)} %copy.52, bf16[8,128,128]{2,1,0:T(8,128)(2,1)S(1)} %copy.49, bf16[144]{0:T(256)(128)(2,1)S(1)} %pad.7.clone, bf16[144,256]{1,0:T(8,128)(2,1)S(1)} %pad.4.clone, ...), kind=kLoop, calls=%fused_computation.3 | loop fusion | flops 4718592 | bytes 1089824 | tf_op jit(solution)/shard_map/concatenate | solution.py:400
  5.3 4.4 %all-to-all-start = ((bf16[8,144,256]{2,1,0:T(8,128)(2,1)}), bf16[8,144,256]{2,1,0:T(8,128)(2,1)S(1)}, u32[]{:S(2)}, u32[]{:S(2)}) async-start(bf16[8,144,256]{2,1,0:T(8,128)(2,1)} %maximum_maximum_fusion), calls=%async_computation | async-start | bytes 1179648 | tf_op jit(solution)/shard_map/all_to_all | solution.py:401
  9.7 2.2 %pack.1 = (bf16[2,4,64,256]{3,2,1,0:T(8,128)(2,1)}, bf16[2,4,64,256]{3,2,1,0:T(8,128)(2,1)}, bf16[2,4,64,256]{3,2,1,0:T(8,128)(2,1)}, bf16[2,4,64,256]{3,2,1,0:T(8,128)(2,1)}) custom-call(bf16[2,2,8,64,256]{4,3,2,1,0:T(8,128)(2,1)} %refs_0_.1), custom_call_target="tpu_custom_call" | custom-call | tf_op jit(solution)/shard_map/pack/pallas_call | solution.py:330
  11.9 2.1 %collective-permute-start.3 = (bf16[2,4,64,256]{3,2,1,0:T(8,128)(2,1)}, bf16[2,4,64,256]{3,2,1,0:T(8,128)(2,1)S(1)}, u32[]{:S(2)}, u32[]{:S(2)}) collective-permute-start(bf16[2,4,64,256]{3,2,1,0:T(8,128)(2,1)} %get-tuple-element.41), channel_id=1, source_target_pairs={{0,64},{32,96},{64,0},{96,32},{128,192},{160,224},{192,128},{224,1... | collective-permute-start | bytes 786440 | tf_op jit(solution)/shard_map/ppermute | solution.py:347
  14.0 2.7 %collective-permute-start.4 = (bf16[2,4,64,256]{3,2,1,0:T(8,128)(2,1)}, bf16[2,4,64,256]{3,2,1,0:T(8,128)(2,1)S(1)}, u32[]{:S(2)}, u32[]{:S(2)}) collective-permute-start(bf16[2,4,64,256]{3,2,1,0:T(8,128)(2,1)} %get-tuple-element.42), channel_id=1, source_target_pairs={{0,128},{32,160},{64,192},{96,224},{128,0},{160,32},{192,64},{224,... | collective-permute-start | bytes 786440 | tf_op jit(solution)/shard_map/ppermute | solution.py:347
  17.2 4.0 %all-to-all-done.refs_0_ = bf16[8,144,256]{2,1,0:T(8,128)(2,1)S(1)} async-done(((bf16[8,144,256]{2,1,0:T(8,128)(2,1)}), bf16[8,144,256]{2,1,0:T(8,128)(2,1)S(1)}, u32[]{:S(2)}, u32[]{:S(2)}) %all-to-all-start) | async-done | bytes 589856 | tf_op jit(solution)/shard_map/all_to_all | solution.py:401
  21.3 0.9 %conv.1 = (bf16[128,256]{1,0:T(8,128)(2,1)S(1)}, bf16[128,128]{1,0:T(8,128)(2,1)S(1)}, bf16[128,128]{1,0:T(8,128)(2,1)S(1)}, f32[1,128]{1,0:T(1,128)S(1)}, bf16[3,32,256]{2,1,0:T(8,128)(2,1)S(1)}) custom-call(bf16[8,144,256]{2,1,0:T(8,128)(2,1)S(1)} %all-to-all-done.refs_0_, s32[128,1]{1,0:T(8,128)S(1)} %reshape.102.refs_1_.refs_0_, ...), custom_call_target="tpu_custom_call" | custom-call | tf_op jit(solution)/shard_map/conv/pallas_call | solution.py:330
  22.2 1.1 %collective-permute-start = (bf16[128,128]{1,0:T(8,128)(2,1)S(1)}, bf16[128,128]{1,0:T(8,128)(2,1)S(1)}, u32[]{:S(2)}, u32[]{:S(2)}) collective-permute-start(bf16[128,128]{1,0:T(8,128)(2,1)S(1)} %get-tuple-element.39.refs_3_), channel_id=1, source_target_pairs={{0,1},{1,0},{2,3},{3,2},{4,5},{5,4},{6,7},{7,6},{8,9},{9,8},{10,11... | collective-permute-start | bytes 98312 | tf_op jit(solution)/shard_map/ppermute | solution.py:347
  23.3 2.4 %collective-permute-start.1 = (bf16[128,128]{1,0:T(8,128)(2,1)S(1)}, bf16[128,128]{1,0:T(8,128)(2,1)S(1)}, u32[]{:S(2)}, u32[]{:S(2)}) collective-permute-start(bf16[128,128]{1,0:T(8,128)(2,1)S(1)} %get-tuple-element.39.refs_3_), channel_id=1, source_target_pairs={{0,2},{1,3},{2,0},{3,1},{4,6},{5,7},{6,4},{7,5},{8,10},{9,11},{10,... | collective-permute-start | bytes 98312 | tf_op jit(solution)/shard_map/ppermute | solution.py:347
  25.7 1.6 %collective-permute-start.2 = (bf16[128,128]{1,0:T(8,128)(2,1)S(1)}, bf16[128,128]{1,0:T(8,128)(2,1)S(1)}, u32[]{:S(2)}, u32[]{:S(2)}) collective-permute-start(bf16[128,128]{1,0:T(8,128)(2,1)S(1)} %get-tuple-element.39.refs_3_), channel_id=1, source_target_pairs={{0,3},{1,2},{2,1},{3,0},{4,7},{5,6},{6,5},{7,4},{8,11},{9,10},{10,... | collective-permute-start | bytes 98312 | tf_op jit(solution)/shard_map/ppermute | solution.py:347
  27.3 4.7 %collective-permute-done.4.refs_2_.refs_14_.refs_8_ = bf16[2,4,64,256]{3,2,1,0:T(8,128)(2,1)S(1)} collective-permute-done((bf16[2,4,64,256]{3,2,1,0:T(8,128)(2,1)}, bf16[2,4,64,256]{3,2,1,0:T(8,128)(2,1)S(1)}, u32[]{:S(2)}, u32[]{:S(2)}) %collective-permute-start.4) | collective-permute-done | bytes 262176 | tf_op jit(solution)/shard_map/ppermute | solution.py:347
  32.1 0.7 copy-done.9
  32.7 1.1 %states.1 = bf16[4,4,64,256]{3,2,1,0:T(8,128)(2,1)S(1)} custom-call(bf16[2,4,64,256]{3,2,1,0:T(8,128)(2,1)} %get-tuple-element.48.refs_0_.refs_12_.refs_6_, bf16[2,4,64,256]{3,2,1,0:T(8,128)(2,1)} %copy-done.8, bf16[2,4,64,256]{3,2,1,0:T(8,128)(2,1)} %copy-done.9, bf16[2,4,64,256]{3,2,1,0:T(8,128)(2,1)} %collective-permute-done.5.refs_3_.refs_15_.refs_9_), custom_call_target="tpu_custom_call" | custom-call | tf_op jit(solution)/shard_map/states/pallas_call | solution.py:330
  34.0 1.9 %collective-permute-done.6.refs_16_.refs_10_ = bf16[4,4,64,256]{3,2,1,0:T(8,128)(2,1)S(1)} collective-permute-done((bf16[4,4,64,256]{3,2,1,0:T(8,128)(2,1)S(1)}, bf16[4,4,64,256]{3,2,1,0:T(8,128)(2,1)S(1)}, u32[]{:S(2)}, u32[]{:S(2)}) %collective-permute-start.6) | collective-permute-done | bytes 524320 | tf_op jit(solution)/shard_map/ppermute | solution.py:347
  35.9 0.8 copy-done.10
  36.7 3.4 %scan.1 = (bf16[8,128,128]{2,1,0:T(8,128)(2,1)}, bf16[128,256]{1,0:T(8,128)(2,1)}, f32[128,128]{1,0:T(8,128)}, f32[128,128]{1,0:T(8,128)}) custom-call(s32[128,1]{1,0:T(8,128)S(1)} %reshape.102.refs_1_.refs_0_, bf16[128,256]{1,0:T(8,128)(2,1)S(1)} %get-tuple-element.37.refs_1_, bf16[128,128]{1,0:T(8,128)(2,1)S(1)} %get-tuple-element.38.refs_2_.refs_1_, ...), custom_call_target="tpu_custom_call" | custom-call | tf_op jit(solution)/shard_map/scan/pallas_call | solution.py:330
  40.1 3.6 %all-to-all-start.1 = ((bf16[8,128,128]{2,1,0:T(8,128)(2,1)}), bf16[8,128,128]{2,1,0:T(8,128)(2,1)S(1)}, u32[]{:S(2)}, u32[]{:S(2)}) async-start(bf16[8,128,128]{2,1,0:T(8,128)(2,1)} %get-tuple-element.52), calls=%async_computation.1 | async-start | bytes 524288 | tf_op jit(solution)/shard_map/all_to_all | solution.py:458
  43.7 4.4 %final.1 = (bf16[2,272,256]{2,1,0:T(8,128)(2,1)}, bf16[2,272,256]{2,1,0:T(8,128)(2,1)}, bf16[2,272,256]{2,1,0:T(8,128)(2,1)}, bf16[2,272,256]{2,1,0:T(8,128)(2,1)}) custom-call(s32[128]{0:T(128)S(1)} %reshape.96.refs_0_, bf16[128,128]{1,0:T(8,128)(2,1)S(1)} %get-tuple-element.38.refs_2_.refs_1_, bf16[128,256]{1,0:T(8,128)(2,1)} %get-tuple-element.53.refs_2_, ...), custom_call_target="tpu_custom_call" | custom-call | tf_op jit(solution)/shard_map/final/pallas_call | solution.py:330
  48.1 3.0 %all-to-all-done.1.refs_0_ = bf16[8,128,128]{2,1,0:T(8,128)(2,1)S(1)} async-done(((bf16[8,128,128]{2,1,0:T(8,128)(2,1)}), bf16[8,128,128]{2,1,0:T(8,128)(2,1)S(1)}, u32[]{:S(2)}, u32[]{:S(2)}) %all-to-all-start.1) | async-done | bytes 262176 | tf_op jit(solution)/shard_map/all_to_all | solution.py:458
  51.1 0.6 collective-permute-start.7
  51.7 2.0 %collective-permute-start.8 = (bf16[2,272,256]{2,1,0:T(8,128)(2,1)}, bf16[2,272,256]{2,1,0:T(8,128)(2,1)}, u32[]{:S(2)}, u32[]{:S(2)}) collective-permute-start(bf16[2,272,256]{2,1,0:T(8,128)(2,1)} %get-tuple-element.64), channel_id=1, source_target_pairs={{0,128},{32,160},{64,192},{96,224},{128,0},{160,32},{192,64},{224,... | collective-permute-start | bytes 835592 | tf_op jit(solution)/shard_map/ppermute | solution.py:347
  53.7 2.1 %collective-permute-start.9 = (bf16[2,272,256]{2,1,0:T(8,128)(2,1)}, bf16[2,272,256]{2,1,0:T(8,128)(2,1)}, u32[]{:S(2)}, u32[]{:S(2)}) collective-permute-start(bf16[2,272,256]{2,1,0:T(8,128)(2,1)} %get-tuple-element.65), channel_id=1, source_target_pairs={{0,192},{32,224},{64,128},{96,160},{128,64},{160,96},{192,0},{224,... | collective-permute-start | bytes 835592 | tf_op jit(solution)/shard_map/ppermute | solution.py:347
  55.8 1.1 %project.1 = bf16[32,4,1152]{2,1,0:T(4,128)(2,1)} custom-call(bf16[8,128,128]{2,1,0:T(8,128)(2,1)S(1)} %all-to-all-done.1.refs_0_, bf16[512,1024]{1,0:T(8,128)(2,1)S(1)} %copy-done.1), custom_call_target="tpu_custom_call" | custom-call | tf_op jit(solution)/shard_map/project/pallas_call | solution.py:330
  56.9 11.3 %all-to-all-start.2 = ((bf16[32,4,1152]{2,1,0:T(4,128)(2,1)}), bf16[32,4,1152]{2,1,0:T(4,128)(2,1)S(1)}, u32[]{:S(2)}, u32[]{:S(2)}) async-start(bf16[32,4,1152]{2,1,0:T(4,128)(2,1)} %project.1), calls=%async_computation.2 | async-start | bytes 589824 | tf_op jit(solution)/shard_map/all_to_all | solution.py:480
  68.7 1.1 %finals.1 = bf16[4,272,256]{2,1,0:T(8,128)(2,1)S(1)} custom-call(bf16[2,272,256]{2,1,0:T(8,128)(2,1)} %get-tuple-element.62.refs_0_, bf16[2,272,256]{2,1,0:T(8,128)(2,1)} %collective-permute-done.7.refs_1_, bf16[2,272,256]{2,1,0:T(8,128)(2,1)} %collective-permute-done.8.refs_2_, bf16[2,272,256]{2,1,0:T(8,128)(2,1)} %collective-permute-done.9.refs_3_), custom_call_target="tpu_custom_call" | custom-call | tf_op jit(solution)/shard_map/finals/pallas_call | solution.py:330
  69.9 0.8 constant_dynamic-slice_fusion
  70.8 0.6 copy.63
  71.9 0.8 %copy-done.11 = bf16[4,272,256]{2,1,0:T(8,128)(2,1)} copy-done((bf16[4,272,256]{2,1,0:T(8,128)(2,1)}, bf16[4,272,256]{2,1,0:T(8,128)(2,1)S(1)}, u32[]{:S(2)}) %copy-start.11) | copy-done | bytes 557080
  72.7 2.9 %unpack.1 = (bf16[2,2,8,64,256]{4,3,2,1,0:T(8,128)(2,1)}, bf16[2,2,3,8,64]{4,3,2,1,0:T(8,128)(2,1)}) custom-call(bf16[2,272,256]{2,1,0:T(8,128)(2,1)} %get-tuple-element.62.refs_0_, bf16[2,272,256]{2,1,0:T(8,128)(2,1)} %collective-permute-done.7.refs_1_, bf16[2,272,256]{2,1,0:T(8,128)(2,1)} %collective-permute-done.8.refs_2_, ...), custom_call_target="tpu_custom_call" | custom-call | tf_op jit(solution)/shard_map/unpack/pallas_call | solution.py:330
  75.7 4.3 %all-to-all-done.2.refs_0_ = bf16[32,4,1152]{2,1,0:T(4,128)(2,1)S(1)} async-done(((bf16[32,4,1152]{2,1,0:T(4,128)(2,1)}), bf16[32,4,1152]{2,1,0:T(4,128)(2,1)S(1)}, u32[]{:S(2)}, u32[]{:S(2)}) %all-to-all-start.2) | async-done | bytes 294944 | tf_op jit(solution)/shard_map/all_to_all | solution.py:480
  80.0 0.8 norm.1
  (75 shorter events, 4.1 us)
Async XLA Ops:
  0.6 1.8 %copy-start = (bf16[1024,2,512]{2,1,0:T(2,128)(2,1)S(1)}, bf16[1024,2,512]{2,1,0:T(2,128)(2,1)}, u32[]{:S(2)}) copy-start(bf16[1024,2,512]{2,1,0:T(2,128)(2,1)} %param.16) | copy-start | bytes 6291460
  0.6 1.6 %copy-start.14 = (bf16[1024,8]{0,1:T(8,128)(2,1)S(1)}, bf16[1024,8]{0,1:T(8,128)(2,1)}, u32[]{:S(2)}) copy-start(bf16[1024,8]{0,1:T(8,128)(2,1)} %param.18) | copy-start | bytes 49156
  0.7 1.8 %copy-start.13 = (bf16[2,2,8,64,3]{3,2,4,1,0:T(8,128)(2,1)S(1)}, bf16[2,2,8,64,3]{3,2,4,1,0:T(8,128)(2,1)}, u32[]{:S(2)}) copy-start(bf16[2,2,8,64,3]{3,2,4,1,0:T(8,128)(2,1)} %param.27) | copy-start | bytes 36868
  2.9 0.7 copy-start.16
  2.9 1.0 %copy-start.12 = (bf16[1024,2,64]{0,2,1:T(8,128)(2,1)S(1)}, bf16[1024,2,64]{0,2,1:T(8,128)(2,1)}, u32[]{:S(2)}) copy-start(bf16[1024,2,64]{0,2,1:T(8,128)(2,1)} %param.17) | copy-start | bytes 786436
  5.3 11.5 %copy-start.15 = (s32[4,2,16]{2,1,0:T(2,128)S(1)}, s32[4,2,16]{2,1,0:T(2,128)}, u32[]{:S(2)}) copy-start(s32[4,2,16]{2,1,0:T(2,128)} %param.29) | copy-start | bytes 1540
  5.3 11.8 %copy-start.17 = (bf16[4,2,64]{2,1,0:T(2,128)(2,1)S(1)}, bf16[4,2,64]{2,1,0:T(2,128)(2,1)}, u32[]{:S(2)}) copy-start(bf16[4,2,64]{2,1,0:T(2,128)(2,1)} %param.20) | copy-start | bytes 3076
  5.3 16.0 %copy-start.3 = (bf16[4,512]{1,0:T(4,128)(2,1)S(1)}, bf16[4,512]{1,0:T(4,128)(2,1)}, u32[]{:S(2)}) copy-start(bf16[4,512]{1,0:T(4,128)(2,1)} %refs_2_.1) | copy-start | bytes 12292
  5.3 16.0 %all-to-all-start = ((bf16[8,144,256]{2,1,0:T(8,128)(2,1)}), bf16[8,144,256]{2,1,0:T(8,128)(2,1)S(1)}, u32[]{:S(2)}, u32[]{:S(2)}) async-start(bf16[8,144,256]{2,1,0:T(8,128)(2,1)} %maximum_maximum_fusion), calls=%async_computation | async-start | bytes 1179648 | tf_op jit(solution)/shard_map/all_to_all | solution.py:401
  11.9 13.7 %collective-permute-start.3 = (bf16[2,4,64,256]{3,2,1,0:T(8,128)(2,1)}, bf16[2,4,64,256]{3,2,1,0:T(8,128)(2,1)S(1)}, u32[]{:S(2)}, u32[]{:S(2)}) collective-permute-start(bf16[2,4,64,256]{3,2,1,0:T(8,128)(2,1)} %get-tuple-element.41), channel_id=1, source_target_pairs={{0,64},{32,96},{64,0},{96,32},{128,192},{160,224},{192,128},{224,1... | collective-permute-start | bytes 786440 | tf_op jit(solution)/shard_map/ppermute | solution.py:347
  14.0 18.0 %collective-permute-start.4 = (bf16[2,4,64,256]{3,2,1,0:T(8,128)(2,1)}, bf16[2,4,64,256]{3,2,1,0:T(8,128)(2,1)S(1)}, u32[]{:S(2)}, u32[]{:S(2)}) collective-permute-start(bf16[2,4,64,256]{3,2,1,0:T(8,128)(2,1)} %get-tuple-element.42), channel_id=1, source_target_pairs={{0,128},{32,160},{64,192},{96,224},{128,0},{160,32},{192,64},{224,... | collective-permute-start | bytes 786440 | tf_op jit(solution)/shard_map/ppermute | solution.py:347
  16.7 15.3 %collective-permute-start.5 = (bf16[2,4,64,256]{3,2,1,0:T(8,128)(2,1)}, bf16[2,4,64,256]{3,2,1,0:T(8,128)(2,1)}, u32[]{:S(2)}, u32[]{:S(2)}) collective-permute-start(bf16[2,4,64,256]{3,2,1,0:T(8,128)(2,1)} %get-tuple-element.43), channel_id=1, source_target_pairs={{0,192},{32,224},{64,128},{96,160},{128,64},{160,96},{192,0},{224,... | collective-permute-start | bytes 786440 | tf_op jit(solution)/shard_map/ppermute | solution.py:347
  16.9 19.8 %copy-start.4 = (f32[512]{0:T(512)S(1)}, f32[512]{0:T(512)}, u32[]{:S(2)}) copy-start(f32[512]{0:T(512)} %param.24) | copy-start | bytes 6148
  16.9 19.8 %copy-start.5 = (f32[8]{0:T(128)S(1)}, f32[8]{0:T(128)}, u32[]{:S(2)}) copy-start(f32[8]{0:T(128)} %param.22) | copy-start | bytes 100
  16.9 19.8 %copy-start.6 = (f32[8]{0:T(128)S(1)}, f32[8]{0:T(128)}, u32[]{:S(2)}) copy-start(f32[8]{0:T(128)} %param.21) | copy-start | bytes 100
  16.9 19.8 %copy-start.7 = (f32[8]{0:T(128)S(1)}, f32[8]{0:T(128)}, u32[]{:S(2)}) copy-start(f32[8]{0:T(128)} %param.23) | copy-start | bytes 100
  22.2 17.9 %copy-start.2 = (bf16[3,32,256]{2,1,0:T(8,128)(2,1)}, bf16[3,32,256]{2,1,0:T(8,128)(2,1)S(1)}, u32[]{:S(2)}) copy-start(bf16[3,32,256]{2,1,0:T(8,128)(2,1)S(1)} %get-tuple-element.56.refs_5_) | copy-start | bytes 147460
  22.2 9.8 %collective-permute-start = (bf16[128,128]{1,0:T(8,128)(2,1)S(1)}, bf16[128,128]{1,0:T(8,128)(2,1)S(1)}, u32[]{:S(2)}, u32[]{:S(2)}) collective-permute-start(bf16[128,128]{1,0:T(8,128)(2,1)S(1)} %get-tuple-element.39.refs_3_), channel_id=1, source_target_pairs={{0,1},{1,0},{2,3},{3,2},{4,5},{5,4},{6,7},{7,6},{8,9},{9,8},{10,11... | collective-permute-start | bytes 98312 | tf_op jit(solution)/shard_map/ppermute | solution.py:347
  23.3 8.7 %collective-permute-start.1 = (bf16[128,128]{1,0:T(8,128)(2,1)S(1)}, bf16[128,128]{1,0:T(8,128)(2,1)S(1)}, u32[]{:S(2)}, u32[]{:S(2)}) collective-permute-start(bf16[128,128]{1,0:T(8,128)(2,1)S(1)} %get-tuple-element.39.refs_3_), channel_id=1, source_target_pairs={{0,2},{1,3},{2,0},{3,1},{4,6},{5,7},{6,4},{7,5},{8,10},{9,11},{10,... | collective-permute-start | bytes 98312 | tf_op jit(solution)/shard_map/ppermute | solution.py:347
  25.7 6.4 %copy-start.8 = (bf16[2,4,64,256]{3,2,1,0:T(8,128)(2,1)}, bf16[2,4,64,256]{3,2,1,0:T(8,128)(2,1)S(1)}, u32[]{:S(2)}) copy-start(bf16[2,4,64,256]{3,2,1,0:T(8,128)(2,1)S(1)} %collective-permute-done.3.refs_1_.refs_13_.refs_7_) | copy-start | bytes 786436
  25.7 6.4 %collective-permute-start.2 = (bf16[128,128]{1,0:T(8,128)(2,1)S(1)}, bf16[128,128]{1,0:T(8,128)(2,1)S(1)}, u32[]{:S(2)}, u32[]{:S(2)}) collective-permute-start(bf16[128,128]{1,0:T(8,128)(2,1)S(1)} %get-tuple-element.39.refs_3_), channel_id=1, source_target_pairs={{0,3},{1,2},{2,1},{3,0},{4,7},{5,6},{6,5},{7,4},{8,11},{9,10},{10,... | collective-permute-start | bytes 98312 | tf_op jit(solution)/shard_map/ppermute | solution.py:347
  32.0 0.7 copy-start.9
  33.9 2.0 %collective-permute-start.6 = (bf16[4,4,64,256]{3,2,1,0:T(8,128)(2,1)S(1)}, bf16[4,4,64,256]{3,2,1,0:T(8,128)(2,1)S(1)}, u32[]{:S(2)}, u32[]{:S(2)}) collective-permute-start(bf16[4,4,64,256]{3,2,1,0:T(8,128)(2,1)S(1)} %states.1), channel_id=1, source_target_pairs={{0,32},{32,0},{64,96},{96,64},{128,160},{160,128},{192,224},{224,1... | collective-permute-start | bytes 1572872 | tf_op jit(solution)/shard_map/ppermute | solution.py:347
  35.9 0.8 copy-start.10
  40.1 15.7 %copy-start.1 = (bf16[512,1024]{1,0:T(8,128)(2,1)S(1)}, bf16[512,1024]{1,0:T(8,128)(2,1)}, u32[]{:S(2)}) copy-start(bf16[512,1024]{1,0:T(8,128)(2,1)} %refs_1_.1) | copy-start | bytes 3145732
  40.1 11.0 %all-to-all-start.1 = ((bf16[8,128,128]{2,1,0:T(8,128)(2,1)}), bf16[8,128,128]{2,1,0:T(8,128)(2,1)S(1)}, u32[]{:S(2)}, u32[]{:S(2)}) async-start(bf16[8,128,128]{2,1,0:T(8,128)(2,1)} %get-tuple-element.52), calls=%async_computation.1 | async-start | bytes 524288 | tf_op jit(solution)/shard_map/all_to_all | solution.py:458
  51.1 17.1 %collective-permute-start.7 = (bf16[2,272,256]{2,1,0:T(8,128)(2,1)}, bf16[2,272,256]{2,1,0:T(8,128)(2,1)}, u32[]{:S(2)}, u32[]{:S(2)}) collective-permute-start(bf16[2,272,256]{2,1,0:T(8,128)(2,1)} %get-tuple-element.63), channel_id=1, source_target_pairs={{0,64},{32,96},{64,0},{96,32},{128,192},{160,224},{192,128},{224,1... | collective-permute-start | bytes 835592 | tf_op jit(solution)/shard_map/ppermute | solution.py:347
  51.7 16.6 %collective-permute-start.8 = (bf16[2,272,256]{2,1,0:T(8,128)(2,1)}, bf16[2,272,256]{2,1,0:T(8,128)(2,1)}, u32[]{:S(2)}, u32[]{:S(2)}) collective-permute-start(bf16[2,272,256]{2,1,0:T(8,128)(2,1)} %get-tuple-element.64), channel_id=1, source_target_pairs={{0,128},{32,160},{64,192},{96,224},{128,0},{160,32},{192,64},{224,... | collective-permute-start | bytes 835592 | tf_op jit(solution)/shard_map/ppermute | solution.py:347
  53.7 15.0 %collective-permute-start.9 = (bf16[2,272,256]{2,1,0:T(8,128)(2,1)}, bf16[2,272,256]{2,1,0:T(8,128)(2,1)}, u32[]{:S(2)}, u32[]{:S(2)}) collective-permute-start(bf16[2,272,256]{2,1,0:T(8,128)(2,1)} %get-tuple-element.65), channel_id=1, source_target_pairs={{0,192},{32,224},{64,128},{96,160},{128,64},{160,96},{192,0},{224,... | collective-permute-start | bytes 835592 | tf_op jit(solution)/shard_map/ppermute | solution.py:347
  56.9 23.1 %all-to-all-start.2 = ((bf16[32,4,1152]{2,1,0:T(4,128)(2,1)}), bf16[32,4,1152]{2,1,0:T(4,128)(2,1)S(1)}, u32[]{:S(2)}, u32[]{:S(2)}) async-start(bf16[32,4,1152]{2,1,0:T(4,128)(2,1)} %project.1), calls=%async_computation.2 | async-start | bytes 589824 | tf_op jit(solution)/shard_map/all_to_all | solution.py:480
  69.8 2.0 %collective-permute-start.10 = (bf16[4,272,256]{2,1,0:T(8,128)(2,1)S(1)}, bf16[4,272,256]{2,1,0:T(8,128)(2,1)S(1)}, u32[]{:S(2)}, u32[]{:S(2)}) collective-permute-start(bf16[4,272,256]{2,1,0:T(8,128)(2,1)S(1)} %finals.1), channel_id=1, source_target_pairs={{0,32},{32,0},{64,96},{96,64},{128,160},{160,128},{192,224},{224,1... | collective-permute-start | bytes 1671176 | tf_op jit(solution)/shard_map/ppermute | solution.py:347
  71.9 0.8 %copy-start.11 = (bf16[4,272,256]{2,1,0:T(8,128)(2,1)}, bf16[4,272,256]{2,1,0:T(8,128)(2,1)S(1)}, u32[]{:S(2)}) copy-start(bf16[4,272,256]{2,1,0:T(8,128)(2,1)S(1)} %collective-permute-done.10.refs_4_) | copy-start | bytes 1671172

commit v8 on v7

--- a/solution.py
+++ b/solution.py
@@ -430,7 +430,7 @@
     send, b_in, coef, first = call(
         scan_kernel,
         "scan",
-        [VM] * 12 + [ANY] * 5,
+        [VM] * 12 + [ANY] * 4 + [VM],
         [((8, ROWS, 128), BF16), ((ROWS, NS), BF16), ((ROWS, ROWS), F32), ((ROWS, 128), F32)],
         [
             pltpu.VMEM((BEAMS, HD, NS), BF16),

time: 81.5 us -> 81.5 us (level)
  local copies, waits for them, and re-layouts: 6.87 us -> 8.1 us
    unnamed x37 -> x41, local copies, waits for them, and re-layouts: 2.6 us -> 3.84 us
  transfers between devices with their start and end apart: 14 -> 14, of which waited for: 7 -> 6; matrix products, arithmetic and copies ran while one was open for 2% -> 2% of each run, Pallas kernels for 16% -> 16%
where the time goes in v8:
time: 81.5 us; the launch traced here: 80.8 us
  starting transfers between devices  34 us (42%)
  waiting for transfers between devices  18.2 us (22%)
  Pallas kernels  17.6 us (22%)
  local copies, waits for them, and re-layouts  8.1 us (10%)
  between operations  1.03 us (1%)
  other arithmetic  0.98 us (1%)
  matrix products  0.85 us (1%)
    pallas_call x9, Pallas kernels, build(): pl.pallas_call(body, name=name, in_specs=list(specs), out_specs=tuple(out...  17.6 us
    ppermute x11, starting transfers between devices, swap(): return lax.ppermute(value, axis, [(i, i ^ mask) for i in range(count)])  14.8 us
    all_to_all x1, starting transfers between devices, local(): lax.all_to_all(parts, 'row', split_axis=0, concat_axis=0, tiled=True)  11.4 us
    ppermute x11, waiting for transfers between devices, swap(): return lax.ppermute(value, axis, [(i, i ^ mask) for i in range(count)])  7.13 us
    all_to_all x1, starting transfers between devices, local(): lax.all_to_all(payload, 'beam', split_axis=0, concat_axis=0, tiled=True)  4.43 us
    all_to_all x1, waiting for transfers between devices, local(): lax.all_to_all(payload, 'beam', split_axis=0, concat_axis=0, tiled=True)  4.05 us
    all_to_all x1, waiting for transfers between devices, local(): lax.all_to_all(parts, 'row', split_axis=0, concat_axis=0, tiled=True)  3.95 us
    unnamed x41, local copies, waits for them, and re-layouts  3.84 us
  transfers between devices with their start and end apart: 14, of which 6 were waited for; matrix products, arithmetic and copies ran while one was open for 2% of the time, Pallas kernels for 16%

profile of v8, /device:TPU:32, one launch (start us, length us, event | category | flops | bytes accessed | tf_op | source)
XLA Modules:
  0.0 80.8 jit_solution(9463723824755714844)
XLA Ops:
  0.7 1.2 %reshape.86 = bf16[4,8,4,1024]{3,2,1,0:T(4,128)(2,1)S(1)} reshape(bf16[4,2,16,1024]{3,2,1,0:T(8,128)(2,1)} %param.15) | data formatting | bytes 524288 | tf_op jit(solution)/shard_map/reshape | solution.py:387
  4.3 1.0 %maximum_maximum_fusion = bf16[8,144,256]{2,1,0:T(8,128)(2,1)} fusion(bf16[8,1,128]{2,1,0:T(2,128)(2,1)S(1)} %copy.54, bf16[8,1,128]{2,1,0:T(2,128)(2,1)S(1)} %copy.53, bf16[8,12,64]{2,1,0:T(8,128)(2,1)S(1)} %copy.52, bf16[8,128,128]{2,1,0:T(8,128)(2,1)S(1)} %copy.49, bf16[144]{0:T(256)(128)(2,1)S(1)} %pad.7.clone, bf16[144,256]{1,0:T(8,128)(2,1)S(1)} %pad.4.clone, ...), kind=kLoop, calls=%fused_computation.3 | loop fusion | flops 4718592 | bytes 1089824 | tf_op jit(solution)/shard_map/concatenate | solution.py:400
  5.3 4.4 %all-to-all-start = ((bf16[8,144,256]{2,1,0:T(8,128)(2,1)}), bf16[8,144,256]{2,1,0:T(8,128)(2,1)S(1)}, u32[]{:S(2)}, u32[]{:S(2)}) async-start(bf16[8,144,256]{2,1,0:T(8,128)(2,1)} %maximum_maximum_fusion), calls=%async_computation | async-start | bytes 1179648 | tf_op jit(solution)/shard_map/all_to_all | solution.py:401
  9.7 2.2 %pack.1 = (bf16[2,4,64,256]{3,2,1,0:T(8,128)(2,1)}, bf16[2,4,64,256]{3,2,1,0:T(8,128)(2,1)}, bf16[2,4,64,256]{3,2,1,0:T(8,128)(2,1)}, bf16[2,4,64,256]{3,2,1,0:T(8,128)(2,1)}) custom-call(bf16[2,2,8,64,256]{4,3,2,1,0:T(8,128)(2,1)} %refs_0_.1), custom_call_target="tpu_custom_call" | custom-call | tf_op jit(solution)/shard_map/pack/pallas_call | solution.py:330
  11.9 2.1 %collective-permute-start.3 = (bf16[2,4,64,256]{3,2,1,0:T(8,128)(2,1)}, bf16[2,4,64,256]{3,2,1,0:T(8,128)(2,1)S(1)}, u32[]{:S(2)}, u32[]{:S(2)}) collective-permute-start(bf16[2,4,64,256]{3,2,1,0:T(8,128)(2,1)} %get-tuple-element.41), channel_id=1, source_target_pairs={{0,64},{32,96},{64,0},{96,32},{128,192},{160,224},{192,128},{224,1... | collective-permute-start | bytes 786440 | tf_op jit(solution)/shard_map/ppermute | solution.py:347
  14.0 2.7 %collective-permute-start.4 = (bf16[2,4,64,256]{3,2,1,0:T(8,128)(2,1)}, bf16[2,4,64,256]{3,2,1,0:T(8,128)(2,1)S(1)}, u32[]{:S(2)}, u32[]{:S(2)}) collective-permute-start(bf16[2,4,64,256]{3,2,1,0:T(8,128)(2,1)} %get-tuple-element.42), channel_id=1, source_target_pairs={{0,128},{32,160},{64,192},{96,224},{128,0},{160,32},{192,64},{224,... | collective-permute-start | bytes 786440 | tf_op jit(solution)/shard_map/ppermute | solution.py:347
  17.2 4.0 %all-to-all-done.refs_0_ = bf16[8,144,256]{2,1,0:T(8,128)(2,1)S(1)} async-done(((bf16[8,144,256]{2,1,0:T(8,128)(2,1)}), bf16[8,144,256]{2,1,0:T(8,128)(2,1)S(1)}, u32[]{:S(2)}, u32[]{:S(2)}) %all-to-all-start) | async-done | bytes 589856 | tf_op jit(solution)/shard_map/all_to_all | solution.py:401
  21.2 0.9 %conv.1 = (bf16[128,256]{1,0:T(8,128)(2,1)S(1)}, bf16[128,128]{1,0:T(8,128)(2,1)S(1)}, bf16[128,128]{1,0:T(8,128)(2,1)S(1)}, f32[1,128]{1,0:T(1,128)S(1)}, bf16[3,32,256]{2,1,0:T(8,128)(2,1)S(1)}) custom-call(bf16[8,144,256]{2,1,0:T(8,128)(2,1)S(1)} %all-to-all-done.refs_0_, s32[128,1]{1,0:T(8,128)S(1)} %reshape.102.refs_1_.refs_0_, ...), custom_call_target="tpu_custom_call" | custom-call | tf_op jit(solution)/shard_map/conv/pallas_call | solution.py:330
  22.2 1.1 %collective-permute-start = (bf16[128,128]{1,0:T(8,128)(2,1)S(1)}, bf16[128,128]{1,0:T(8,128)(2,1)S(1)}, u32[]{:S(2)}, u32[]{:S(2)}) collective-permute-start(bf16[128,128]{1,0:T(8,128)(2,1)S(1)} %get-tuple-element.39.refs_3_), channel_id=1, source_target_pairs={{0,1},{1,0},{2,3},{3,2},{4,5},{5,4},{6,7},{7,6},{8,9},{9,8},{10,11... | collective-permute-start | bytes 98312 | tf_op jit(solution)/shard_map/ppermute | solution.py:347
  23.3 2.4 %collective-permute-start.1 = (bf16[128,128]{1,0:T(8,128)(2,1)S(1)}, bf16[128,128]{1,0:T(8,128)(2,1)S(1)}, u32[]{:S(2)}, u32[]{:S(2)}) collective-permute-start(bf16[128,128]{1,0:T(8,128)(2,1)S(1)} %get-tuple-element.39.refs_3_), channel_id=1, source_target_pairs={{0,2},{1,3},{2,0},{3,1},{4,6},{5,7},{6,4},{7,5},{8,10},{9,11},{10,... | collective-permute-start | bytes 98312 | tf_op jit(solution)/shard_map/ppermute | solution.py:347
  25.7 1.6 %collective-permute-start.2 = (bf16[128,128]{1,0:T(8,128)(2,1)S(1)}, bf16[128,128]{1,0:T(8,128)(2,1)S(1)}, u32[]{:S(2)}, u32[]{:S(2)}) collective-permute-start(bf16[128,128]{1,0:T(8,128)(2,1)S(1)} %get-tuple-element.39.refs_3_), channel_id=1, source_target_pairs={{0,3},{1,2},{2,1},{3,0},{4,7},{5,6},{6,5},{7,4},{8,11},{9,10},{10,... | collective-permute-start | bytes 98312 | tf_op jit(solution)/shard_map/ppermute | solution.py:347
  27.3 4.7 %collective-permute-done.4.refs_2_.refs_14_.refs_8_ = bf16[2,4,64,256]{3,2,1,0:T(8,128)(2,1)S(1)} collective-permute-done((bf16[2,4,64,256]{3,2,1,0:T(8,128)(2,1)}, bf16[2,4,64,256]{3,2,1,0:T(8,128)(2,1)S(1)}, u32[]{:S(2)}, u32[]{:S(2)}) %collective-permute-start.4) | collective-permute-done | bytes 262176 | tf_op jit(solution)/shard_map/ppermute | solution.py:347
  32.0 0.7 copy-done.10
  32.7 1.1 %states.1 = bf16[4,4,64,256]{3,2,1,0:T(8,128)(2,1)S(1)} custom-call(bf16[2,4,64,256]{3,2,1,0:T(8,128)(2,1)} %get-tuple-element.48.refs_0_.refs_12_.refs_6_, bf16[2,4,64,256]{3,2,1,0:T(8,128)(2,1)} %copy-done.9, bf16[2,4,64,256]{3,2,1,0:T(8,128)(2,1)} %copy-done.10, bf16[2,4,64,256]{3,2,1,0:T(8,128)(2,1)} %collective-permute-done.5.refs_3_.refs_15_.refs_9_), custom_call_target="tpu_custom_call" | custom-call | tf_op jit(solution)/shard_map/states/pallas_call | solution.py:330
  34.0 1.9 %collective-permute-done.6.refs_16_.refs_10_ = bf16[4,4,64,256]{3,2,1,0:T(8,128)(2,1)S(1)} collective-permute-done((bf16[4,4,64,256]{3,2,1,0:T(8,128)(2,1)S(1)}, bf16[4,4,64,256]{3,2,1,0:T(8,128)(2,1)S(1)}, u32[]{:S(2)}, u32[]{:S(2)}) %collective-permute-start.6) | collective-permute-done | bytes 524320 | tf_op jit(solution)/shard_map/ppermute | solution.py:347
  35.9 3.1 %scan.1 = (bf16[8,128,128]{2,1,0:T(8,128)(2,1)}, bf16[128,256]{1,0:T(8,128)(2,1)}, f32[128,128]{1,0:T(8,128)}, f32[128,128]{1,0:T(8,128)}) custom-call(s32[128,1]{1,0:T(8,128)S(1)} %reshape.102.refs_1_.refs_0_, bf16[128,256]{1,0:T(8,128)(2,1)S(1)} %get-tuple-element.37.refs_1_, bf16[128,128]{1,0:T(8,128)(2,1)S(1)} %get-tuple-element.38.refs_2_.refs_1_, ...), custom_call_target="tpu_custom_call" | custom-call | tf_op jit(solution)/shard_map/scan/pallas_call | solution.py:330
  39.0 3.4 %all-to-all-start.1 = ((bf16[8,128,128]{2,1,0:T(8,128)(2,1)}), bf16[8,128,128]{2,1,0:T(8,128)(2,1)S(1)}, u32[]{:S(2)}, u32[]{:S(2)}) async-start(bf16[8,128,128]{2,1,0:T(8,128)(2,1)} %get-tuple-element.52), calls=%async_computation.1 | async-start | bytes 524288 | tf_op jit(solution)/shard_map/all_to_all | solution.py:458
  42.5 4.3 %final.1 = (bf16[2,272,256]{2,1,0:T(8,128)(2,1)}, bf16[2,272,256]{2,1,0:T(8,128)(2,1)}, bf16[2,272,256]{2,1,0:T(8,128)(2,1)}, bf16[2,272,256]{2,1,0:T(8,128)(2,1)}) custom-call(s32[128]{0:T(128)S(1)} %reshape.96.refs_0_, bf16[128,128]{1,0:T(8,128)(2,1)S(1)} %get-tuple-element.38.refs_2_.refs_1_, bf16[128,256]{1,0:T(8,128)(2,1)} %get-tuple-element.53.refs_2_, ...), custom_call_target="tpu_custom_call" | custom-call | tf_op jit(solution)/shard_map/final/pallas_call | solution.py:330
  46.8 3.0 %all-to-all-done.1.refs_0_ = bf16[8,128,128]{2,1,0:T(8,128)(2,1)S(1)} async-done(((bf16[8,128,128]{2,1,0:T(8,128)(2,1)}), bf16[8,128,128]{2,1,0:T(8,128)(2,1)S(1)}, u32[]{:S(2)}, u32[]{:S(2)}) %all-to-all-start.1) | async-done | bytes 262176 | tf_op jit(solution)/shard_map/all_to_all | solution.py:458
  50.4 2.0 %collective-permute-start.8 = (bf16[2,272,256]{2,1,0:T(8,128)(2,1)}, bf16[2,272,256]{2,1,0:T(8,128)(2,1)S(1)}, u32[]{:S(2)}, u32[]{:S(2)}) collective-permute-start(bf16[2,272,256]{2,1,0:T(8,128)(2,1)} %get-tuple-element.64), channel_id=1, source_target_pairs={{0,128},{32,160},{64,192},{96,224},{128,0},{160,32},{192,64},{224,... | collective-permute-start | bytes 835592 | tf_op jit(solution)/shard_map/ppermute | solution.py:347
  52.5 2.1 %collective-permute-start.9 = (bf16[2,272,256]{2,1,0:T(8,128)(2,1)}, bf16[2,272,256]{2,1,0:T(8,128)(2,1)}, u32[]{:S(2)}, u32[]{:S(2)}) collective-permute-start(bf16[2,272,256]{2,1,0:T(8,128)(2,1)} %get-tuple-element.65), channel_id=1, source_target_pairs={{0,192},{32,224},{64,128},{96,160},{128,64},{160,96},{192,0},{224,... | collective-permute-start | bytes 835592 | tf_op jit(solution)/shard_map/ppermute | solution.py:347
  54.6 1.2 %copy-done.2 = bf16[512,1024]{1,0:T(8,128)(2,1)S(1)} copy-done((bf16[512,1024]{1,0:T(8,128)(2,1)S(1)}, bf16[512,1024]{1,0:T(8,128)(2,1)}, u32[]{:S(2)}) %copy-start.2) | copy-done | bytes 1048600
  55.8 1.1 %project.1 = bf16[32,4,1152]{2,1,0:T(4,128)(2,1)} custom-call(bf16[8,128,128]{2,1,0:T(8,128)(2,1)S(1)} %all-to-all-done.1.refs_0_, bf16[512,1024]{1,0:T(8,128)(2,1)S(1)} %copy-done.2), custom_call_target="tpu_custom_call" | custom-call | tf_op jit(solution)/shard_map/project/pallas_call | solution.py:330
  56.9 11.4 %all-to-all-start.2 = ((bf16[32,4,1152]{2,1,0:T(4,128)(2,1)}), bf16[32,4,1152]{2,1,0:T(4,128)(2,1)S(1)}, u32[]{:S(2)}, u32[]{:S(2)}) async-start(bf16[32,4,1152]{2,1,0:T(4,128)(2,1)} %project.1), calls=%async_computation.2 | async-start | bytes 589824 | tf_op jit(solution)/shard_map/all_to_all | solution.py:480
  68.3 0.7 copy-done.11
  69.1 1.1 %finals.1 = bf16[4,272,256]{2,1,0:T(8,128)(2,1)S(1)} custom-call(bf16[2,272,256]{2,1,0:T(8,128)(2,1)} %get-tuple-element.62.refs_0_, bf16[2,272,256]{2,1,0:T(8,128)(2,1)} %copy-done.11, bf16[2,272,256]{2,1,0:T(8,128)(2,1)} %copy-done.12, bf16[2,272,256]{2,1,0:T(8,128)(2,1)} %collective-permute-done.9.refs_3_), custom_call_target="tpu_custom_call" | custom-call | tf_op jit(solution)/shard_map/finals/pallas_call | solution.py:330
  70.3 0.8 constant_dynamic-slice_fusion
  71.2 0.6 copy.63
  72.3 0.8 %copy-done.13 = bf16[4,272,256]{2,1,0:T(8,128)(2,1)} copy-done((bf16[4,272,256]{2,1,0:T(8,128)(2,1)}, bf16[4,272,256]{2,1,0:T(8,128)(2,1)S(1)}, u32[]{:S(2)}) %copy-start.13) | copy-done | bytes 557080
  73.1 2.9 %unpack.1 = (bf16[2,2,8,64,256]{4,3,2,1,0:T(8,128)(2,1)}, bf16[2,2,3,8,64]{4,3,2,1,0:T(8,128)(2,1)}) custom-call(bf16[2,272,256]{2,1,0:T(8,128)(2,1)} %get-tuple-element.62.refs_0_, bf16[2,272,256]{2,1,0:T(8,128)(2,1)} %copy-done.11, bf16[2,272,256]{2,1,0:T(8,128)(2,1)} %copy-done.12, bf16[2,272,256]{2,1,0:T(8,128)(2,1)} %collective-permute-done.9.refs_3_, ...), custom_call_target="tpu_custom_call" | custom-call | tf_op jit(solution)/shard_map/unpack/pallas_call | solution.py:330
  76.1 4.0 %all-to-all-done.2.refs_0_ = bf16[32,4,1152]{2,1,0:T(4,128)(2,1)S(1)} async-done(((bf16[32,4,1152]{2,1,0:T(4,128)(2,1)}), bf16[32,4,1152]{2,1,0:T(4,128)(2,1)S(1)}, u32[]{:S(2)}, u32[]{:S(2)}) %all-to-all-start.2) | async-done | bytes 294944 | tf_op jit(solution)/shard_map/all_to_all | solution.py:480
  80.0 0.8 norm.1
  (79 shorter events, 4.3 us)
Async XLA Ops:
  0.6 1.8 %copy-start = (bf16[1024,2,512]{2,1,0:T(2,128)(2,1)S(1)}, bf16[1024,2,512]{2,1,0:T(2,128)(2,1)}, u32[]{:S(2)}) copy-start(bf16[1024,2,512]{2,1,0:T(2,128)(2,1)} %param.16) | copy-start | bytes 6291460
  0.6 1.6 %copy-start.16 = (bf16[1024,8]{0,1:T(8,128)(2,1)S(1)}, bf16[1024,8]{0,1:T(8,128)(2,1)}, u32[]{:S(2)}) copy-start(bf16[1024,8]{0,1:T(8,128)(2,1)} %param.18) | copy-start | bytes 49156
  0.7 1.8 %copy-start.15 = (bf16[2,2,8,64,3]{3,2,4,1,0:T(8,128)(2,1)S(1)}, bf16[2,2,8,64,3]{3,2,4,1,0:T(8,128)(2,1)}, u32[]{:S(2)}) copy-start(bf16[2,2,8,64,3]{3,2,4,1,0:T(8,128)(2,1)} %param.27) | copy-start | bytes 36868
  3.0 1.0 %copy-start.14 = (bf16[1024,2,64]{0,2,1:T(8,128)(2,1)S(1)}, bf16[1024,2,64]{0,2,1:T(8,128)(2,1)}, u32[]{:S(2)}) copy-start(bf16[1024,2,64]{0,2,1:T(8,128)(2,1)} %param.17) | copy-start | bytes 786436
  5.3 11.5 %copy-start.17 = (s32[4,2,16]{2,1,0:T(2,128)S(1)}, s32[4,2,16]{2,1,0:T(2,128)}, u32[]{:S(2)}) copy-start(s32[4,2,16]{2,1,0:T(2,128)} %param.29) | copy-start | bytes 1540
  5.3 11.8 %copy-start.19 = (bf16[4,2,64]{2,1,0:T(2,128)(2,1)S(1)}, bf16[4,2,64]{2,1,0:T(2,128)(2,1)}, u32[]{:S(2)}) copy-start(bf16[4,2,64]{2,1,0:T(2,128)(2,1)} %param.20) | copy-start | bytes 3076
  5.3 16.0 %copy-start.4 = (bf16[4,512]{1,0:T(4,128)(2,1)S(1)}, bf16[4,512]{1,0:T(4,128)(2,1)}, u32[]{:S(2)}) copy-start(bf16[4,512]{1,0:T(4,128)(2,1)} %refs_2_.1) | copy-start | bytes 12292
  5.3 16.0 %all-to-all-start = ((bf16[8,144,256]{2,1,0:T(8,128)(2,1)}), bf16[8,144,256]{2,1,0:T(8,128)(2,1)S(1)}, u32[]{:S(2)}, u32[]{:S(2)}) async-start(bf16[8,144,256]{2,1,0:T(8,128)(2,1)} %maximum_maximum_fusion), calls=%async_computation | async-start | bytes 1179648 | tf_op jit(solution)/shard_map/all_to_all | solution.py:401
  11.9 13.7 %collective-permute-start.3 = (bf16[2,4,64,256]{3,2,1,0:T(8,128)(2,1)}, bf16[2,4,64,256]{3,2,1,0:T(8,128)(2,1)S(1)}, u32[]{:S(2)}, u32[]{:S(2)}) collective-permute-start(bf16[2,4,64,256]{3,2,1,0:T(8,128)(2,1)} %get-tuple-element.41), channel_id=1, source_target_pairs={{0,64},{32,96},{64,0},{96,32},{128,192},{160,224},{192,128},{224,1... | collective-permute-start | bytes 786440 | tf_op jit(solution)/shard_map/ppermute | solution.py:347
  14.0 18.0 %collective-permute-start.4 = (bf16[2,4,64,256]{3,2,1,0:T(8,128)(2,1)}, bf16[2,4,64,256]{3,2,1,0:T(8,128)(2,1)S(1)}, u32[]{:S(2)}, u32[]{:S(2)}) collective-permute-start(bf16[2,4,64,256]{3,2,1,0:T(8,128)(2,1)} %get-tuple-element.42), channel_id=1, source_target_pairs={{0,128},{32,160},{64,192},{96,224},{128,0},{160,32},{192,64},{224,... | collective-permute-start | bytes 786440 | tf_op jit(solution)/shard_map/ppermute | solution.py:347
  16.7 15.3 %collective-permute-start.5 = (bf16[2,4,64,256]{3,2,1,0:T(8,128)(2,1)}, bf16[2,4,64,256]{3,2,1,0:T(8,128)(2,1)}, u32[]{:S(2)}, u32[]{:S(2)}) collective-permute-start(bf16[2,4,64,256]{3,2,1,0:T(8,128)(2,1)} %get-tuple-element.43), channel_id=1, source_target_pairs={{0,192},{32,224},{64,128},{96,160},{128,64},{160,96},{192,0},{224,... | collective-permute-start | bytes 786440 | tf_op jit(solution)/shard_map/ppermute | solution.py:347
  16.9 19.0 %copy-start.5 = (f32[512]{0:T(512)S(1)}, f32[512]{0:T(512)}, u32[]{:S(2)}) copy-start(f32[512]{0:T(512)} %param.24) | copy-start | bytes 6148
  16.9 19.0 %copy-start.6 = (f32[8]{0:T(128)S(1)}, f32[8]{0:T(128)}, u32[]{:S(2)}) copy-start(f32[8]{0:T(128)} %param.22) | copy-start | bytes 100
  16.9 19.0 %copy-start.7 = (f32[8]{0:T(128)S(1)}, f32[8]{0:T(128)}, u32[]{:S(2)}) copy-start(f32[8]{0:T(128)} %param.21) | copy-start | bytes 100
  16.9 19.0 %copy-start.8 = (f32[8]{0:T(128)S(1)}, f32[8]{0:T(128)}, u32[]{:S(2)}) copy-start(f32[8]{0:T(128)} %param.23) | copy-start | bytes 100
  22.2 16.8 %copy-start.3 = (bf16[3,32,256]{2,1,0:T(8,128)(2,1)}, bf16[3,32,256]{2,1,0:T(8,128)(2,1)S(1)}, u32[]{:S(2)}) copy-start(bf16[3,32,256]{2,1,0:T(8,128)(2,1)S(1)} %get-tuple-element.56.refs_5_) | copy-start | bytes 147460
  22.2 9.8 %collective-permute-start = (bf16[128,128]{1,0:T(8,128)(2,1)S(1)}, bf16[128,128]{1,0:T(8,128)(2,1)S(1)}, u32[]{:S(2)}, u32[]{:S(2)}) collective-permute-start(bf16[128,128]{1,0:T(8,128)(2,1)S(1)} %get-tuple-element.39.refs_3_), channel_id=1, source_target_pairs={{0,1},{1,0},{2,3},{3,2},{4,5},{5,4},{6,7},{7,6},{8,9},{9,8},{10,11... | collective-permute-start | bytes 98312 | tf_op jit(solution)/shard_map/ppermute | solution.py:347
  23.3 8.7 %collective-permute-start.1 = (bf16[128,128]{1,0:T(8,128)(2,1)S(1)}, bf16[128,128]{1,0:T(8,128)(2,1)S(1)}, u32[]{:S(2)}, u32[]{:S(2)}) collective-permute-start(bf16[128,128]{1,0:T(8,128)(2,1)S(1)} %get-tuple-element.39.refs_3_), channel_id=1, source_target_pairs={{0,2},{1,3},{2,0},{3,1},{4,6},{5,7},{6,4},{7,5},{8,10},{9,11},{10,... | collective-permute-start | bytes 98312 | tf_op jit(solution)/shard_map/ppermute | solution.py:347
  25.7 6.4 %copy-start.9 = (bf16[2,4,64,256]{3,2,1,0:T(8,128)(2,1)}, bf16[2,4,64,256]{3,2,1,0:T(8,128)(2,1)S(1)}, u32[]{:S(2)}) copy-start(bf16[2,4,64,256]{3,2,1,0:T(8,128)(2,1)S(1)} %collective-permute-done.3.refs_1_.refs_13_.refs_7_) | copy-start | bytes 786436
  25.7 6.4 %collective-permute-start.2 = (bf16[128,128]{1,0:T(8,128)(2,1)S(1)}, bf16[128,128]{1,0:T(8,128)(2,1)S(1)}, u32[]{:S(2)}, u32[]{:S(2)}) collective-permute-start(bf16[128,128]{1,0:T(8,128)(2,1)S(1)} %get-tuple-element.39.refs_3_), channel_id=1, source_target_pairs={{0,3},{1,2},{2,1},{3,0},{4,7},{5,6},{6,5},{7,4},{8,11},{9,10},{10,... | collective-permute-start | bytes 98312 | tf_op jit(solution)/shard_map/ppermute | solution.py:347
  33.9 2.0 %collective-permute-start.6 = (bf16[4,4,64,256]{3,2,1,0:T(8,128)(2,1)S(1)}, bf16[4,4,64,256]{3,2,1,0:T(8,128)(2,1)S(1)}, u32[]{:S(2)}, u32[]{:S(2)}) collective-permute-start(bf16[4,4,64,256]{3,2,1,0:T(8,128)(2,1)S(1)} %states.1), channel_id=1, source_target_pairs={{0,32},{32,0},{64,96},{96,64},{128,160},{160,128},{192,224},{224,1... | collective-permute-start | bytes 1572872 | tf_op jit(solution)/shard_map/ppermute | solution.py:347
  35.9 3.1 %copy-start.1 = (bf16[4,4,64,256]{3,2,1,0:T(8,128)(2,1)}, bf16[4,4,64,256]{3,2,1,0:T(8,128)(2,1)S(1)}, u32[]{:S(2)}) copy-start(bf16[4,4,64,256]{3,2,1,0:T(8,128)(2,1)S(1)} %collective-permute-done.6.refs_16_.refs_10_) | copy-start | bytes 1572868
  39.0 10.9 %all-to-all-start.1 = ((bf16[8,128,128]{2,1,0:T(8,128)(2,1)}), bf16[8,128,128]{2,1,0:T(8,128)(2,1)S(1)}, u32[]{:S(2)}, u32[]{:S(2)}) async-start(bf16[8,128,128]{2,1,0:T(8,128)(2,1)} %get-tuple-element.52), calls=%async_computation.1 | async-start | bytes 524288 | tf_op jit(solution)/shard_map/all_to_all | solution.py:458
  49.9 18.4 %collective-permute-start.7 = (bf16[2,272,256]{2,1,0:T(8,128)(2,1)}, bf16[2,272,256]{2,1,0:T(8,128)(2,1)S(1)}, u32[]{:S(2)}, u32[]{:S(2)}) collective-permute-start(bf16[2,272,256]{2,1,0:T(8,128)(2,1)} %get-tuple-element.63), channel_id=1, source_target_pairs={{0,64},{32,96},{64,0},{96,32},{128,192},{160,224},{192,128},{224,1... | collective-permute-start | bytes 835592 | tf_op jit(solution)/shard_map/ppermute | solution.py:347
  50.4 17.8 %collective-permute-start.8 = (bf16[2,272,256]{2,1,0:T(8,128)(2,1)}, bf16[2,272,256]{2,1,0:T(8,128)(2,1)S(1)}, u32[]{:S(2)}, u32[]{:S(2)}) collective-permute-start(bf16[2,272,256]{2,1,0:T(8,128)(2,1)} %get-tuple-element.64), channel_id=1, source_target_pairs={{0,128},{32,160},{64,192},{96,224},{128,0},{160,32},{192,64},{224,... | collective-permute-start | bytes 835592 | tf_op jit(solution)/shard_map/ppermute | solution.py:347
  52.5 15.8 %collective-permute-start.9 = (bf16[2,272,256]{2,1,0:T(8,128)(2,1)}, bf16[2,272,256]{2,1,0:T(8,128)(2,1)}, u32[]{:S(2)}, u32[]{:S(2)}) collective-permute-start(bf16[2,272,256]{2,1,0:T(8,128)(2,1)} %get-tuple-element.65), channel_id=1, source_target_pairs={{0,192},{32,224},{64,128},{96,160},{128,64},{160,96},{192,0},{224,... | collective-permute-start | bytes 835592 | tf_op jit(solution)/shard_map/ppermute | solution.py:347
  54.6 1.2 %copy-start.2 = (bf16[512,1024]{1,0:T(8,128)(2,1)S(1)}, bf16[512,1024]{1,0:T(8,128)(2,1)}, u32[]{:S(2)}) copy-start(bf16[512,1024]{1,0:T(8,128)(2,1)} %refs_1_.1) | copy-start | bytes 3145732
  56.9 23.1 %all-to-all-start.2 = ((bf16[32,4,1152]{2,1,0:T(4,128)(2,1)}), bf16[32,4,1152]{2,1,0:T(4,128)(2,1)S(1)}, u32[]{:S(2)}, u32[]{:S(2)}) async-start(bf16[32,4,1152]{2,1,0:T(4,128)(2,1)} %project.1), calls=%async_computation.2 | async-start | bytes 589824 | tf_op jit(solution)/shard_map/all_to_all | solution.py:480
  68.3 0.7 copy-start.11
  68.3 0.8 %copy-start.12 = (bf16[2,272,256]{2,1,0:T(8,128)(2,1)}, bf16[2,272,256]{2,1,0:T(8,128)(2,1)S(1)}, u32[]{:S(2)}) copy-start(bf16[2,272,256]{2,1,0:T(8,128)(2,1)S(1)} %collective-permute-done.8.refs_2_) | copy-start | bytes 835588
  70.2 2.0 %collective-permute-start.10 = (bf16[4,272,256]{2,1,0:T(8,128)(2,1)S(1)}, bf16[4,272,256]{2,1,0:T(8,128)(2,1)S(1)}, u32[]{:S(2)}, u32[]{:S(2)}) collective-permute-start(bf16[4,272,256]{2,1,0:T(8,128)(2,1)S(1)} %finals.1), channel_id=1, source_target_pairs={{0,32},{32,0},{64,96},{96,64},{128,160},{160,128},{192,224},{224,1... | collective-permute-start | bytes 1671176 | tf_op jit(solution)/shard_map/ppermute | solution.py:347
  72.3 0.8 %copy-start.13 = (bf16[4,272,256]{2,1,0:T(8,128)(2,1)}, bf16[4,272,256]{2,1,0:T(8,128)(2,1)S(1)}, u32[]{:S(2)}) copy-start(bf16[4,272,256]{2,1,0:T(8,128)(2,1)S(1)} %collective-permute-done.10.refs_4_) | copy-start | bytes 1671172
  (2 other events, 1.4 us)
